TPU v7x, 256 devices: a whole 4x4x8 slice. The times are simulated.
256 devices in a mesh: ctx: 16 (over y, x_lo, core), hs: 16 (over x_hi, z).
Axes of the slice: x: 4 (x_hi: 2, x_lo: 2; x = x_hi * 2 + x_lo), y: 4, z: 8, core: 2. Of those that a mesh axis runs over, the one named last changes fastest.
Arguments:
- queries: bfloat16 [16, 16384, 512], P('hs', 'ctx'), may hold values from -40 to 40
- keys: bfloat16 [16, 16384, 512], P('hs', 'ctx'), may hold values from -6 to 6
- values: bfloat16 [16, 16384, 512], P('hs', 'ctx'), may hold values from -6 to 6
- rates: float32 [16, 16384], P('hs', 'ctx'), may hold values from 0.02 to 0.2
- doc_ids: int32 [2, 16384], replicated, may hold values from 0 to 3, never falling along the last dimension, each value on 1 to 8192 neighbouring positions
- fast_weights: bfloat16 [16, 3, 512, 512], P('hs'), may hold values from -0.25 to 0.25
- momentum: float32 [16, 3, 512, 512], P('hs'), may hold values from -0.2 to 0.2
- head_gain: float32 [16, 512], P('hs'), may hold values from 0.5 to 2
Outputs:
- tokens_out: bfloat16 [16, 16384, 512], P('hs', 'ctx')
- new_weights: bfloat16 [16, 3, 512, 512], P('hs')
Inputs may be any that keep to these rules, and one draw needn't show every extreme that they name: `doc_ids`: each row never falls; a document has at most 8192 positions and some document has exactly that many.
All inputs are finite; a program needn't handle non-finite values.
Results may differ from a plain program's by a relative error of at most 0.0092.
Values may be sent and summed in bfloat16 or wider, within the bound.
No kernel may reach another device: no remote copies, remote signals or barrier semaphores. Data moves between devices by JAX's collectives and lax.ppermute only.
A program may use at most 64 MiB of HBM per device.

v0:
```python
import math

import jax
import jax.numpy as jnp
from jax import lax
from jax.sharding import PartitionSpec as P

WINDOW_TOKENS = 512


def passed_along(array, axis, by):
    peers = lax.axis_size(axis)
    pairs = [(i, i + by) for i in range(peers) if 0 <= i + by < peers]
    return lax.ppermute(array, axis, pairs)


def attend_block(qb, kb, value_block, qpos, kpos, qdoc, kdoc):
    scores = jnp.einsum("qd,kd->qk", qb, kb, preferred_element_type=jnp.float32) / math.sqrt(
        qb.shape[1]
    )
    valid = (
        (kpos[None, :] <= qpos[:, None])
        & (kpos[None, :] > qpos[:, None] - WINDOW_TOKENS)
        & (kpos[None, :] >= 0)
        & (kdoc[None, :] == qdoc[:, None])
    )
    scores = jnp.where(valid, scores, -1e30)
    top = jnp.max(scores, axis=1, keepdims=True)
    expo = jnp.where(valid, jnp.exp(scores - top), 0.0)
    probs = (expo / jnp.sum(expo, axis=1, keepdims=True)).astype(jnp.bfloat16)
    return jnp.dot(probs, value_block, preferred_element_type=jnp.float32)


def renew(weights, mom_old, grads):
    mom = 0.9 * mom_old + grads
    wf = weights.astype(jnp.float32)
    cand = wf - mom
    old_rms = jnp.sqrt(jnp.mean(wf * wf, axis=1, keepdims=True) + 1e-06)
    new_rms = jnp.sqrt(jnp.mean(cand * cand, axis=1, keepdims=True) + 1e-06)
    return (cand * old_rms / new_rms).astype(jnp.bfloat16)


def per_device(queries, keys, values, rates, doc_ids, fast_weights, momentum, head_gain):
    qrow = queries[0]
    krow = keys[0]
    value_row_index = values[0]
    lrow = rates[0]
    weights = fast_weights[0]
    mom_old = momentum[0]
    local_rows = qrow.shape[0]
    ctx_count = lax.axis_size("ctx")
    token_total_count = local_rows * ctx_count
    seq_count = doc_ids.shape[0]
    heads = lax.axis_size("hs") // seq_count
    seq = lax.axis_index("hs") // heads
    docrow = lax.dynamic_index_in_dim(doc_ids, seq, 0, keepdims=False)
    offset = lax.axis_index("ctx") * local_rows
    rim_keys, rim_values = passed_along(
        (krow[local_rows - WINDOW_TOKENS :], value_row_index[local_rows - WINDOW_TOKENS :]),
        "ctx",
        1,
    )
    ext_keys = jnp.concatenate([rim_keys, krow], axis=0)
    ext_values = jnp.concatenate([rim_values, value_row_index], axis=0)
    dpad = jnp.concatenate([jnp.zeros((WINDOW_TOKENS,), jnp.int32), docrow], axis=0)

    def block(index):
        begin_offset = index * WINDOW_TOKENS
        qb = lax.dynamic_slice_in_dim(qrow, begin_offset, WINDOW_TOKENS, 0)
        kb = lax.dynamic_slice_in_dim(ext_keys, begin_offset, 2 * WINDOW_TOKENS, 0)
        value_block = lax.dynamic_slice_in_dim(ext_values, begin_offset, 2 * WINDOW_TOKENS, 0)
        qpos = offset + begin_offset + jnp.arange(WINDOW_TOKENS, dtype=jnp.int32)
        kpos = (
            offset + begin_offset - WINDOW_TOKENS + jnp.arange(2 * WINDOW_TOKENS, dtype=jnp.int32)
        )
        qdoc = lax.dynamic_slice_in_dim(docrow, offset + begin_offset, WINDOW_TOKENS, 0)
        kdoc = lax.dynamic_slice_in_dim(dpad, offset + begin_offset, 2 * WINDOW_TOKENS, 0)
        return attend_block(qb, kb, value_block, qpos, kpos, qdoc, kdoc)

    attn = lax.map(block, jnp.arange(local_rows // WINDOW_TOKENS, dtype=jnp.int32)).reshape(
        local_rows, qrow.shape[1]
    )
    h1 = jnp.dot(krow, weights[0], preferred_element_type=jnp.float32)
    h3 = jnp.dot(krow, weights[1], preferred_element_type=jnp.float32)
    act = jax.nn.silu(h1)
    gk = (act * h3).astype(jnp.bfloat16)
    scaled = (
        lrow[:, None] * value_row_index.astype(jnp.float32) / math.sqrt(token_total_count)
    ).astype(jnp.bfloat16)
    dg = -jnp.dot(scaled, weights[2], preferred_element_type=jnp.float32)
    sig = jax.nn.sigmoid(h1)
    dh1 = (dg * h3 * sig * (1.0 + h1 * (1.0 - sig))).astype(jnp.bfloat16)
    dh3 = (dg * act).astype(jnp.bfloat16)
    g_one = jnp.einsum("td,tf->df", krow, dh1, preferred_element_type=jnp.float32)
    g_three = jnp.einsum("td,tf->df", krow, dh3, preferred_element_type=jnp.float32)
    g_down = -jnp.einsum("td,tf->df", scaled, gk, preferred_element_type=jnp.float32)
    grads = jnp.stack([g_one, g_three, g_down])
    summed = lax.psum(grads, "ctx")
    fresh = renew(weights, mom_old, summed)
    o_one = jnp.dot(qrow, fresh[0], preferred_element_type=jnp.float32)
    o_three = jnp.dot(qrow, fresh[1], preferred_element_type=jnp.float32)
    gq = (jax.nn.silu(o_one) * o_three).astype(jnp.bfloat16)
    fast_out = jnp.einsum("tf,df->td", gq, fresh[2], preferred_element_type=jnp.float32)
    mixed = attn + fast_out
    squares = jnp.sum(mixed * mixed, axis=1)
    own_row = (jnp.arange(seq_count, dtype=jnp.int32) == seq).astype(jnp.float32)
    placed = own_row[:, None] * squares[None, :]
    totals = lax.psum(placed, "hs")
    mine = lax.dynamic_index_in_dim(totals, seq, 0, keepdims=False)
    scale_row = 1.0 / jnp.sqrt(mine / (heads * qrow.shape[1]) + 1e-06)
    result = (mixed * scale_row[:, None] * head_gain[0][None, :]).astype(jnp.bfloat16)
    return (result[None], fresh[None])


def solution(mesh):
    return jax.shard_map(
        per_device,
        mesh=mesh,
        in_specs=(
            P("hs", "ctx", None),
            P("hs", "ctx", None),
            P("hs", "ctx", None),
            P("hs", "ctx"),
            P(),
            P("hs", None, None, None),
            P("hs", None, None, None),
            P("hs", None),
        ),
        out_specs=(P("hs", "ctx", None), P("hs", None, None, None)),
        check_vma=False,
    )
```

profile of v0, /device:TPU:6, one launch (start us, length us, event | category | flops | bytes accessed | tf_op | source)
XLA Modules:
  0.0 225.5 jit_solution(102038582774702046)
XLA Ops:
  7.2 0.0 copy-start
  7.2 0.0 all-reduce.3.cloned.1.call-start
  7.2 2.0 slice_bitcast_fusion.8
  9.2 1.9 collective-permute-start
  11.1 1.9 slice_bitcast_fusion.7
  13.0 4.0 %collective-permute-start.1 = (bf16[512,512]{1,0:T(8,128)(2,1)}, bf16[512,512]{1,0:T(8,128)(2,1)}, u32[]{:S(2)}, u32[]{:S(2)}) collective-permute-start(bf16[512,512]{1,0:T(8,128)(2,1)} %slice_bitcast_fusion.7), channel_id=1, source_target_pairs={{0,16},{16,32},{32,48},{48,64},{64,80},{80,96},{96,112},{112,128},... | collective-permute-start | bytes 1572872 | tf_op jit(solution)/shard_map/ppermute | solution.py:14
  17.0 1.7 fusion.34
  18.8 0.0 copy-start.7
  18.8 0.7 fusion.36
  19.5 0.5 copy-done.7
  20.0 0.8 fusion.25
  20.8 0.9 convolution_bitcast_fusion.1
  21.7 1.4 convolution_bitcast_fusion.2
  23.0 1.2 fusion.23
  24.2 2.0 pad_maximum_fusion
  26.2 0.0 all-reduce.3.cloned.1.call-update
  26.2 0.1 constant_dynamic-slice_fusion
  26.3 1.8 copy.11
  28.1 2.4 %copy.12 = f32[1,3,512,512]{2,3,1,0:T(8,128)S(1)} copy(f32[1,3,512,512]{3,2,1,0:T(8,128)} %param.16) | data formatting | bytes 6291456 | tf_op args[6]
  30.5 2.7 %pad_maximum_fusion.1 = bf16[1536,512]{1,0:T(8,128)(2,1)} fusion(bf16[1024,512]{1,0:T(8,128)(2,1)} %bitcast.120, bf16[512,512]{1,0:T(8,128)(2,1)} %collective-permute-done), kind=kLoop, calls=%fused_computation.50 | loop fusion | flops 3145728 | bytes 3145728 | tf_op jit(solution)/shard_map/concatenate | solution.py:63
  33.2 2.4 %pad_maximum_fusion.2 = bf16[1536,512]{1,0:T(8,128)(2,1)} fusion(bf16[1024,512]{1,0:T(8,128)(2,1)S(1)} %bitcast.122, bf16[512,512]{1,0:T(8,128)(2,1)} %collective-permute-done.1), kind=kLoop, calls=%fused_computation.51 | loop fusion | flops 3145728 | bytes 3145728 | tf_op jit(solution)/shard_map/concatenate | solution.py:64
  35.6 16.3 %while.13 = (s32[]{:T(128)}, f32[2,512,512]{2,1,0:T(8,128)}, s32[2]{0:T(128)S(1)}, s32[]{:T(128)}, s32[16896]{0:T(1024)S(1)}, /*index=5*/s32[16384]{0:T(1024)S(1...) while((s32[]{:T(128)}, f32[2,512,512]{2,1,0:T(8,128)}, ...), condition=%wide.region_3.4_spmd, body=%wide.region_0.3_spmd.sunk | while | flops 1090522112 | bytes 16331647 | solution.py:80
  35.6 0.6 dynamic_slice.74
  36.8 0.1 dynamic_slice.76
  36.9 0.1 dynamic_slice.75
  37.0 2.6 %fusion.65 = (f32[512]{0:T(512)S(1)}, f32[512,1024]{1,0:T(8,128)S(1)}) fusion(s32[512]{0:T(512)S(1)} %dynamic_slice.75, s32[1024]{0:T(1024)S(1)} %dynamic_slice.76, pred[1024]{0:T(1024)(128)(4,1)S(1)} %broadcast_compare_fusion.2, s32[512]{0:T(512)S(1)} %get-tuple-element.229, s32[512]{0:T(512)S(1)} %get-tuple-element.230, ...), kind=kOutput, calls=%fused_computation.4.clone.1 | convolution fusion | flops 541588992 | bytes 3687432 | tf_op jit(solution)/shard_map/while/body/eval_jaxpr/qd,kd->qk/dot_general | solution.py:18
  39.6 1.5 fusion.66
  41.1 2.6 %fusion.67 = f32[2,512,512]{2,1,0:T(8,128)} fusion(f32[2,512,512]{2,1,0:T(8,128)} %get-tuple-element.251, s32[]{:T(128)} %get-tuple-element.250, f32[512,1024]{1,0:T(8,128)S(1)} %get-tuple-element.231, bf16[1536,512]{1,0:T(8,128)(2,1)S(1)} %copy-done.9, s32[]{:T(128)S(6)} %select_n.89, f32[512]{0:T(512)S(1)} %fusion.66, ...), kind=kOutput, calls=%fused_computation.6.clone.1 | convolution fusion | flops 543162368 | bytes 4214276 | tf_op jit(solution)/shard_map/while/body/eval_jaxpr/dot_general | solution.py:31
  43.7 0.6 dynamic_slice.74
  44.9 0.1 dynamic_slice.76
  45.0 0.1 dynamic_slice.75
  45.1 2.7 %fusion.65 = (f32[512]{0:T(512)S(1)}, f32[512,1024]{1,0:T(8,128)S(1)}) fusion(s32[512]{0:T(512)S(1)} %dynamic_slice.75, s32[1024]{0:T(1024)S(1)} %dynamic_slice.76, pred[1024]{0:T(1024)(128)(4,1)S(1)} %broadcast_compare_fusion.2, s32[512]{0:T(512)S(1)} %get-tuple-element.229, s32[512]{0:T(512)S(1)} %get-tuple-element.230, ...), kind=kOutput, calls=%fused_computation.4.clone.1 | convolution fusion | flops 541588992 | bytes 3687432 | tf_op jit(solution)/shard_map/while/body/eval_jaxpr/qd,kd->qk/dot_general | solution.py:18
  47.8 1.5 fusion.66
  49.3 2.6 %fusion.67 = f32[2,512,512]{2,1,0:T(8,128)} fusion(f32[2,512,512]{2,1,0:T(8,128)} %get-tuple-element.251, s32[]{:T(128)} %get-tuple-element.250, f32[512,1024]{1,0:T(8,128)S(1)} %get-tuple-element.231, bf16[1536,512]{1,0:T(8,128)(2,1)S(1)} %copy-done.9, s32[]{:T(128)S(6)} %select_n.89, f32[512]{0:T(512)S(1)} %fusion.66, ...), kind=kOutput, calls=%fused_computation.6.clone.1 | convolution fusion | flops 543162368 | bytes 4214276 | tf_op jit(solution)/shard_map/while/body/eval_jaxpr/dot_general | solution.py:31
  51.8 2.9 %copy.19 = f32[1024,512]{0,1:T(8,128)} copy(f32[1024,512]{1,0:T(8,128)} %bitcast.8) | data formatting | bytes 4194304 | tf_op jit(solution)/shard_map/reshape | solution.py:80
  54.8 105.9 %all-reduce.3.cloned.1.call-done = f32[3,512,512]{1,2,0:T(8,128)} async-done(((f32[3,512,512]{1,2,0:T(8,128)}), f32[3,512,512]{1,2,0:T(8,128)}) %all-reduce.3.cloned.1.call-update) | async-done | bytes 3145744 | tf_op jit(solution)/shard_map/psum | solution.py:98
  160.6 3.4 %fusion.17 = (f32[3,512]{1,0:T(4,128)S(1)}, f32[3,512]{1,0:T(4,128)S(1)}) fusion(bf16[1,3,512,512]{2,3,1,0:T(8,128)(2,1)} %copy.11, f32[3,512,512]{1,2,0:T(8,128)} %all-reduce.3.cloned.1.call-done, f32[1,3,512,512]{2,3,1,0:T(8,128)S(1)} %copy.12), kind=kLoop, calls=%fused_computation.28 | loop fusion | flops 6288384 | bytes 7876608 | tf_op jit(solution)/shard_map/reduce_sum | solution.py:38
  164.1 0.3 copy-done.3
  164.4 0.8 divide_convert_fusion.2
  165.3 1.1 copy-done.4
  166.4 0.7 fusion.33
  167.1 0.5 copy-done.11
  167.6 4.8 %multiply_reduce_fusion.1 = (f32[1024]{0:T(1024)S(1)}, f32[1024,512]{0,1:T(8,128)}) fusion(f32[1024,512]{0,1:T(8,128)} %copy.19, bf16[3,512,512]{1,2,0:T(8,128)(2,1)} %copy-done.4, f32[512,1024]{0,1:T(8,128)S(1)} %fusion.33, bf16[1,1024,512]{2,1,0:T(8,128)(2,1)S(1)} %bitcast.125), kind=kOutput, calls=%fused_computation.41 | convolution fusion | flops 1078459392 | bytes 8392704 | tf_op jit(solution)/shard_map/tf,df->td/dot_general | solution.py:103
  172.4 0.1 broadcast_multiply_fusion
  172.4 41.3 %psum.15 = f32[2,1024]{1,0:T(2,128)S(1)} all-reduce(f32[2,1024]{1,0:T(2,128)S(1)} %broadcast_multiply_fusion), channel_id=1, replica_groups=mesh['ctx'=16,'hs'=16] {'hs'}, use_global_device_ids=true, to_apply=%region_8.9 | all-reduce | flops 2048 | bytes 16384 | tf_op jit(solution)/shard_map/psum | solution.py:108
  213.8 1.9 fusion.27
  215.8 1.3 copy.15
  217.1 1.6 copy.16
  (38 shorter events, 0.1 us)
Async XLA Ops:
  7.2 19.0 %copy-start = (s32[2,16384]{1,0:T(2,128)S(1)}, s32[2,16384]{1,0:T(2,128)}, u32[]{:S(2)}) copy-start(s32[2,16384]{1,0:T(2,128)} %param.14) | copy-start | bytes 393220
  7.2 9.8 %copy-start.2 = (bf16[1,1024,512]{2,1,0:T(8,128)(2,1)S(1)}, bf16[1,1024,512]{2,1,0:T(8,128)(2,1)}, u32[]{:S(2)}) copy-start(bf16[1,1024,512]{2,1,0:T(8,128)(2,1)} %param.11) | copy-start | bytes 3145732
  7.2 153.5 %all-reduce.3.cloned.1.call-start = ((), (), s32[]{:S(2)}) async-start(), calls=%async_computation | async-start | bytes 6291456 | tf_op jit(solution)/shard_map/psum | solution.py:98
  9.2 21.3 %collective-permute-start = (bf16[512,512]{1,0:T(8,128)(2,1)}, bf16[512,512]{1,0:T(8,128)(2,1)}, u32[]{:S(2)}, u32[]{:S(2)}) collective-permute-start(bf16[512,512]{1,0:T(8,128)(2,1)} %slice_bitcast_fusion.8), channel_id=1, source_target_pairs={{0,16},{16,32},{32,48},{48,64},{64,80},{80,96},{96,112},{112,128},... | collective-permute-start | bytes 1572872 | tf_op jit(solution)/shard_map/ppermute | solution.py:14
  13.0 5.7 %copy-start.6 = (bf16[1,3,512,512]{3,2,1,0:T(8,128)(2,1)S(1)}, bf16[1,3,512,512]{3,2,1,0:T(8,128)(2,1)}, u32[]{:S(2)}) copy-start(bf16[1,3,512,512]{3,2,1,0:T(8,128)(2,1)} %param.15) | copy-start | bytes 4718596
  13.0 20.2 %collective-permute-start.1 = (bf16[512,512]{1,0:T(8,128)(2,1)}, bf16[512,512]{1,0:T(8,128)(2,1)}, u32[]{:S(2)}, u32[]{:S(2)}) collective-permute-start(bf16[512,512]{1,0:T(8,128)(2,1)} %slice_bitcast_fusion.7), channel_id=1, source_target_pairs={{0,16},{16,32},{32,48},{48,64},{64,80},{80,96},{96,112},{112,128},... | collective-permute-start | bytes 1572872 | tf_op jit(solution)/shard_map/ppermute | solution.py:14
  18.8 1.2 copy-start.7
  18.8 1.2 copy-start.13
  30.5 2.7 %copy-start.8 = (bf16[1,1024,512]{2,1,0:T(8,128)(2,1)S(1)}, bf16[1,1024,512]{2,1,0:T(8,128)(2,1)}, u32[]{:S(2)}) copy-start(bf16[1,1024,512]{2,1,0:T(8,128)(2,1)} %param.12) | copy-start | bytes 3145732
  39.6 1.5 copy-start.9
  47.7 1.5 copy-start.9
  160.6 3.5 %copy-start.1 = (bf16[1,3,512,512]{2,3,1,0:T(8,128)(2,1)S(1)}, bf16[1,3,512,512]{2,3,1,0:T(8,128)(2,1)}, u32[]{:S(2)}) copy-start(bf16[1,3,512,512]{2,3,1,0:T(8,128)(2,1)} %copy.11) | copy-start | bytes 4718596
  160.6 3.8 %copy-start.3 = (f32[3,512,512]{1,2,0:T(8,128)S(1)}, f32[3,512,512]{1,2,0:T(8,128)}, u32[]{:S(2)}) copy-start(f32[3,512,512]{1,2,0:T(8,128)} %all-reduce.3.cloned.1.call-done) | copy-start | bytes 9437188
  164.4 2.0 copy-start.10
  165.2 1.1 copy-start.4
  166.4 1.2 copy-start.11
  167.6 46.2 %copy-start.12 = (f32[1,512]{1,0:T(1,128)S(1)}, f32[1,512]{1,0:T(1,128)}, u32[]{:S(2)}) copy-start(f32[1,512]{1,0:T(1,128)} %param.17) | copy-start | bytes 6148
  213.8 3.3 %copy-start.5 = (bf16[3,512,512]{1,2,0:T(8,128)(2,1)S(1)}, bf16[3,512,512]{1,2,0:T(8,128)(2,1)}, u32[]{:S(2)}) copy-start(bf16[3,512,512]{1,2,0:T(8,128)(2,1)} %copy-done.4) | copy-start | bytes 4718596
Sparse Core Ops, SparseCore 0:
  26.3 134.2 all-reduce.2
where the time goes:
time: 229 us; the launch traced here: 225 us
  waiting for transfers between devices  106 us (46%)
  blocking collectives  41.3 us (18%)
  matrix products  22.5 us (10%)
  local copies, waits for them, and re-layouts  17.9 us (8%)
  other arithmetic  16.3 us (7%)
  between operations  14.3 us (6%)
  starting transfers between devices  5.92 us (3%)
    psum x1, waiting for transfers between devices, per_device(): summed = lax.psum(grads, 'ctx')  106 us
    psum x1, blocking collectives, per_device(): totals = lax.psum(placed, 'hs')  41.3 us
    unnamed x30, local copies, waits for them, and re-layouts  9.54 us
    ppermute x2, starting transfers between devices, passed_along(): return lax.ppermute(array, axis, pairs)  5.88 us
    dot_general x2, matrix products, attend_block(): jnp.einsum('qd,kd->qk', qb, kb, preferred_element_type=jnp.float32)  5.28 us
    dot_general x2, matrix products, attend_block(): return jnp.dot(probs, value_block, preferred_element_type=jnp.float32)  5.14 us
    dot_general x1, matrix products, per_device(): jnp.einsum('tf,df->td', gq, fresh[2], preferred_element_type=jnp.float32)  4.75 us
  transfers between devices with their start and end apart: 3, of which 1 were waited for; matrix products, arithmetic and copies ran while one was open for 17% of the time, Pallas kernels for 0%

commit v1 on v0

v1 whole, which is shorter than its diff:
```python
import functools
import math

import jax
import jax.numpy as jnp
from jax import lax
from jax.experimental import pallas as pl
from jax.experimental.pallas import tpu as pltpu
from jax.sharding import Mesh, PartitionSpec as P

WINDOW = 512
TILE = 256
BLOCK = 16
MIB = 1024 * 1024
BF16 = jnp.bfloat16
F32 = jnp.float32
NEG = -1e30

Y, X, CORE, SEQ, HEAD = "y", "x", "core", "seq", "head"


def nt(a, b):
    return lax.dot_general(a, b, (((1,), (1,)), ((), ())), preferred_element_type=F32)


def nn(a, b):
    return lax.dot_general(a, b, (((1,), (0,)), ((), ())), preferred_element_type=F32)


def tn(a, b):
    return lax.dot_general(a, b, (((0,), (0,)), ((), ())), preferred_element_type=F32)


def whole():
    return pl.BlockSpec(memory_space=pltpu.VMEM)


def params(limit, **kw):
    return pltpu.CompilerParams(vmem_limit_bytes=limit * MIB, **kw)


def cost(flops, read, trans=0):
    return pl.CostEstimate(flops=int(flops), bytes_accessed=int(read), transcendentals=int(trans))


def column_of(row):
    return jnp.transpose(jnp.broadcast_to(row, (128, 128)))


def grad_kernel(inv, me_ref, k_ref, v_ref, r_ref, w_ref, keep_ref, send_ref, acc):
    step = pl.program_id(0)

    @pl.when(step == 0)
    def _():
        acc[...] = jnp.zeros_like(acc)

    keys = k_ref[0]
    tiles = TILE // 128
    parts = []
    for t in range(tiles):
        rate = column_of(r_ref[pl.ds(step * tiles + t, 1), :])
        rows = v_ref[0, t * 128 : (t + 1) * 128, :].astype(F32)
        wide = jnp.concatenate([rate] * (rows.shape[1] // 128), axis=1)
        parts.append((wide * rows * inv).astype(BF16))
    u = jnp.concatenate(parts, axis=0)
    h1 = nn(keys, w_ref[0, 0])
    h3 = nn(keys, w_ref[0, 1])
    dg = nn(u, w_ref[0, 2])
    sig = 0.5 + 0.5 * jnp.tanh(0.5 * h1)
    act = h1 * sig
    gk = (act * h3).astype(BF16)
    dh3 = (dg * act).astype(BF16)
    dh1 = (dg * h3 * (sig + act * (1.0 - sig))).astype(BF16)
    acc[0] += tn(dh1, keys)
    acc[1] += tn(dh3, keys)
    acc[2] += tn(gk, u)

    @pl.when(step == pl.num_programs(0) - 1)
    def _():
        me = me_ref[0]
        half = keep_ref.shape[0]
        for l in range(2 * half):
            at = pl.multiple_of((me ^ l) * BLOCK, BLOCK)
            rows = acc[:, pl.ds(at, BLOCK), :].astype(BF16)
            if l < half:
                keep_ref[l] = rows
            else:
                send_ref[l - half] = rows


def grad_half(half, me, keys, values, rates, weights, inv):
    rows, dim = keys.shape[1:]
    hidden = weights.shape[3] // 2
    blocks = hidden // BLOCK // 2
    out = jax.ShapeDtypeStruct((blocks, 3, BLOCK, dim), BF16)
    return pl.pallas_call(
        functools.partial(grad_kernel, inv),
        grid_spec=pltpu.PrefetchScalarGridSpec(
            num_scalar_prefetch=1,
            grid=(rows // TILE,),
            in_specs=[
                pl.BlockSpec((1, TILE, dim), lambda i, s: (0, i, 0)),
                pl.BlockSpec((1, TILE, dim), lambda i, s: (0, i, 0)),
                pl.BlockSpec(rates.shape, lambda i, s: (0, 0)),
                pl.BlockSpec((1, 3, dim, hidden), lambda i, s: (0, 0, 0, half)),
            ],
            out_specs=[pl.BlockSpec(out.shape, lambda i, s: (0, 0, 0, 0))] * 2,
            scratch_shapes=[pltpu.VMEM((3, hidden, dim), F32)],
        ),
        out_shape=[out, out],
        compiler_params=params(20),
        cost_estimate=cost(12 * rows * dim * hidden, 4 * MIB, rows * hidden),
        name="grad" + "ab"[half],
    )(me, keys, values, rates, weights)


def attend(q, ks, vs, first, low, scale):
    tile = q.shape[0]
    col = lax.broadcasted_iota(jnp.int32, (tile, tile), 1)
    row = lax.broadcasted_iota(jnp.int32, (tile, tile), 0)
    scores = []
    for b in range(3):
        s = nt(q, ks[b])
        ok = col >= low - (first + b * tile)
        if b == 2:
            ok = ok & (col <= row)
        scores.append(jnp.where(ok, s, NEG))
    top = jnp.max(jnp.maximum(jnp.maximum(scores[0], scores[1]), scores[2]), axis=1, keepdims=True)
    total, out = None, None
    for b in range(3):
        p = jnp.exp2((scores[b] - top) * scale)
        total = p if total is None else total + p
        o = nn(p.astype(BF16), vs[b])
        out = o if out is None else out + o
    return out / jnp.sum(total, axis=1, keepdims=True)


def lowest(meta_ref, first, tile):
    pos = first + 2 * tile + lax.broadcasted_iota(jnp.int32, (tile, 1), 0)
    low = jnp.zeros_like(pos)
    for b in range(1, 4):
        low = jnp.where(pos >= meta_ref[b], meta_ref[b], low)
    return jnp.maximum(low, pos - (WINDOW - 1))


def attn_kernel(scale, part, meta_ref, *refs):
    if part == 0:
        q_ref, rk_ref, rv_ref, k_ref, v_ref, o_ref = refs
    else:
        q_ref, k_ref, v_ref, o_ref = refs
    for t in range(WINDOW // TILE):
        first = meta_ref[0] + part * WINDOW + (t - 2) * TILE
        ks, vs = [], []
        for b in range(3):
            at = part * WINDOW + (t + b - 2) * TILE
            if at < 0:
                at += WINDOW
                ks.append(rk_ref[at : at + TILE, :])
                vs.append(rv_ref[at : at + TILE, :])
            else:
                ks.append(k_ref[0, at : at + TILE, :])
                vs.append(v_ref[0, at : at + TILE, :])
        q = q_ref[0, t * TILE : (t + 1) * TILE, :]
        o_ref[t * TILE : (t + 1) * TILE, :] = attend(
            q, ks, vs, first, lowest(meta_ref, first, TILE), scale
        )


def attention(part, meta, queries, rims, keys, values):
    dim = queries.shape[2]
    rows = keys.shape[1] if part else WINDOW
    smem = pl.BlockSpec(memory_space=pltpu.SMEM)
    own = pl.BlockSpec((1, rows, dim), lambda i: (0, 0, 0))
    rim = pl.BlockSpec((WINDOW, dim), lambda i: (0, 0))
    return pl.pallas_call(
        functools.partial(attn_kernel, math.log2(math.e) / math.sqrt(dim), part),
        grid=(1,),
        in_specs=[smem, pl.BlockSpec((1, WINDOW, dim), lambda i: (0, part, 0))]
        + [rim] * len(rims)
        + [own, own],
        out_specs=pl.BlockSpec((WINDOW, dim), lambda i: (0, 0)),
        out_shape=jax.ShapeDtypeStruct((WINDOW, dim), F32),
        compiler_params=params(20),
        cost_estimate=cost(4 * WINDOW * 3 * TILE * dim, 4 * MIB, 3 * WINDOW * TILE),
        name="attn" + "ab"[part],
    )(meta, queries, *rims, keys, values)


def prep_kernel(me_ref, w_ref, m_ref, base_ref, rms_ref, wt, mt):
    half = pl.program_id(0)
    me = jnp.where(half == 0, me_ref[0], me_ref[1])
    at = pl.multiple_of((me % 8) * BLOCK, BLOCK)
    for m in range(3):
        wt[...] = jnp.transpose(w_ref[0, m].astype(F32))
        mt[...] = jnp.transpose(m_ref[0, m])
        w = wt[pl.ds(at, BLOCK), :]
        base_ref[0, m] = w - 0.9 * mt[pl.ds(at, BLOCK), :]
        rms = jnp.sqrt(jnp.mean(w * w, axis=1, keepdims=True) + 1e-06)
        rms_ref[0, m] = jnp.broadcast_to(rms, (BLOCK, 128))


def prepare(me, weights, momentum):
    dim, hidden = weights.shape[2:]
    pick = lambda i, s: (0, 0, 0, 2 * i + jnp.where(i == 0, s[0], s[1]) // 8)
    return pl.pallas_call(
        prep_kernel,
        grid_spec=pltpu.PrefetchScalarGridSpec(
            num_scalar_prefetch=1,
            grid=(2,),
            in_specs=[pl.BlockSpec((1, 3, dim, 128), pick)] * 2,
            out_specs=[
                pl.BlockSpec((1, 3, BLOCK, dim), lambda i, s: (i, 0, 0, 0)),
                pl.BlockSpec((1, 3, BLOCK, 128), lambda i, s: (i, 0, 0, 0)),
            ],
            scratch_shapes=[pltpu.VMEM((128, dim), F32)] * 2,
        ),
        out_shape=[
            jax.ShapeDtypeStruct((2, 3, BLOCK, dim), F32),
            jax.ShapeDtypeStruct((2, 3, BLOCK, 128), F32),
        ],
        compiler_params=params(12),
        cost_estimate=cost(3 * MIB, 3 * MIB),
        name="prep",
    )(me, weights, momentum)


def renew_kernel(half, base_ref, rms_ref, *refs):
    out_ref = refs[-1]
    neg = refs[0][...].astype(F32).reshape(out_ref.shape)
    for r in refs[1:-1]:
        neg = neg + r[...].astype(F32).reshape(out_ref.shape)
    cand = base_ref[half] + neg
    new = lax.rsqrt(jnp.mean(cand * cand, axis=2, keepdims=True) + 1e-06)
    out_ref[...] = (cand * (rms_ref[half][:, :, :1] * new)).astype(BF16)


def renew(half, base, rms, pieces):
    return pl.pallas_call(
        functools.partial(renew_kernel, half),
        in_specs=[whole()] * (2 + len(pieces)),
        out_specs=whole(),
        out_shape=jax.ShapeDtypeStruct(base.shape[1:], BF16),
        compiler_params=params(8),
        cost_estimate=cost(MIB, MIB // 2),
        name="renew" + "ab"[half],
    )(base, rms, *pieces)


def fill(new, mine_ref, other_ref):
    half, _, block, dim = mine_ref.shape
    for m in range(3):
        new[m, : half * block, :] = mine_ref[:, m].reshape(half * block, dim)
        new[m, half * block :, :] = other_ref[:, m].reshape(half * block, dim)


def fast_part(q, new):
    one = nt(q, new[0])
    three = nt(q, new[1])
    gq = (one * (0.5 + 0.5 * jnp.tanh(0.5 * one)) * three).astype(BF16)
    return nn(gq, new[2])


def out_a_kernel(q_ref, lo_ref, hi_ref, mine_ref, other_ref, y_ref, new):
    step = pl.program_id(0)

    @pl.when(step == 0)
    def _():
        fill(new, mine_ref, other_ref)

    attn = jnp.where(step < pl.num_programs(0) // 2, lo_ref[...], hi_ref[...])
    y_ref[...] = attn + fast_part(q_ref[0], new)


def out_b_kernel(q_ref, y1_ref, mine_ref, other_ref, y_ref, ss_ref, new):
    step = pl.program_id(0)

    @pl.when(step == 0)
    def _():
        fill(new, mine_ref, other_ref)

    y = y1_ref[...] + fast_part(q_ref[0], new)
    y_ref[...] = y
    sq = y * y
    lanes = sq[:, :128]
    for c in range(1, sq.shape[1] // 128):
        lanes = lanes + sq[:, c * 128 : (c + 1) * 128]
    tiles = TILE // 128
    for t in range(tiles):
        turned = jnp.transpose(lanes[t * 128 : (t + 1) * 128, :])
        ss_ref[pl.ds(step * tiles + t, 1), :] = jnp.sum(turned, axis=0, keepdims=True)


def out_a(queries, lo, hi, mine, other):
    rows, dim = queries.shape[1:]
    hidden = 2 * mine.shape[0] * BLOCK
    half = rows // TILE // 2
    full = pl.BlockSpec(mine.shape, lambda i: (0, 0, 0, 0))
    return pl.pallas_call(
        out_a_kernel,
        grid=(rows // TILE,),
        in_specs=[
            pl.BlockSpec((1, TILE, dim), lambda i: (0, i, 0)),
            pl.BlockSpec((TILE, dim), lambda i: (jnp.minimum(i, half - 1), 0)),
            pl.BlockSpec((TILE, dim), lambda i: (jnp.maximum(i - half, 0), 0)),
            full,
            full,
        ],
        out_specs=pl.BlockSpec((TILE, dim), lambda i: (i, 0)),
        out_shape=jax.ShapeDtypeStruct((rows, dim), F32),
        scratch_shapes=[pltpu.VMEM((3, hidden, dim), BF16)],
        compiler_params=params(16),
        cost_estimate=cost(6 * rows * dim * hidden, 6 * MIB, rows * hidden),
        name="outa",
    )(queries, lo, hi, mine, other)


def out_b(queries, y1, mine, other):
    rows, dim = queries.shape[1:]
    hidden = 2 * mine.shape[0] * BLOCK
    full = pl.BlockSpec(mine.shape, lambda i: (0, 0, 0, 0))
    return pl.pallas_call(
        out_b_kernel,
        grid=(rows // TILE,),
        in_specs=[
            pl.BlockSpec((1, TILE, dim), lambda i: (0, i, 0)),
            pl.BlockSpec((TILE, dim), lambda i: (i, 0)),
            full,
            full,
        ],
        out_specs=[
            pl.BlockSpec((TILE, dim), lambda i: (i, 0)),
            pl.BlockSpec((rows // 128, 128), lambda i: (0, 0)),
        ],
        out_shape=[
            jax.ShapeDtypeStruct((rows, dim), F32),
            jax.ShapeDtypeStruct((rows // 128, 128), F32),
        ],
        scratch_shapes=[pltpu.VMEM((3, hidden, dim), BF16)],
        compiler_params=params(16),
        cost_estimate=cost(6 * rows * dim * hidden, 6 * MIB, rows * hidden),
        name="outb",
    )(queries, y1, mine, other)


def weights_kernel(me_ref, am_ref, ao_ref, bm_ref, bo_ref, out_ref, rows):
    half = am_ref.shape[0]
    for m in range(3):
        for h, (mine, other) in enumerate(((am_ref, ao_ref), (bm_ref, bo_ref))):
            for l in range(2 * half):
                at = pl.multiple_of(((me_ref[h] ^ l) + h * 2 * half) * BLOCK, BLOCK)
                rows[pl.ds(at, BLOCK), :] = mine[l, m] if l < half else other[l - half, m]
        out_ref[0, m] = jnp.transpose(rows[...])


def weights_out(me, am, ao, bm, bo):
    dim = am.shape[3]
    hidden = 4 * am.shape[0] * BLOCK
    return pl.pallas_call(
        weights_kernel,
        in_specs=[pl.BlockSpec(memory_space=pltpu.SMEM)] + [whole()] * 4,
        out_specs=whole(),
        out_shape=jax.ShapeDtypeStruct((1, 3, dim, hidden), BF16),
        scratch_shapes=[pltpu.VMEM((hidden, dim), BF16)],
        compiler_params=params(12),
        cost_estimate=cost(MIB, 3 * MIB),
        name="weightsout",
    )(me, am, ao, bm, bo)


def norm_kernel(count, y_ref, a_ref, b_ref, gain_ref, out_ref):
    step = pl.program_id(0)
    tiles = y_ref.shape[0] // 128
    dim = y_ref.shape[1]
    gain = gain_ref[...]
    for t in range(tiles):
        at = pl.ds(step * tiles + t, 1)
        total = a_ref[at, :] + b_ref[at, :]
        scale = column_of(lax.rsqrt(total * (1.0 / count) + 1e-06))
        wide = jnp.concatenate([scale] * (dim // 128), axis=1)
        rows = slice(t * 128, (t + 1) * 128)
        out_ref[0, rows, :] = (y_ref[rows, :] * wide * gain).astype(BF16)


def norm(y, a, b, gain, count):
    rows, dim = y.shape
    small = pl.BlockSpec(a.shape, lambda i: (0, 0))
    return pl.pallas_call(
        functools.partial(norm_kernel, count),
        grid=(rows // TILE,),
        in_specs=[
            pl.BlockSpec((TILE, dim), lambda i: (i, 0)),
            small,
            small,
            pl.BlockSpec((1, dim), lambda i: (0, 0)),
        ],
        out_specs=pl.BlockSpec((1, TILE, dim), lambda i: (0, i, 0)),
        out_shape=jax.ShapeDtypeStruct((1, rows, dim), BF16),
        compiler_params=params(12),
        cost_estimate=cost(MIB, 3 * MIB),
        name="norm",
    )(y, a, b, gain)


def swap(x, axis, by):
    return lax.ppermute(x, axis, [(i, i ^ by) for i in range(lax.axis_size(axis))])


def added(*xs):
    return sum(x.astype(F32) for x in xs).astype(BF16)


def scatter_a(keep, send):
    got = swap(send, CORE, 1)
    n = keep.shape[0] // 2
    keep, send = added(keep[:n], got[:n]), added(keep[n:], got[n:])
    got = swap(send, X, 1)
    s = [added(keep[k : k + 1], got[k : k + 1]) for k in range(keep.shape[0])]
    return [s[0]] + [swap(s[k], Y, k) for k in range(1, len(s))]


def scatter_b(keep, send):
    got = swap(send, CORE, 1)
    s = [added(keep[2 * k : 2 * k + 2], got[2 * k : 2 * k + 2]) for k in range(keep.shape[0] // 2)]
    got = [swap(s[k], Y, k) for k in range(1, len(s))]
    keep = added(s[0][:1], *(g[:1] for g in got))
    send = added(s[0][1:], *(g[1:] for g in got))
    return [keep, swap(send, X, 1)]


def gather_a(new):
    new = new[None]
    new = jnp.concatenate([new] + [swap(new, Y, k) for k in range(1, lax.axis_size(Y))], axis=0)
    new = jnp.concatenate([new, swap(new, X, 1)], axis=0)
    return new, swap(new, CORE, 1)


def gather_b(new):
    new = new[None]
    new = jnp.concatenate([new, swap(new, X, 1)], axis=0)
    new = jnp.concatenate([new] + [swap(new, Y, k) for k in range(1, lax.axis_size(Y))], axis=0)
    return new, swap(new, CORE, 1)


def ring_sum(s):
    n = lax.axis_size(HEAD)
    s = s + swap(s, HEAD, 1)
    s = s + lax.ppermute(s, HEAD, [(i, (i + 1) % n if i % 2 else (i - 1) % n) for i in range(n)])
    far = lax.ppermute(s, HEAD, [((d - 3) % n if d % 2 else (d + 3) % n, d) for d in range(n)])
    return s, far


def per_device(queries, keys, values, rates, doc_ids, fast_weights, momentum, head_gain):
    rows, dim = queries.shape[1:]
    ys, xs, cores = lax.axis_size(Y), lax.axis_size(X), lax.axis_size(CORE)
    y, x, core = lax.axis_index(Y), lax.axis_index(X), lax.axis_index(CORE)
    ctx = (Y, X, CORE)
    n = ys * xs * cores
    me_a = (core * xs + x) * ys + y
    me_b = (core * ys + y) * xs + x
    me = jnp.stack([me_a, me_b]).astype(jnp.int32)
    offset = lax.axis_index(ctx) * rows
    docs = lax.dynamic_index_in_dim(doc_ids, lax.axis_index(SEQ), 0, keepdims=False)
    bounds = jnp.sum(
        docs[None, :] < jnp.arange(1, 4, dtype=jnp.int32)[:, None], axis=1, dtype=jnp.int32
    )
    meta = jnp.concatenate([offset.astype(jnp.int32)[None], bounds])
    ahead = [(i, i + 1) for i in range(n - 1)]
    rim_keys = lax.ppermute(keys[0, rows - WINDOW :], ctx, ahead)
    rim_values = lax.ppermute(values[0, rows - WINDOW :], ctx, ahead)
    rate_rows = rates.reshape(rows // 128, 128)
    inv = 1.0 / math.sqrt(rows * n)

    part_a = grad_half(0, me[0:1], keys, values, rate_rows, fast_weights, inv)
    part_b = grad_half(1, me[1:2], keys, values, rate_rows, fast_weights, inv)
    base, rms = prepare(me, fast_weights, momentum)
    pieces_a = scatter_a(*part_a)
    pieces_b = scatter_b(*part_b)
    hi = attention(1, meta, queries, (), keys, values)
    lo = attention(0, meta, queries, (rim_keys, rim_values), keys, values)
    new_a = renew(0, base, rms, pieces_a)
    new_b = renew(1, base, rms, pieces_b)
    full_a = gather_a(new_a)
    full_b = gather_b(new_b)
    mixed = out_a(queries, lo, hi, *full_a)
    mixed, squares = out_b(queries, mixed, *full_b)
    sums = ring_sum(squares)
    fresh = weights_out(me, *full_a, *full_b)
    result = norm(mixed, *sums, head_gain, lax.axis_size(HEAD) * dim)
    return result, fresh


def solution(mesh):
    seqs = 2
    sizes = mesh.shape
    fine = Mesh(
        mesh.devices.reshape(sizes["ctx"] // 4, 2, 2, seqs, sizes["hs"] // seqs),
        (Y, X, CORE, SEQ, HEAD),
    )
    ctx, hs = (Y, X, CORE), (SEQ, HEAD)
    return jax.shard_map(
        per_device,
        mesh=fine,
        in_specs=(
            P(hs, ctx, None),
            P(hs, ctx, None),
            P(hs, ctx, None),
            P(hs, ctx),
            P(),
            P(hs, None, None, None),
            P(hs, None, None, None),
            P(hs, None),
        ),
        out_specs=(P(hs, ctx, None), P(hs, None, None, None)),
        check_vma=False,
    )
```

time: 229 us -> 114 us (0.50)
  waiting for transfers between devices: 106 us -> 23.8 us
  blocking collectives: 41.3 us -> 0 us
  starting transfers between devices: 5.92 us -> 38.5 us
  Pallas kernels: 0 us -> 28 us
  matrix products: 22.5 us -> 0 us
  between operations: 14.3 us -> 0.88 us
  other arithmetic: 16.3 us -> 2.95 us
    psum x1 -> x0, waiting for transfers between devices: 106 us -> none  [per_device(): summed = lax.psum(grads, 'ctx')]
    psum x1 -> x0, blocking collectives: 41.3 us -> none  [per_device(): totals = lax.psum(placed, 'hs')]
    ppermute x2 -> x25, starting transfers between devices: 5.88 us -> 38.5 us  [the longest x21 26.8 us: swap(): lax.ppermute(x, axis, [(i, i ^ by) for i in range(lax.axis_size(axis))])]
    pallas_call x0 -> x11, Pallas kernels: none -> 28 us  [the longest x2 9.1 us: grad_half(): pl.pallas_call(functools.partial(grad_kernel, inv), grid_spec=pltpu.Prefe...]
    ppermute x2 -> x25, waiting for transfers between devices: 0.01 us -> 23.8 us  [the longest x21 21.9 us: swap(): lax.ppermute(x, axis, [(i, i ^ by) for i in range(lax.axis_size(axis))])]
    dot_general x12 -> x0, matrix products: 22.5 us -> none  [the longest x2 5.28 us: attend_block(): jnp.einsum('qd,kd->qk', qb, kb, preferred_element_type=jnp.float32)]
    reduce_sum x3 -> x1, other arithmetic: 6.39 us -> 0.31 us  [per_device(): jnp.sum(docs[None, :] < jnp.arange(1, 4, dtype=jnp.int32)[:, None], axis=...]
    concatenate x2 -> x3, other arithmetic: 5.05 us -> 0.11 us  [the longest x1 0.08 us: per_device(): meta = jnp.concatenate([offset.astype(jnp.int32)[None], bounds])]
  transfers between devices with their start and end apart: 3 -> 25, of which waited for: 1 -> 11; matrix products, arithmetic and copies ran while one was open for 17% -> 9% of each run, Pallas kernels for 0% -> 20%
where the time goes in v1:
time: 114 us; the launch traced here: 113 us
  starting transfers between devices  38.5 us (34%)
  Pallas kernels  28 us (25%)
  waiting for transfers between devices  23.8 us (21%)
  local copies, waits for them, and re-layouts  18.4 us (16%)
  other arithmetic  2.95 us (3%)
    ppermute x21, starting transfers between devices, swap(): lax.ppermute(x, axis, [(i, i ^ by) for i in range(lax.axis_size(axis))])  26.8 us
    ppermute x21, waiting for transfers between devices, swap(): lax.ppermute(x, axis, [(i, i ^ by) for i in range(lax.axis_size(axis))])  21.9 us
    unnamed x34, local copies, waits for them, and re-layouts  14.3 us
    pallas_call x2, Pallas kernels, grad_half(): pl.pallas_call(functools.partial(grad_kernel, inv), grid_spec=pltpu.Prefe...  9.1 us
    ppermute x1, starting transfers between devices, ring_sum(): lax.ppermute(s, HEAD, [(i, (i + 1) % n if i % 2 else (i - 1) % n) for i i...  5.85 us
    pallas_call x2, Pallas kernels, attention(): pl.pallas_call(functools.partial(attn_kernel, math.log2(math.e) / math.sq...  5.07 us
    pallas_call x1, Pallas kernels, out_b(): pl.pallas_call(out_b_kernel, grid=(rows // TILE,), in_specs=[pl.BlockSpec...  3.49 us
    pallas_call x1, Pallas kernels, out_a(): pl.pallas_call(out_a_kernel, grid=(rows // TILE,), in_specs=[pl.BlockSpec...  3.2 us
  transfers between devices with their start and end apart: 25, of which 11 were waited for; matrix products, arithmetic and copies ran while one was open for 9% of the time, Pallas kernels for 20%

profile of v1, /device:TPU:6, one launch (start us, length us, event | category | flops | bytes accessed | tf_op | source)
XLA Modules:
  0.0 112.6 jit_solution(9962820384179835704)
XLA Ops:
  0.6 1.9 %slice_bitcast_fusion = bf16[512,512]{1,0:T(8,128)(2,1)} fusion(bf16[1,1024,512]{2,1,0:T(8,128)(2,1)} %v_ref.3), kind=kLoop, calls=%fused_computation | loop fusion | bytes 1048576 | tf_op jit(solution)/shard_map/squeeze | solution.py:469
  2.6 1.9 %collective-permute-start.1 = (bf16[512,512]{1,0:T(8,128)(2,1)}, bf16[512,512]{1,0:T(8,128)(2,1)}, u32[]{:S(2)}, u32[]{:S(2)}) collective-permute-start(bf16[512,512]{1,0:T(8,128)(2,1)} %slice_bitcast_fusion), channel_id=1, source_target_pairs={{0,16},{16,32},{32,48},{48,64},{64,80},{80,96},{96,112},{112,128},... | collective-permute-start | bytes 1572872 | tf_op jit(solution)/shard_map/ppermute | solution.py:469
  4.5 1.2 %copy-done.2 = bf16[1,1024,512]{2,1,0:T(8,128)(2,1)S(1)} copy-done((bf16[1,1024,512]{2,1,0:T(8,128)(2,1)S(1)}, bf16[1,1024,512]{2,1,0:T(8,128)(2,1)}, u32[]{:S(2)}) %copy-start.2) | copy-done | bytes 1048600
  5.7 1.2 %copy-done.4 = bf16[1,1024,512]{2,1,0:T(8,128)(2,1)S(1)} copy-done((bf16[1,1024,512]{2,1,0:T(8,128)(2,1)S(1)}, bf16[1,1024,512]{2,1,0:T(8,128)(2,1)}, u32[]{:S(2)}) %copy-start.4) | copy-done | bytes 1048600
  6.9 1.4 %copy-done.7 = bf16[1,3,512,512]{3,2,1,0:T(8,128)(2,1)S(1)} copy-done((bf16[1,3,512,512]{3,2,1,0:T(8,128)(2,1)S(1)}, bf16[1,3,512,512]{3,2,1,0:T(8,128)(2,1)}, u32[]{:S(2)}) %copy-start.7) | copy-done | bytes 1572888
  8.3 0.7 copy-done.11
  9.0 4.5 %grada.1 = (bf16[8,3,16,512]{3,2,1,0:T(8,128)(2,1)S(1)}, bf16[8,3,16,512]{3,2,1,0:T(8,128)(2,1)}) custom-call(s32[1]{0:T(128)} %bitcast.4.me_ref, bf16[1,1024,512]{2,1,0:T(8,128)(2,1)S(1)} %copy-done.2, bf16[1,1024,512]{2,1,0:T(8,128)(2,1)S(1)} %copy-done.4, f32[8,128]{1,0:T(8,128)S(1)} %bitcast.19, bf16[1,3,512,512]{3,2,1,0:T(8,128)(2,1)S(1)} %copy-done.7), custom_call_target="tpu_custom_call" | custom-call | flops 1610612736 | bytes 4194304 | tf_op jit(solution)/shard_map/grada/pallas_call | solution.py:96
  13.6 1.9 %collective-permute-start.2 = (bf16[8,3,16,512]{3,2,1,0:T(8,128)(2,1)}, bf16[8,3,16,512]{3,2,1,0:T(8,128)(2,1)}, u32[]{:S(2)}, u32[]{:S(2)}) collective-permute-start(bf16[8,3,16,512]{3,2,1,0:T(8,128)(2,1)} %get-tuple-element.13), channel_id=1, source_target_pairs={{0,16},{16,0},{1,17},{17,1},{2,18},{18,2},{3,19},{19,3},{4,20},{20... | collective-permute-start | bytes 1179656 | tf_op jit(solution)/shard_map/ppermute | solution.py:405
  15.5 1.4 %copy-done.8 = bf16[1,3,512,512]{3,2,1,0:T(8,128)(2,1)S(1)} copy-done((bf16[1,3,512,512]{3,2,1,0:T(8,128)(2,1)S(1)}, bf16[1,3,512,512]{3,2,1,0:T(8,128)(2,1)}, u32[]{:S(2)}) %copy-start.8) | copy-done | bytes 1572888
  16.9 4.6 %gradb.1 = (bf16[8,3,16,512]{3,2,1,0:T(8,128)(2,1)S(1)}, bf16[8,3,16,512]{3,2,1,0:T(8,128)(2,1)}) custom-call(s32[1]{0:T(128)} %bitcast.5.me_ref, bf16[1,1024,512]{2,1,0:T(8,128)(2,1)S(1)} %copy-done.3, bf16[1,1024,512]{2,1,0:T(8,128)(2,1)S(1)} %copy-done.5, f32[8,128]{1,0:T(8,128)S(1)} %bitcast.20, bf16[1,3,512,512]{3,2,1,0:T(8,128)(2,1)S(1)} %copy-done.8), custom_call_target="tpu_custom_call" | custom-call | flops 1610612736 | bytes 4194304 | tf_op jit(solution)/shard_map/gradb/pallas_call | solution.py:96
  21.7 1.9 %copy-done.6 = f32[1,3,512,512]{3,2,1,0:T(8,128)S(1)} copy-done((f32[1,3,512,512]{3,2,1,0:T(8,128)S(1)}, f32[1,3,512,512]{3,2,1,0:T(8,128)}, u32[]{:S(2)}) %copy-start.6) | copy-done | bytes 3145752
  23.6 1.4 %copy-done.9 = bf16[1,3,512,512]{3,2,1,0:T(8,128)(2,1)S(1)} copy-done((bf16[1,3,512,512]{3,2,1,0:T(8,128)(2,1)S(1)}, bf16[1,3,512,512]{3,2,1,0:T(8,128)(2,1)}, u32[]{:S(2)}) %copy-start.9) | copy-done | bytes 1572888
  25.0 2.0 %prep.1 = (f32[2,3,16,512]{3,2,1,0:T(8,128)S(1)}, f32[2,3,16,128]{3,2,1,0:T(8,128)S(1)}) custom-call(s32[2]{0:T(128)S(1)} %pad_add_fusion.1.me_ref, bf16[1,3,512,512]{3,2,1,0:T(8,128)(2,1)S(1)} %copy-done.9, f32[1,3,512,512]{3,2,1,0:T(8,128)S(1)} %copy-done.6), custom_call_target="tpu_custom_call" | custom-call | flops 3145728 | bytes 3145728 | tf_op jit(solution)/shard_map/prep/pallas_call | solution.py:205
  27.0 0.8 slice_bitcast_fusion.1
  27.8 1.2 %add_convert_fusion.5 = (bf16[2,3,16,512]{3,2,1,0:T(8,128)(2,1)S(1)}, bf16[2,3,16,512]{3,2,1,0:T(8,128)(2,1)S(1)}, bf16[2,3,16,512]{3,2,1,0:T(8,128)(2,1)S(1)}, bf16[2,3,16,512]{3,2,1,0:T(8,128)(2,1)S(1)}) fusion(bf16[8,3,16,512]{3,2,1,0:T(8,128)(2,1)} %collective-permute-done.12, bf16[8,3,16,512]{3,2,1,0:T(8,128)(2,1)S(1)} %get-tuple-element.14), kind=kLoop, calls=%fused_computation.9 | loop fusion | flops 786432 | bytes 1179648 | tf_op jit(solution)/shard_map/convert_element_type | solution.py:409
  29.0 1.7 %collective-permute-start.15 = (bf16[2,3,16,512]{3,2,1,0:T(8,128)(2,1)S(1)}, bf16[2,3,16,512]{3,2,1,0:T(8,128)(2,1)S(1)}, u32[]{:S(2)}, u32[]{:S(2)}) collective-permute-start(bf16[2,3,16,512]{3,2,1,0:T(8,128)(2,1)S(1)} %get-tuple-element.19), channel_id=1, source_target_pairs={{0,192},{64,128},{128,64},{192,0},{1,193},{65,129},{129,65},{193,1... | collective-permute-start | bytes 294920 | tf_op jit(solution)/shard_map/ppermute | solution.py:405
  30.6 2.1 %collective-permute-start.14 = (bf16[2,3,16,512]{3,2,1,0:T(8,128)(2,1)S(1)}, bf16[2,3,16,512]{3,2,1,0:T(8,128)(2,1)S(1)}, u32[]{:S(2)}, u32[]{:S(2)}) collective-permute-start(bf16[2,3,16,512]{3,2,1,0:T(8,128)(2,1)S(1)} %get-tuple-element.20), channel_id=1, source_target_pairs={{0,128},{64,192},{128,0},{192,64},{1,129},{65,193},{129,1},{193,65... | collective-permute-start | bytes 294920 | tf_op jit(solution)/shard_map/ppermute | solution.py:405
  33.1 4.4 %collective-permute-done.15 = bf16[2,3,16,512]{3,2,1,0:T(8,128)(2,1)S(1)} collective-permute-done((bf16[2,3,16,512]{3,2,1,0:T(8,128)(2,1)S(1)}, bf16[2,3,16,512]{3,2,1,0:T(8,128)(2,1)S(1)}, u32[]{:S(2)}, u32[]{:S(2)}) %collective-permute-start.15) | collective-permute-done | bytes 98336 | tf_op jit(solution)/shard_map/ppermute | solution.py:405
  37.6 1.9 %collective-permute-start = (bf16[512,512]{1,0:T(8,128)(2,1)}, bf16[512,512]{1,0:T(8,128)(2,1)}, u32[]{:S(2)}, u32[]{:S(2)}) collective-permute-start(bf16[512,512]{1,0:T(8,128)(2,1)} %slice_bitcast_fusion.1), channel_id=1, source_target_pairs={{0,16},{16,32},{32,48},{48,64},{64,80},{80,96},{96,112},{112,128},... | collective-permute-start | bytes 1572872 | tf_op jit(solution)/shard_map/ppermute | solution.py:468
  39.7 1.2 %add_convert_fusion.1 = (bf16[4,3,16,512]{3,2,1,0:T(8,128)(2,1)S(1)}, bf16[4,3,16,512]{3,2,1,0:T(8,128)(2,1)S(1)}) fusion(bf16[8,3,16,512]{3,2,1,0:T(8,128)(2,1)} %collective-permute-done.2, bf16[8,3,16,512]{3,2,1,0:T(8,128)(2,1)S(1)} %get-tuple-element.12), kind=kLoop, calls=%fused_computation.3 | loop fusion | flops 786432 | bytes 1179648 | tf_op jit(solution)/shard_map/convert_element_type | solution.py:409
  40.8 2.1 %collective-permute-start.3 = (bf16[4,3,16,512]{3,2,1,0:T(8,128)(2,1)S(1)}, bf16[4,3,16,512]{3,2,1,0:T(8,128)(2,1)S(1)}, u32[]{:S(2)}, u32[]{:S(2)}) collective-permute-start(bf16[4,3,16,512]{3,2,1,0:T(8,128)(2,1)S(1)} %get-tuple-element.23), channel_id=1, source_target_pairs={{0,32},{32,0},{1,33},{33,1},{2,34},{34,2},{3,35},{35,3},{4,36},{36... | collective-permute-start | bytes 589832 | tf_op jit(solution)/shard_map/ppermute | solution.py:405
  42.9 1.3 %collective-permute-done.16.refs_1_ = bf16[1,3,16,512]{3,2,1,0:T(8,128)(2,1)S(1)} collective-permute-done((bf16[1,3,16,512]{3,2,1,0:T(8,128)(2,1)S(1)}, bf16[1,3,16,512]{3,2,1,0:T(8,128)(2,1)S(1)}, u32[]{:S(2)}, u32[]{:S(2)}) %collective-permute-start.16) | collective-permute-done | bytes 49184 | tf_op jit(solution)/shard_map/ppermute | solution.py:405
  45.2 3.6 %collective-permute-done.3 = bf16[4,3,16,512]{3,2,1,0:T(8,128)(2,1)S(1)} collective-permute-done((bf16[4,3,16,512]{3,2,1,0:T(8,128)(2,1)S(1)}, bf16[4,3,16,512]{3,2,1,0:T(8,128)(2,1)S(1)}, u32[]{:S(2)}, u32[]{:S(2)}) %collective-permute-start.3) | collective-permute-done | bytes 196640 | tf_op jit(solution)/shard_map/ppermute | solution.py:405
  48.8 3.3 %collective-permute-start.6 = (bf16[1,3,16,512]{3,2,1,0:T(8,128)(2,1)S(1)}, bf16[1,3,16,512]{3,2,1,0:T(8,128)(2,1)S(1)}, u32[]{:S(2)}, u32[]{:S(2)}) collective-permute-start(bf16[1,3,16,512]{3,2,1,0:T(8,128)(2,1)S(1)} %get-tuple-element.26), channel_id=1, source_target_pairs={{0,192},{64,128},{128,64},{192,0},{1,193},{65,129},{129,65},{193,1... | collective-permute-start | bytes 147464 | tf_op jit(solution)/shard_map/ppermute | solution.py:405
  52.1 1.0 collective-permute-start.4
  54.2 3.7 %collective-permute-start.20 = (bf16[2,3,16,512]{3,2,1,0:T(8,128)(2,1)S(1)}, bf16[2,3,16,512]{3,2,1,0:T(8,128)(2,1)S(1)}, u32[]{:S(2)}, u32[]{:S(2)}) collective-permute-start(bf16[2,3,16,512]{3,2,1,0:T(8,128)(2,1)S(1)} %pad_maximum_fusion.1), channel_id=1, source_target_pairs={{0,192},{64,128},{128,64},{192,0},{1,193},{65,129},{129,65},{193,1... | collective-permute-start | bytes 294920 | tf_op jit(solution)/shard_map/ppermute | solution.py:405
  58.1 0.9 collective-permute-start.9
  59.1 0.9 collective-permute-start.7
  60.6 2.6 %collective-permute-done.7 = bf16[1,3,16,512]{3,2,1,0:T(8,128)(2,1)S(1)} collective-permute-done((bf16[1,3,16,512]{3,2,1,0:T(8,128)(2,1)S(1)}, bf16[1,3,16,512]{3,2,1,0:T(8,128)(2,1)S(1)}, u32[]{:S(2)}, u32[]{:S(2)}) %collective-permute-start.7) | collective-permute-done | bytes 49184 | tf_op jit(solution)/shard_map/ppermute | solution.py:405
  63.1 1.8 %collective-permute-start.8 = (bf16[1,3,16,512]{3,2,1,0:T(8,128)(2,1)S(1)}, bf16[1,3,16,512]{3,2,1,0:T(8,128)(2,1)S(1)}, u32[]{:S(2)}, u32[]{:S(2)}) collective-permute-start(bf16[1,3,16,512]{3,2,1,0:T(8,128)(2,1)S(1)} %bitcast.17), channel_id=1, source_target_pairs={{0,128},{64,192},{128,0},{192,64},{1,129},{65,193},{129,1},{193,65... | collective-permute-start | bytes 147464 | tf_op jit(solution)/shard_map/ppermute | solution.py:405
  65.6 1.7 %collective-permute-start.19 = (bf16[2,3,16,512]{3,2,1,0:T(8,128)(2,1)S(1)}, bf16[2,3,16,512]{3,2,1,0:T(8,128)(2,1)S(1)}, u32[]{:S(2)}, u32[]{:S(2)}) collective-permute-start(bf16[2,3,16,512]{3,2,1,0:T(8,128)(2,1)S(1)} %pad_maximum_fusion.1), channel_id=1, source_target_pairs={{0,128},{64,192},{128,0},{192,64},{1,129},{65,193},{129,1},{193,65... | collective-permute-start | bytes 294920 | tf_op jit(solution)/shard_map/ppermute | solution.py:405
  67.3 1.4 %collective-permute-done.8 = bf16[1,3,16,512]{3,2,1,0:T(8,128)(2,1)S(1)} collective-permute-done((bf16[1,3,16,512]{3,2,1,0:T(8,128)(2,1)S(1)}, bf16[1,3,16,512]{3,2,1,0:T(8,128)(2,1)S(1)}, u32[]{:S(2)}, u32[]{:S(2)}) %collective-permute-start.8) | collective-permute-done | bytes 49184 | tf_op jit(solution)/shard_map/ppermute | solution.py:405
  68.7 1.3 %collective-permute-start.18 = (bf16[2,3,16,512]{3,2,1,0:T(8,128)(2,1)S(1)}, bf16[2,3,16,512]{3,2,1,0:T(8,128)(2,1)S(1)}, u32[]{:S(2)}, u32[]{:S(2)}) collective-permute-start(bf16[2,3,16,512]{3,2,1,0:T(8,128)(2,1)S(1)} %pad_maximum_fusion.1), channel_id=1, source_target_pairs={{0,64},{64,0},{128,192},{192,128},{1,65},{65,1},{129,193},{193,129... | collective-permute-start | bytes 294920 | tf_op jit(solution)/shard_map/ppermute | solution.py:405
  70.7 3.1 %collective-permute-done.18 = bf16[2,3,16,512]{3,2,1,0:T(8,128)(2,1)S(1)} collective-permute-done((bf16[2,3,16,512]{3,2,1,0:T(8,128)(2,1)S(1)}, bf16[2,3,16,512]{3,2,1,0:T(8,128)(2,1)S(1)}, u32[]{:S(2)}, u32[]{:S(2)}) %collective-permute-start.18) | collective-permute-done | bytes 98336 | tf_op jit(solution)/shard_map/ppermute | solution.py:405
  73.8 1.2 %collective-permute-start.10 = (bf16[4,3,16,512]{3,2,1,0:T(8,128)(2,1)S(1)}, bf16[4,3,16,512]{3,2,1,0:T(8,128)(2,1)S(1)}, u32[]{:S(2)}, u32[]{:S(2)}) collective-permute-start(bf16[4,3,16,512]{3,2,1,0:T(8,128)(2,1)S(1)} %pad_maximum_fusion), channel_id=1, source_target_pairs={{0,32},{32,0},{1,33},{33,1},{2,34},{34,2},{3,35},{35,3},{4,36},{36... | collective-permute-start | bytes 589832 | tf_op jit(solution)/shard_map/ppermute | solution.py:405
  76.9 3.2 %collective-permute-done.10 = bf16[4,3,16,512]{3,2,1,0:T(8,128)(2,1)S(1)} collective-permute-done((bf16[4,3,16,512]{3,2,1,0:T(8,128)(2,1)S(1)}, bf16[4,3,16,512]{3,2,1,0:T(8,128)(2,1)S(1)}, u32[]{:S(2)}, u32[]{:S(2)}) %collective-permute-start.10) | collective-permute-done | bytes 196640 | tf_op jit(solution)/shard_map/ppermute | solution.py:405
  80.1 0.7 constant_dynamic-update-slice_fusion.mine_ref.am_ref
  82.4 2.2 %attnb.1.hi_ref = f32[512,512]{1,0:T(8,128)S(1)} custom-call(s32[4]{0:T(128)S(1)} %pad_add_fusion.meta_ref, bf16[1,1024,512]{2,1,0:T(8,128)(2,1)S(1)} %copy-done.1, bf16[1,1024,512]{2,1,0:T(8,128)(2,1)S(1)} %copy-done.3, bf16[1,1024,512]{2,1,0:T(8,128)(2,1)S(1)} %copy-done.5), custom_call_target="tpu_custom_call" | custom-call | flops 805306368 | bytes 4194304 | tf_op jit(solution)/shard_map/attnb/pallas_call | solution.py:175
  84.6 2.9 %attna.1.lo_ref = f32[512,512]{1,0:T(8,128)S(1)} custom-call(s32[4]{0:T(128)S(1)} %pad_add_fusion.meta_ref, bf16[1,1024,512]{2,1,0:T(8,128)(2,1)S(1)} %copy-done.1, bf16[512,512]{1,0:T(8,128)(2,1)} %collective-permute-done.refs_1_, bf16[512,512]{1,0:T(8,128)(2,1)} %collective-permute-done.1.refs_2_, bf16[1,1024,512]{2,1,0:T(8,128)(2,1)S(1)} %copy-done.3, ...), custom_call_target="tpu_custom_call" | custom-call | flops 805306368 | bytes 4194304 | tf_op jit(solution)/shard_map/attna/pallas_call | solution.py:175
  87.5 3.2 %outa.1.y1_ref = f32[1024,512]{1,0:T(8,128)S(1)} custom-call(bf16[1,1024,512]{2,1,0:T(8,128)(2,1)S(1)} %copy-done.1, f32[512,512]{1,0:T(8,128)S(1)} %attna.1.lo_ref, f32[512,512]{1,0:T(8,128)S(1)} %attnb.1.hi_ref, bf16[8,3,16,512]{3,2,1,0:T(8,128)(2,1)} %constant_dynamic-update-slice_fusion.mine_ref.am_ref, ...), custom_call_target="tpu_custom_call" | custom-call | flops 805306368 | bytes 6291456 | tf_op jit(solution)/shard_map/outa/pallas_call | solution.py:298
  90.7 3.5 %outb.1 = (f32[1024,512]{1,0:T(8,128)S(1)}, f32[8,128]{1,0:T(8,128)S(1)}) custom-call(bf16[1,1024,512]{2,1,0:T(8,128)(2,1)S(1)} %copy-done.1, f32[1024,512]{1,0:T(8,128)S(1)} %outa.1.y1_ref, bf16[8,3,16,512]{3,2,1,0:T(8,128)(2,1)} %constant_dynamic-update-slice_fusion.5.mine_ref.bm_ref, bf16[8,3,16,512]{3,2,1,0:T(8,128)(2,1)} %collective-permute-done.21.other_ref.bo_ref), custom_call_target="tpu_custom_call" | custom-call | flops 805306368 | bytes 6291456 | tf_op jit(solution)/shard_map/outb/pallas_call | solution.py:321
  94.2 2.0 %collective-permute-start.22 = (f32[8,128]{1,0:T(8,128)S(1)}, f32[8,128]{1,0:T(8,128)S(1)}, u32[]{:S(2)}, u32[]{:S(2)}) collective-permute-start(f32[8,128]{1,0:T(8,128)S(1)} %get-tuple-element.17), channel_id=1, source_target_pairs={{0,1},{1,0},{2,3},{3,2},{4,5},{5,4},{6,7},{7,6},{8,9},{9,8},{10,11... | collective-permute-start | bytes 12296 | tf_op jit(solution)/shard_map/ppermute | solution.py:405
  96.2 1.7 %collective-permute-done.22 = f32[8,128]{1,0:T(8,128)S(1)} collective-permute-done((f32[8,128]{1,0:T(8,128)S(1)}, f32[8,128]{1,0:T(8,128)S(1)}, u32[]{:S(2)}, u32[]{:S(2)}) %collective-permute-start.22) | collective-permute-done | bytes 4128 | tf_op jit(solution)/shard_map/ppermute | solution.py:405
  97.9 5.9 %collective-permute-start.23 = (f32[8,128]{1,0:T(8,128)S(1)}, f32[8,128]{1,0:T(8,128)S(1)}, u32[]{:S(2)}, u32[]{:S(2)}) collective-permute-start(f32[8,128]{1,0:T(8,128)S(1)} %add.107), channel_id=1, source_target_pairs={{0,7},{1,2},{2,1},{3,4},{4,3},{5,6},{6,5},{7,0},{8,15},{9,10},{10,... | collective-permute-start | bytes 12296 | tf_op jit(solution)/shard_map/ppermute | solution.py:447
  103.8 1.6 %collective-permute-done.23 = f32[8,128]{1,0:T(8,128)S(1)} collective-permute-done((f32[8,128]{1,0:T(8,128)S(1)}, f32[8,128]{1,0:T(8,128)S(1)}, u32[]{:S(2)}, u32[]{:S(2)}) %collective-permute-start.23) | collective-permute-done | bytes 4128 | tf_op jit(solution)/shard_map/ppermute | solution.py:447
  105.4 2.0 %collective-permute-start.24 = (f32[8,128]{1,0:T(8,128)S(1)}, f32[8,128]{1,0:T(8,128)S(1)}, u32[]{:S(2)}, u32[]{:S(2)}) collective-permute-start(f32[8,128]{1,0:T(8,128)S(1)} %add.108.a_ref), channel_id=1, source_target_pairs={{3,0},{6,1},{5,2},{0,3},{7,4},{2,5},{1,6},{4,7},{11,8},{14,9},{13,... | collective-permute-start | bytes 12296 | tf_op jit(solution)/shard_map/ppermute | solution.py:448
  107.4 3.0 %weightsout.1 = bf16[1,3,512,512]{3,2,1,0:T(8,128)(2,1)} custom-call(s32[2]{0:T(128)S(1)} %pad_add_fusion.1.me_ref, bf16[8,3,16,512]{3,2,1,0:T(8,128)(2,1)} %constant_dynamic-update-slice_fusion.mine_ref.am_ref, bf16[8,3,16,512]{3,2,1,0:T(8,128)(2,1)} %collective-permute-done.11.other_ref.ao_ref, ...), custom_call_target="tpu_custom_call" | custom-call | flops 1048576 | bytes 3145728 | tf_op jit(solution)/shard_map/weightsout/pallas_call | solution.py:358
  110.8 1.8 %norm.1 = bf16[1,1024,512]{2,1,0:T(8,128)(2,1)} custom-call(f32[1024,512]{1,0:T(8,128)S(1)} %get-tuple-element.16.y_ref, f32[8,128]{1,0:T(8,128)S(1)} %add.108.a_ref, f32[8,128]{1,0:T(8,128)S(1)} %collective-permute-done.24.b_ref, f32[1,512]{1,0:T(1,128)S(1)} %copy-done.10), custom_call_target="tpu_custom_call" | custom-call | flops 1048576 | bytes 3145728 | tf_op jit(solution)/shard_map/norm/pallas_call | solution.py:387
  (64 shorter events, 8.9 us)
Async XLA Ops:
  0.6 20.9 %copy-start = (s32[2,16384]{1,0:T(2,128)S(1)}, s32[2,16384]{1,0:T(2,128)}, u32[]{:S(2)}) copy-start(s32[2,16384]{1,0:T(2,128)} %param.12) | copy-start | bytes 393220
  2.6 82.0 %collective-permute-start.1 = (bf16[512,512]{1,0:T(8,128)(2,1)}, bf16[512,512]{1,0:T(8,128)(2,1)}, u32[]{:S(2)}, u32[]{:S(2)}) collective-permute-start(bf16[512,512]{1,0:T(8,128)(2,1)} %slice_bitcast_fusion), channel_id=1, source_target_pairs={{0,16},{16,32},{32,48},{48,64},{64,80},{80,96},{96,112},{112,128},... | collective-permute-start | bytes 1572872 | tf_op jit(solution)/shard_map/ppermute | solution.py:469
  4.5 1.2 %copy-start.2 = (bf16[1,1024,512]{2,1,0:T(8,128)(2,1)S(1)}, bf16[1,1024,512]{2,1,0:T(8,128)(2,1)}, u32[]{:S(2)}) copy-start(bf16[1,1024,512]{2,1,0:T(8,128)(2,1)} %k_ref.3) | copy-start | bytes 3145732
  5.7 1.2 %copy-start.4 = (bf16[1,1024,512]{2,1,0:T(8,128)(2,1)S(1)}, bf16[1,1024,512]{2,1,0:T(8,128)(2,1)}, u32[]{:S(2)}) copy-start(bf16[1,1024,512]{2,1,0:T(8,128)(2,1)} %v_ref.3) | copy-start | bytes 3145732
  6.9 1.4 %copy-start.7 = (bf16[1,3,512,512]{3,2,1,0:T(8,128)(2,1)S(1)}, bf16[1,3,512,512]{3,2,1,0:T(8,128)(2,1)}, u32[]{:S(2)}) copy-start(bf16[1,3,512,512]{3,2,1,0:T(8,128)(2,1)} %w_ref.5) | copy-start | bytes 4718596
  8.3 0.7 copy-start.11
  9.0 6.5 %copy-start.3 = (bf16[1,1024,512]{2,1,0:T(8,128)(2,1)S(1)}, bf16[1,1024,512]{2,1,0:T(8,128)(2,1)}, u32[]{:S(2)}) copy-start(bf16[1,1024,512]{2,1,0:T(8,128)(2,1)} %k_ref.3) | copy-start | bytes 3145732
  9.0 6.5 %copy-start.5 = (bf16[1,1024,512]{2,1,0:T(8,128)(2,1)S(1)}, bf16[1,1024,512]{2,1,0:T(8,128)(2,1)}, u32[]{:S(2)}) copy-start(bf16[1,1024,512]{2,1,0:T(8,128)(2,1)} %v_ref.3) | copy-start | bytes 3145732
  9.0 6.5 %copy-start.12 = (f32[1,1024]{1,0:T(1,128)S(1)}, f32[1,1024]{1,0:T(1,128)}, u32[]{:S(2)}) copy-start(f32[1,1024]{1,0:T(1,128)} %param.11) | copy-start | bytes 12292
  13.6 26.1 %collective-permute-start.2 = (bf16[8,3,16,512]{3,2,1,0:T(8,128)(2,1)}, bf16[8,3,16,512]{3,2,1,0:T(8,128)(2,1)}, u32[]{:S(2)}, u32[]{:S(2)}) collective-permute-start(bf16[8,3,16,512]{3,2,1,0:T(8,128)(2,1)} %get-tuple-element.13), channel_id=1, source_target_pairs={{0,16},{16,0},{1,17},{17,1},{2,18},{18,2},{3,19},{19,3},{4,20},{20... | collective-permute-start | bytes 1179656 | tf_op jit(solution)/shard_map/ppermute | solution.py:405
  15.5 1.4 %copy-start.8 = (bf16[1,3,512,512]{3,2,1,0:T(8,128)(2,1)S(1)}, bf16[1,3,512,512]{3,2,1,0:T(8,128)(2,1)}, u32[]{:S(2)}) copy-start(bf16[1,3,512,512]{3,2,1,0:T(8,128)(2,1)} %w_ref.5) | copy-start | bytes 4718596
  21.5 6.3 %collective-permute-start.12 = (bf16[8,3,16,512]{3,2,1,0:T(8,128)(2,1)}, bf16[8,3,16,512]{3,2,1,0:T(8,128)(2,1)}, u32[]{:S(2)}, u32[]{:S(2)}) collective-permute-start(bf16[8,3,16,512]{3,2,1,0:T(8,128)(2,1)} %get-tuple-element.15), channel_id=1, source_target_pairs={{0,16},{16,0},{1,17},{17,1},{2,18},{18,2},{3,19},{19,3},{4,20},{20... | collective-permute-start | bytes 1179656 | tf_op jit(solution)/shard_map/ppermute | solution.py:405
  21.7 1.9 %copy-start.6 = (f32[1,3,512,512]{3,2,1,0:T(8,128)S(1)}, f32[1,3,512,512]{3,2,1,0:T(8,128)}, u32[]{:S(2)}) copy-start(f32[1,3,512,512]{3,2,1,0:T(8,128)} %m_ref.1) | copy-start | bytes 9437188
  23.6 1.4 %copy-start.9 = (bf16[1,3,512,512]{3,2,1,0:T(8,128)(2,1)S(1)}, bf16[1,3,512,512]{3,2,1,0:T(8,128)(2,1)}, u32[]{:S(2)}) copy-start(bf16[1,3,512,512]{3,2,1,0:T(8,128)(2,1)} %w_ref.5) | copy-start | bytes 4718596
  29.0 8.6 %collective-permute-start.15 = (bf16[2,3,16,512]{3,2,1,0:T(8,128)(2,1)S(1)}, bf16[2,3,16,512]{3,2,1,0:T(8,128)(2,1)S(1)}, u32[]{:S(2)}, u32[]{:S(2)}) collective-permute-start(bf16[2,3,16,512]{3,2,1,0:T(8,128)(2,1)S(1)} %get-tuple-element.19), channel_id=1, source_target_pairs={{0,192},{64,128},{128,64},{192,0},{1,193},{65,129},{129,65},{193,1... | collective-permute-start | bytes 294920 | tf_op jit(solution)/shard_map/ppermute | solution.py:405
  30.6 8.9 %collective-permute-start.14 = (bf16[2,3,16,512]{3,2,1,0:T(8,128)(2,1)S(1)}, bf16[2,3,16,512]{3,2,1,0:T(8,128)(2,1)S(1)}, u32[]{:S(2)}, u32[]{:S(2)}) collective-permute-start(bf16[2,3,16,512]{3,2,1,0:T(8,128)(2,1)S(1)} %get-tuple-element.20), channel_id=1, source_target_pairs={{0,128},{64,192},{128,0},{192,64},{1,129},{65,193},{129,1},{193,65... | collective-permute-start | bytes 294920 | tf_op jit(solution)/shard_map/ppermute | solution.py:405
  32.7 6.8 %collective-permute-start.13 = (bf16[2,3,16,512]{3,2,1,0:T(8,128)(2,1)S(1)}, bf16[2,3,16,512]{3,2,1,0:T(8,128)(2,1)S(1)}, u32[]{:S(2)}, u32[]{:S(2)}) collective-permute-start(bf16[2,3,16,512]{3,2,1,0:T(8,128)(2,1)S(1)} %get-tuple-element.21), channel_id=1, source_target_pairs={{0,64},{64,0},{128,192},{192,128},{1,65},{65,1},{129,193},{193,129... | collective-permute-start | bytes 294920 | tf_op jit(solution)/shard_map/ppermute | solution.py:405
  37.6 47.0 %collective-permute-start = (bf16[512,512]{1,0:T(8,128)(2,1)}, bf16[512,512]{1,0:T(8,128)(2,1)}, u32[]{:S(2)}, u32[]{:S(2)}) collective-permute-start(bf16[512,512]{1,0:T(8,128)(2,1)} %slice_bitcast_fusion.1), channel_id=1, source_target_pairs={{0,16},{16,32},{32,48},{48,64},{64,80},{80,96},{96,112},{112,128},... | collective-permute-start | bytes 1572872 | tf_op jit(solution)/shard_map/ppermute | solution.py:468
  39.6 4.6 %collective-permute-start.16 = (bf16[1,3,16,512]{3,2,1,0:T(8,128)(2,1)S(1)}, bf16[1,3,16,512]{3,2,1,0:T(8,128)(2,1)S(1)}, u32[]{:S(2)}, u32[]{:S(2)}) collective-permute-start(bf16[1,3,16,512]{3,2,1,0:T(8,128)(2,1)S(1)} %get-tuple-element.24), channel_id=1, source_target_pairs={{0,32},{32,0},{1,33},{33,1},{2,34},{34,2},{3,35},{35,3},{4,36},{36... | collective-permute-start | bytes 147464 | tf_op jit(solution)/shard_map/ppermute | solution.py:405
  40.8 41.5 %copy-start.1 = (bf16[1,1024,512]{2,1,0:T(8,128)(2,1)S(1)}, bf16[1,1024,512]{2,1,0:T(8,128)(2,1)}, u32[]{:S(2)}) copy-start(bf16[1,1024,512]{2,1,0:T(8,128)(2,1)} %q_ref.3) | copy-start | bytes 3145732
  40.8 7.9 %collective-permute-start.3 = (bf16[4,3,16,512]{3,2,1,0:T(8,128)(2,1)S(1)}, bf16[4,3,16,512]{3,2,1,0:T(8,128)(2,1)S(1)}, u32[]{:S(2)}, u32[]{:S(2)}) collective-permute-start(bf16[4,3,16,512]{3,2,1,0:T(8,128)(2,1)S(1)} %get-tuple-element.23), channel_id=1, source_target_pairs={{0,32},{32,0},{1,33},{33,1},{2,34},{34,2},{3,35},{35,3},{4,36},{36... | collective-permute-start | bytes 589832 | tf_op jit(solution)/shard_map/ppermute | solution.py:405
  44.4 7.7 %collective-permute-start.17 = (bf16[1,3,16,512]{3,2,1,0:T(8,128)(2,1)S(1)}, bf16[1,3,16,512]{3,2,1,0:T(8,128)(2,1)S(1)}, u32[]{:S(2)}, u32[]{:S(2)}) collective-permute-start(bf16[1,3,16,512]{3,2,1,0:T(8,128)(2,1)S(1)} %bitcast.13), channel_id=1, source_target_pairs={{0,32},{32,0},{1,33},{33,1},{2,34},{34,2},{3,35},{35,3},{4,36},{36... | collective-permute-start | bytes 147464 | tf_op jit(solution)/shard_map/ppermute | solution.py:405
  48.8 5.4 %collective-permute-start.6 = (bf16[1,3,16,512]{3,2,1,0:T(8,128)(2,1)S(1)}, bf16[1,3,16,512]{3,2,1,0:T(8,128)(2,1)S(1)}, u32[]{:S(2)}, u32[]{:S(2)}) collective-permute-start(bf16[1,3,16,512]{3,2,1,0:T(8,128)(2,1)S(1)} %get-tuple-element.26), channel_id=1, source_target_pairs={{0,192},{64,128},{128,64},{192,0},{1,193},{65,129},{129,65},{193,1... | collective-permute-start | bytes 147464 | tf_op jit(solution)/shard_map/ppermute | solution.py:405
  52.1 5.8 %collective-permute-start.5 = (bf16[1,3,16,512]{3,2,1,0:T(8,128)(2,1)S(1)}, bf16[1,3,16,512]{3,2,1,0:T(8,128)(2,1)S(1)}, u32[]{:S(2)}, u32[]{:S(2)}) collective-permute-start(bf16[1,3,16,512]{3,2,1,0:T(8,128)(2,1)S(1)} %get-tuple-element.27), channel_id=1, source_target_pairs={{0,128},{64,192},{128,0},{192,64},{1,129},{65,193},{129,1},{193,65... | collective-permute-start | bytes 147464 | tf_op jit(solution)/shard_map/ppermute | solution.py:405
  52.1 5.8 %collective-permute-start.4 = (bf16[1,3,16,512]{3,2,1,0:T(8,128)(2,1)S(1)}, bf16[1,3,16,512]{3,2,1,0:T(8,128)(2,1)S(1)}, u32[]{:S(2)}, u32[]{:S(2)}) collective-permute-start(bf16[1,3,16,512]{3,2,1,0:T(8,128)(2,1)S(1)} %get-tuple-element.28), channel_id=1, source_target_pairs={{0,64},{64,0},{128,192},{192,128},{1,65},{65,1},{129,193},{193,129... | collective-permute-start | bytes 147464 | tf_op jit(solution)/shard_map/ppermute | solution.py:405
  54.2 26.6 %collective-permute-start.20 = (bf16[2,3,16,512]{3,2,1,0:T(8,128)(2,1)S(1)}, bf16[2,3,16,512]{3,2,1,0:T(8,128)(2,1)S(1)}, u32[]{:S(2)}, u32[]{:S(2)}) collective-permute-start(bf16[2,3,16,512]{3,2,1,0:T(8,128)(2,1)S(1)} %pad_maximum_fusion.1), channel_id=1, source_target_pairs={{0,192},{64,128},{128,64},{192,0},{1,193},{65,129},{129,65},{193,1... | collective-permute-start | bytes 294920 | tf_op jit(solution)/shard_map/ppermute | solution.py:405
  58.1 7.5 %collective-permute-start.9 = (bf16[1,3,16,512]{3,2,1,0:T(8,128)(2,1)S(1)}, bf16[1,3,16,512]{3,2,1,0:T(8,128)(2,1)S(1)}, u32[]{:S(2)}, u32[]{:S(2)}) collective-permute-start(bf16[1,3,16,512]{3,2,1,0:T(8,128)(2,1)S(1)} %bitcast.15), channel_id=1, source_target_pairs={{0,192},{64,128},{128,64},{192,0},{1,193},{65,129},{129,65},{193,1... | collective-permute-start | bytes 147464 | tf_op jit(solution)/shard_map/ppermute | solution.py:405
  59.1 4.1 %collective-permute-start.7 = (bf16[1,3,16,512]{3,2,1,0:T(8,128)(2,1)S(1)}, bf16[1,3,16,512]{3,2,1,0:T(8,128)(2,1)S(1)}, u32[]{:S(2)}, u32[]{:S(2)}) collective-permute-start(bf16[1,3,16,512]{3,2,1,0:T(8,128)(2,1)S(1)} %bitcast.16), channel_id=1, source_target_pairs={{0,64},{64,0},{128,192},{192,128},{1,65},{65,1},{129,193},{193,129... | collective-permute-start | bytes 147464 | tf_op jit(solution)/shard_map/ppermute | solution.py:405
  63.1 5.6 %collective-permute-start.8 = (bf16[1,3,16,512]{3,2,1,0:T(8,128)(2,1)S(1)}, bf16[1,3,16,512]{3,2,1,0:T(8,128)(2,1)S(1)}, u32[]{:S(2)}, u32[]{:S(2)}) collective-permute-start(bf16[1,3,16,512]{3,2,1,0:T(8,128)(2,1)S(1)} %bitcast.17), channel_id=1, source_target_pairs={{0,128},{64,192},{128,0},{192,64},{1,129},{65,193},{129,1},{193,65... | collective-permute-start | bytes 147464 | tf_op jit(solution)/shard_map/ppermute | solution.py:405
  65.6 10.7 %collective-permute-start.19 = (bf16[2,3,16,512]{3,2,1,0:T(8,128)(2,1)S(1)}, bf16[2,3,16,512]{3,2,1,0:T(8,128)(2,1)S(1)}, u32[]{:S(2)}, u32[]{:S(2)}) collective-permute-start(bf16[2,3,16,512]{3,2,1,0:T(8,128)(2,1)S(1)} %pad_maximum_fusion.1), channel_id=1, source_target_pairs={{0,128},{64,192},{128,0},{192,64},{1,129},{65,193},{129,1},{193,65... | collective-permute-start | bytes 294920 | tf_op jit(solution)/shard_map/ppermute | solution.py:405
  68.7 5.1 %collective-permute-start.18 = (bf16[2,3,16,512]{3,2,1,0:T(8,128)(2,1)S(1)}, bf16[2,3,16,512]{3,2,1,0:T(8,128)(2,1)S(1)}, u32[]{:S(2)}, u32[]{:S(2)}) collective-permute-start(bf16[2,3,16,512]{3,2,1,0:T(8,128)(2,1)S(1)} %pad_maximum_fusion.1), channel_id=1, source_target_pairs={{0,64},{64,0},{128,192},{192,128},{1,65},{65,1},{129,193},{193,129... | collective-permute-start | bytes 294920 | tf_op jit(solution)/shard_map/ppermute | solution.py:405
  73.8 6.3 %collective-permute-start.10 = (bf16[4,3,16,512]{3,2,1,0:T(8,128)(2,1)S(1)}, bf16[4,3,16,512]{3,2,1,0:T(8,128)(2,1)S(1)}, u32[]{:S(2)}, u32[]{:S(2)}) collective-permute-start(bf16[4,3,16,512]{3,2,1,0:T(8,128)(2,1)S(1)} %pad_maximum_fusion), channel_id=1, source_target_pairs={{0,32},{32,0},{1,33},{33,1},{2,34},{34,2},{3,35},{35,3},{4,36},{36... | collective-permute-start | bytes 589832 | tf_op jit(solution)/shard_map/ppermute | solution.py:405
  80.8 6.7 %collective-permute-start.11 = (bf16[8,3,16,512]{3,2,1,0:T(8,128)(2,1)}, bf16[8,3,16,512]{3,2,1,0:T(8,128)(2,1)}, u32[]{:S(2)}, u32[]{:S(2)}) collective-permute-start(bf16[8,3,16,512]{3,2,1,0:T(8,128)(2,1)} %constant_dynamic-update-slice_fusion.mine_ref.am_ref), channel_id=1, source_target_pairs={{0,16},{16,0},{1,17},{17,1},{2,18},{18,2},{3,19},{19,3},{4,20},{20... | collective-permute-start | bytes 1179656 | tf_op jit(solution)/shard_map/ppermute | solution.py:405
  81.5 9.2 %collective-permute-start.21 = (bf16[8,3,16,512]{3,2,1,0:T(8,128)(2,1)}, bf16[8,3,16,512]{3,2,1,0:T(8,128)(2,1)}, u32[]{:S(2)}, u32[]{:S(2)}) collective-permute-start(bf16[8,3,16,512]{3,2,1,0:T(8,128)(2,1)} %constant_dynamic-update-slice_fusion.5.mine_ref.bm_ref), channel_id=1, source_target_pairs={{0,16},{16,0},{1,17},{17,1},{2,18},{18,2},{3,19},{19,3},{4,20},{20... | collective-permute-start | bytes 1179656 | tf_op jit(solution)/shard_map/ppermute | solution.py:405
  94.2 16.6 %copy-start.10 = (f32[1,512]{1,0:T(1,128)S(1)}, f32[1,512]{1,0:T(1,128)}, u32[]{:S(2)}) copy-start(f32[1,512]{1,0:T(1,128)} %gain_ref.1) | copy-start | bytes 6148
  94.2 3.7 %collective-permute-start.22 = (f32[8,128]{1,0:T(8,128)S(1)}, f32[8,128]{1,0:T(8,128)S(1)}, u32[]{:S(2)}, u32[]{:S(2)}) collective-permute-start(f32[8,128]{1,0:T(8,128)S(1)} %get-tuple-element.17), channel_id=1, source_target_pairs={{0,1},{1,0},{2,3},{3,2},{4,5},{5,4},{6,7},{7,6},{8,9},{9,8},{10,11... | collective-permute-start | bytes 12296 | tf_op jit(solution)/shard_map/ppermute | solution.py:405
  97.9 7.4 %collective-permute-start.23 = (f32[8,128]{1,0:T(8,128)S(1)}, f32[8,128]{1,0:T(8,128)S(1)}, u32[]{:S(2)}, u32[]{:S(2)}) collective-permute-start(f32[8,128]{1,0:T(8,128)S(1)} %add.107), channel_id=1, source_target_pairs={{0,7},{1,2},{2,1},{3,4},{4,3},{5,6},{6,5},{7,0},{8,15},{9,10},{10,... | collective-permute-start | bytes 12296 | tf_op jit(solution)/shard_map/ppermute | solution.py:447
  105.4 5.4 %collective-permute-start.24 = (f32[8,128]{1,0:T(8,128)S(1)}, f32[8,128]{1,0:T(8,128)S(1)}, u32[]{:S(2)}, u32[]{:S(2)}) collective-permute-start(f32[8,128]{1,0:T(8,128)S(1)} %add.108.a_ref), channel_id=1, source_target_pairs={{3,0},{6,1},{5,2},{0,3},{7,4},{2,5},{1,6},{4,7},{11,8},{14,9},{13,... | collective-permute-start | bytes 12296 | tf_op jit(solution)/shard_map/ppermute | solution.py:448

commit v2 on v1

v2 whole, which is shorter than its diff:
```python
import functools
import math

import jax
import jax.numpy as jnp
from jax import lax
from jax.experimental import pallas as pl
from jax.experimental.pallas import tpu as pltpu
from jax.sharding import Mesh, PartitionSpec as P

WINDOW = 512
TILE = 256
BLOCK = 16
MIB = 1024 * 1024
BF16 = jnp.bfloat16
F32 = jnp.float32
NEG = -1e30

Y, X, CORE, SEQ, HEAD = "y", "x", "core", "seq", "head"


def nt(a, b):
    return lax.dot_general(a, b, (((1,), (1,)), ((), ())), preferred_element_type=F32)


def nn(a, b):
    return lax.dot_general(a, b, (((1,), (0,)), ((), ())), preferred_element_type=F32)


def tn(a, b):
    return lax.dot_general(a, b, (((0,), (0,)), ((), ())), preferred_element_type=F32)


def whole():
    return pl.BlockSpec(memory_space=pltpu.VMEM)


def params(limit, **kw):
    return pltpu.CompilerParams(vmem_limit_bytes=limit * MIB, **kw)


def cost(flops, read, trans=0):
    return pl.CostEstimate(flops=int(flops), bytes_accessed=int(read), transcendentals=int(trans))


def column_of(row):
    return jnp.transpose(jnp.broadcast_to(row, (128, 128)))


def grad_kernel(inv, me_ref, k_ref, v_ref, r_ref, w_ref, keep_ref, send_ref, kk, uu, dd, acc):
    step = pl.program_id(0)
    last = pl.num_programs(0) - 1
    here = pl.ds(pl.multiple_of(step * TILE, TILE), TILE)
    keys = k_ref[0]
    kk[here, :] = keys
    tiles = TILE // 128
    parts = []
    for t in range(tiles):
        rate = column_of(r_ref[0:1, t * 128 : (t + 1) * 128])
        rows = v_ref[0, t * 128 : (t + 1) * 128, :].astype(F32)
        wide = jnp.concatenate([rate] * (rows.shape[1] // 128), axis=1)
        parts.append((wide * rows * inv).astype(BF16))
    u = jnp.concatenate(parts, axis=0)
    uu[here, :] = u
    h1 = nn(keys, w_ref[0, 0])
    h3 = nn(keys, w_ref[0, 1])
    dg = nn(u, w_ref[0, 2])
    sig = 0.5 + 0.5 * jnp.tanh(0.5 * h1)
    act = h1 * sig
    dd[0, here, :] = (dg * h3 * (sig + act * (1.0 - sig))).astype(BF16)
    dd[1, here, :] = (dg * act).astype(BF16)
    dd[2, here, :] = (act * h3).astype(BF16)

    @pl.when(step == last)
    def _():
        acc[0] = tn(dd[0], kk[...]).astype(BF16)
        acc[1] = tn(dd[1], kk[...]).astype(BF16)
        acc[2] = tn(dd[2], uu[...]).astype(BF16)
        half = keep_ref.shape[1]
        for h in range(2):
            me = me_ref[h]
            for l in range(2 * half):
                at = pl.multiple_of(((me ^ l) + h * 2 * half) * BLOCK, BLOCK)
                rows = acc[:, pl.ds(at, BLOCK), :]
                if l < half:
                    keep_ref[h, l] = rows
                else:
                    send_ref[h, l - half] = rows


def gradients(me, keys, values, rates, weights, inv):
    rows, dim = keys.shape[1:]
    hidden = weights.shape[3]
    blocks = hidden // BLOCK // 4
    out = jax.ShapeDtypeStruct((2, blocks, 3, BLOCK, dim), BF16)
    tile = pl.BlockSpec((1, TILE, dim), lambda i, s: (0, i, 0))
    return pl.pallas_call(
        functools.partial(grad_kernel, inv),
        grid_spec=pltpu.PrefetchScalarGridSpec(
            num_scalar_prefetch=1,
            grid=(rows // TILE,),
            in_specs=[
                tile,
                tile,
                pl.BlockSpec((1, TILE), lambda i, s: (0, i)),
                pl.BlockSpec(weights.shape, lambda i, s: (0, 0, 0, 0)),
            ],
            out_specs=[whole()] * 2,
            scratch_shapes=[
                pltpu.VMEM((rows, dim), BF16),
                pltpu.VMEM((rows, dim), BF16),
                pltpu.VMEM((3, rows, hidden), BF16),
                pltpu.VMEM((3, hidden, dim), BF16),
            ],
        ),
        out_shape=[out, out],
        compiler_params=params(24),
        cost_estimate=cost(12 * rows * dim * hidden, 6 * MIB, rows * hidden),
        name="grad",
    )(me, keys, values, rates, weights)


def rim_kernel(k_ref, v_ref, rim_ref):
    rim_ref[0] = k_ref[0]
    rim_ref[1] = v_ref[0]


def rim_of(keys, values):
    rows, dim = keys.shape[1:]
    end = pl.BlockSpec((1, WINDOW, dim), lambda i: (0, rows // WINDOW - 1, 0))
    return pl.pallas_call(
        rim_kernel,
        grid=(1,),
        in_specs=[end, end],
        out_specs=whole(),
        out_shape=jax.ShapeDtypeStruct((2, WINDOW, dim), BF16),
        compiler_params=params(6),
        cost_estimate=cost(1, 3 * MIB),
        name="rim",
    )(keys, values)


def attend(q, ks, vs, first, low, scale):
    tile = q.shape[0]
    col = lax.broadcasted_iota(jnp.int32, (tile, tile), 1)
    row = lax.broadcasted_iota(jnp.int32, (tile, tile), 0)
    scores = []
    for b in range(3):
        s = nt(q, ks[b])
        ok = col >= low - (first + b * tile)
        if b == 2:
            ok = ok & (col <= row)
        scores.append(jnp.where(ok, s, NEG))
    top = jnp.max(jnp.maximum(jnp.maximum(scores[0], scores[1]), scores[2]), axis=1, keepdims=True)
    total, out = None, None
    for b in range(3):
        p = jnp.exp2((scores[b] - top) * scale)
        total = p if total is None else total + p
        o = nn(p.astype(BF16), vs[b])
        out = o if out is None else out + o
    return out / jnp.sum(total, axis=1, keepdims=True)


def lowest(meta_ref, first, tile):
    pos = first + 2 * tile + lax.broadcasted_iota(jnp.int32, (tile, 1), 0)
    low = jnp.zeros_like(pos)
    for b in range(1, 4):
        low = jnp.where(pos >= meta_ref[b], meta_ref[b], low)
    return jnp.maximum(low, pos - (WINDOW - 1))


def attn_kernel(scale, part, meta_ref, *refs):
    if part == 0:
        q_ref, rim_ref, k_ref, v_ref, o_ref = refs
    else:
        q_ref, k_ref, v_ref, o_ref = refs
    for t in range(WINDOW // TILE):
        first = meta_ref[0] + part * WINDOW + (t - 2) * TILE
        ks, vs = [], []
        for b in range(3):
            at = part * WINDOW + (t + b - 2) * TILE
            if at < 0:
                at += WINDOW
                ks.append(rim_ref[0, at : at + TILE, :])
                vs.append(rim_ref[1, at : at + TILE, :])
            else:
                ks.append(k_ref[0, at : at + TILE, :])
                vs.append(v_ref[0, at : at + TILE, :])
        q = q_ref[0, t * TILE : (t + 1) * TILE, :]
        o_ref[t * TILE : (t + 1) * TILE, :] = attend(
            q, ks, vs, first, lowest(meta_ref, first, TILE), scale
        )


def attention(part, meta, queries, rims, keys, values):
    dim = queries.shape[2]
    rows = keys.shape[1] if part else WINDOW
    smem = pl.BlockSpec(memory_space=pltpu.SMEM)
    own = pl.BlockSpec((1, rows, dim), lambda i: (0, 0, 0))
    rim = pl.BlockSpec((2, WINDOW, dim), lambda i: (0, 0, 0))
    return pl.pallas_call(
        functools.partial(attn_kernel, math.log2(math.e) / math.sqrt(dim), part),
        grid=(1,),
        in_specs=[smem, pl.BlockSpec((1, WINDOW, dim), lambda i: (0, part, 0))]
        + [rim] * len(rims)
        + [own, own],
        out_specs=pl.BlockSpec((WINDOW, dim), lambda i: (0, 0)),
        out_shape=jax.ShapeDtypeStruct((WINDOW, dim), F32),
        compiler_params=params(14),
        cost_estimate=cost(4 * WINDOW * 3 * TILE * dim, 4 * MIB, 3 * WINDOW * TILE),
        name="attn" + "ab"[part],
    )(meta, queries, *rims, keys, values)


def prep_kernel(me_ref, w_ref, m_ref, base_ref, rms_ref, wt, mt):
    half = pl.program_id(0)
    me = jnp.where(half == 0, me_ref[0], me_ref[1])
    at = pl.multiple_of((me % 8) * BLOCK, BLOCK)
    for m in range(3):
        wt[...] = jnp.transpose(w_ref[0, m].astype(F32))
        mt[...] = jnp.transpose(m_ref[0, m])
        w = wt[pl.ds(at, BLOCK), :]
        base_ref[0, m] = w - 0.9 * mt[pl.ds(at, BLOCK), :]
        rms = jnp.sqrt(jnp.mean(w * w, axis=1, keepdims=True) + 1e-06)
        rms_ref[0, m] = jnp.broadcast_to(rms, (BLOCK, 128))


def prepare(me, weights, momentum):
    dim, hidden = weights.shape[2:]
    pick = lambda i, s: (0, 0, 0, 2 * i + jnp.where(i == 0, s[0], s[1]) // 8)
    return pl.pallas_call(
        prep_kernel,
        grid_spec=pltpu.PrefetchScalarGridSpec(
            num_scalar_prefetch=1,
            grid=(2,),
            in_specs=[pl.BlockSpec((1, 3, dim, 128), pick)] * 2,
            out_specs=[
                pl.BlockSpec((1, 3, BLOCK, dim), lambda i, s: (i, 0, 0, 0)),
                pl.BlockSpec((1, 3, BLOCK, 128), lambda i, s: (i, 0, 0, 0)),
            ],
            scratch_shapes=[pltpu.VMEM((128, dim), F32)] * 2,
        ),
        out_shape=[
            jax.ShapeDtypeStruct((2, 3, BLOCK, dim), F32),
            jax.ShapeDtypeStruct((2, 3, BLOCK, 128), F32),
        ],
        compiler_params=params(12),
        cost_estimate=cost(3 * MIB, 3 * MIB),
        name="prep",
    )(me, weights, momentum)


def renew_kernel(base_ref, rms_ref, a_ref, ga_ref, b_ref, gb_ref, *outs):
    for h, (one, two) in enumerate(((a_ref, ga_ref), (b_ref, gb_ref))):
        cand = base_ref[h] + (one[0].astype(F32) + two[0].astype(F32))
        new = lax.rsqrt(jnp.mean(cand * cand, axis=2, keepdims=True) + 1e-06)
        outs[h][0] = (cand * (rms_ref[h][:, :, :1] * new)).astype(BF16)


def renew(base, rms, *pieces):
    return pl.pallas_call(
        renew_kernel,
        in_specs=[whole()] * 6,
        out_specs=[whole()] * 2,
        out_shape=[jax.ShapeDtypeStruct((1,) + base.shape[1:], BF16)] * 2,
        compiler_params=params(8),
        cost_estimate=cost(MIB, MIB // 2),
        name="renew",
    )(base, rms, *pieces)


def fill(new, mine_ref, other_ref):
    _, half, _, block, dim = mine_ref.shape
    size = half * block
    for m in range(3):
        for h in range(2):
            new[m, 2 * h * size : (2 * h + 1) * size, :] = mine_ref[h, :, m].reshape(size, dim)
            new[m, (2 * h + 1) * size : (2 * h + 2) * size, :] = other_ref[h, :, m].reshape(size, dim)


def fast_part(q, new):
    one = nt(q, new[0])
    three = nt(q, new[1])
    gq = (one * (0.5 + 0.5 * jnp.tanh(0.5 * one)) * three).astype(BF16)
    return nn(gq, new[2])


def out_kernel(q_ref, lo_ref, hi_ref, mine_ref, other_ref, y_ref, ss_ref, new):
    step = pl.program_id(0)

    @pl.when(step == 0)
    def _():
        fill(new, mine_ref, other_ref)

    attn = jnp.where(step < pl.num_programs(0) // 2, lo_ref[...], hi_ref[...])
    y = attn + fast_part(q_ref[0], new)
    y_ref[...] = y
    sq = y * y
    lanes = sq[:, :128]
    for c in range(1, sq.shape[1] // 128):
        lanes = lanes + sq[:, c * 128 : (c + 1) * 128]
    tiles = TILE // 128
    for t in range(tiles):
        turned = jnp.transpose(lanes[t * 128 : (t + 1) * 128, :])
        ss_ref[pl.ds(step * tiles + t, 1), :] = jnp.sum(turned, axis=0, keepdims=True)


def outputs(queries, lo, hi, mine, other):
    rows, dim = queries.shape[1:]
    hidden = 4 * mine.shape[1] * BLOCK
    half = rows // TILE // 2
    full = pl.BlockSpec(mine.shape, lambda i: (0, 0, 0, 0, 0))
    return pl.pallas_call(
        out_kernel,
        grid=(rows // TILE,),
        in_specs=[
            pl.BlockSpec((1, TILE, dim), lambda i: (0, i, 0)),
            pl.BlockSpec((TILE, dim), lambda i: (jnp.minimum(i, half - 1), 0)),
            pl.BlockSpec((TILE, dim), lambda i: (jnp.maximum(i - half, 0), 0)),
            full,
            full,
        ],
        out_specs=[
            pl.BlockSpec((TILE, dim), lambda i: (i, 0)),
            pl.BlockSpec((rows // 128, 128), lambda i: (0, 0)),
        ],
        out_shape=[
            jax.ShapeDtypeStruct((rows, dim), F32),
            jax.ShapeDtypeStruct((rows // 128, 128), F32),
        ],
        scratch_shapes=[pltpu.VMEM((3, hidden, dim), BF16)],
        compiler_params=params(14),
        cost_estimate=cost(6 * rows * dim * hidden, 6 * MIB, rows * hidden),
        name="out",
    )(queries, lo, hi, mine, other)


def weights_kernel(me_ref, mine_ref, other_ref, out_ref, rows):
    half = mine_ref.shape[1]
    for m in range(3):
        for h in range(2):
            for l in range(2 * half):
                at = pl.multiple_of(((me_ref[h] ^ l) + h * 2 * half) * BLOCK, BLOCK)
                rows[pl.ds(at, BLOCK), :] = (
                    mine_ref[h, l, m] if l < half else other_ref[h, l - half, m]
                )
        out_ref[0, m] = jnp.transpose(rows[...])


def weights_out(me, mine, other):
    dim = mine.shape[4]
    hidden = 4 * mine.shape[1] * BLOCK
    return pl.pallas_call(
        weights_kernel,
        in_specs=[pl.BlockSpec(memory_space=pltpu.SMEM)] + [whole()] * 2,
        out_specs=whole(),
        out_shape=jax.ShapeDtypeStruct((1, 3, dim, hidden), BF16),
        scratch_shapes=[pltpu.VMEM((hidden, dim), BF16)],
        compiler_params=params(12),
        cost_estimate=cost(MIB, 3 * MIB),
        name="weightsout",
    )(me, mine, other)


def norm_kernel(count, y_ref, a_ref, b_ref, gain_ref, out_ref):
    step = pl.program_id(0)
    tiles = y_ref.shape[0] // 128
    dim = y_ref.shape[1]
    gain = gain_ref[...]
    for t in range(tiles):
        at = pl.ds(step * tiles + t, 1)
        total = a_ref[at, :] + b_ref[at, :]
        scale = column_of(lax.rsqrt(total * (1.0 / count) + 1e-06))
        wide = jnp.concatenate([scale] * (dim // 128), axis=1)
        rows = slice(t * 128, (t + 1) * 128)
        out_ref[0, rows, :] = (y_ref[rows, :] * wide * gain).astype(BF16)


def norm(y, a, b, gain, count):
    rows, dim = y.shape
    small = pl.BlockSpec(a.shape, lambda i: (0, 0))
    return pl.pallas_call(
        functools.partial(norm_kernel, count),
        grid=(rows // TILE,),
        in_specs=[
            pl.BlockSpec((TILE, dim), lambda i: (i, 0)),
            small,
            small,
            pl.BlockSpec((1, dim), lambda i: (0, 0)),
        ],
        out_specs=pl.BlockSpec((1, TILE, dim), lambda i: (0, i, 0)),
        out_shape=jax.ShapeDtypeStruct((1, rows, dim), BF16),
        compiler_params=params(12),
        cost_estimate=cost(MIB, 3 * MIB),
        name="norm",
    )(y, a, b, gain)


def swap(x, axis, by):
    return lax.ppermute(x, axis, [(i, i ^ by) for i in range(lax.axis_size(axis))])


def added_kernel(*refs):
    pairs = len(refs) // 4
    for p in range(pairs):
        keep, got = refs[2 * p], refs[2 * p + 1]
        n = keep.shape[0] // 2
        for o, part in ((0, slice(0, n)), (1, slice(n, 2 * n))):
            refs[2 * pairs + 2 * p + o][...] = (
                keep[part].astype(F32) + got[part].astype(F32)
            ).astype(BF16)


def first_kernel(keep_ref, got_ref, *outs):
    n = keep_ref.shape[1] // 2
    for h in range(2):
        for o, part in ((0, slice(0, n)), (1, slice(n, 2 * n))):
            outs[2 * h + o][...] = (
                keep_ref[h, part].astype(F32) + got_ref[h, part].astype(F32)
            ).astype(BF16)


def added(kernel, name, *arrays):
    n = arrays[0].shape[-4] // 2
    shape = (n,) + arrays[0].shape[-3:]
    return pl.pallas_call(
        kernel,
        in_specs=[whole()] * len(arrays),
        out_specs=[whole()] * 4,
        out_shape=[jax.ShapeDtypeStruct(shape, BF16)] * 4,
        compiler_params=params(8),
        cost_estimate=cost(MIB, MIB),
        name=name,
    )(*arrays)


def joined_kernel(a_ref, ga_ref, b_ref, gb_ref, *outs):
    n = a_ref.shape[0]
    for h, (one, two) in enumerate(((a_ref, ga_ref), (b_ref, gb_ref))):
        out = outs[h] if len(outs) == 2 else outs[0].at[h]
        out[:n] = one[...]
        out[n:] = two[...]


def joined(last, *arrays):
    n = arrays[0].shape[0]
    shape = (2 * n,) + arrays[0].shape[1:]
    outs = [jax.ShapeDtypeStruct((2,) + shape, BF16)] if last else [jax.ShapeDtypeStruct(shape, BF16)] * 2
    return pl.pallas_call(
        joined_kernel,
        in_specs=[whole()] * 4,
        out_specs=[whole()] * len(outs),
        out_shape=outs,
        compiler_params=params(8),
        cost_estimate=cost(1, MIB),
        name="join%d" % n,
    )(*arrays)


def ring_sum(s):
    n = lax.axis_size(HEAD)
    s = s + swap(s, HEAD, 1)
    s = s + lax.ppermute(s, HEAD, [(i, (i + 1) % n if i % 2 else (i - 1) % n) for i in range(n)])
    far = lax.ppermute(s, HEAD, [((d - 3) % n if d % 2 else (d + 3) % n, d) for d in range(n)])
    return s, far


def per_device(queries, keys, values, rates, doc_ids, fast_weights, momentum, head_gain):
    rows, dim = queries.shape[1:]
    y, x, core = lax.axis_index(Y), lax.axis_index(X), lax.axis_index(CORE)
    ctx = (Y, X, CORE)
    n = lax.axis_size(Y) * lax.axis_size(X) * lax.axis_size(CORE)
    far = y // 2
    near = (y + far) % 2
    me_a = core * 8 + x * 4 + near * 2 + far
    me_b = core * 8 + near * 4 + far * 2 + x
    me = jnp.stack([me_a, me_b]).astype(jnp.int32)
    offset = lax.axis_index(ctx) * rows
    docs = lax.dynamic_index_in_dim(doc_ids, lax.axis_index(SEQ), 0, keepdims=False)
    bounds = jnp.sum(
        docs[None, :] < jnp.arange(1, 4, dtype=jnp.int32)[:, None], axis=1, dtype=jnp.int32
    )
    meta = jnp.concatenate([offset.astype(jnp.int32)[None], bounds])
    inv = 1.0 / math.sqrt(rows * n)
    hbm = lambda array: pltpu.with_memory_space_constraint(array, pltpu.HBM)

    rim = rim_of(hbm(keys), hbm(values))
    rim, me = lax.optimization_barrier((rim, me))
    rim = lax.ppermute(rim, ctx, [(i, (i + 1) % n) for i in range(n)])
    keep, send = gradients(me, hbm(keys), hbm(values), rates, hbm(fast_weights), inv)
    got = swap(send, CORE, 1)
    ka, sa, kb, sb = added(first_kernel, "add8", keep, got)
    ga, gb = swap(sa, X, 1), swap(sb, Y, 1)
    ka, kb, meta = lax.optimization_barrier((ka, kb, meta))
    hi = attention(1, meta, queries, (), keys, values)
    ga, gb, hi = lax.optimization_barrier((ga, gb, hi))
    ka, sa, kb, sb = added(added_kernel, "add4", ka, ga, kb, gb)
    ga, gb = swap(sa, Y, 1), swap(sb, Y, 3)
    ka, kb, me = lax.optimization_barrier((ka, kb, me))
    base, rms = prepare(me, fast_weights, momentum)
    ga, gb, base, rms = lax.optimization_barrier((ga, gb, base, rms))
    ka, sa, kb, sb = added(added_kernel, "add2", ka, ga, kb, gb)
    ga, gb = swap(sa, Y, 3), swap(sb, X, 1)
    na, nb = renew(base, rms, ka, ga, kb, gb)

    na, nb = joined(False, na, swap(na, Y, 3), nb, swap(nb, X, 1))
    na, nb = joined(False, na, swap(na, Y, 1), nb, swap(nb, Y, 3))
    ga, gb = swap(na, X, 1), swap(nb, Y, 1)
    na, nb, rim, meta = lax.optimization_barrier((na, nb, rim, meta))
    lo = attention(0, meta, queries, (rim,), keys, values)
    ga, gb, lo = lax.optimization_barrier((ga, gb, lo))
    (mine,) = joined(True, na, ga, nb, gb)
    other = swap(mine, CORE, 1)
    mixed, squares = outputs(queries, lo, hi, mine, other)
    sums = ring_sum(squares)
    fresh = weights_out(me, mine, other)
    result = norm(mixed, *sums, head_gain, lax.axis_size(HEAD) * dim)
    return result, fresh


def solution(mesh):
    seqs = 2
    sizes = mesh.shape
    fine = Mesh(
        mesh.devices.reshape(sizes["ctx"] // 4, 2, 2, seqs, sizes["hs"] // seqs),
        (Y, X, CORE, SEQ, HEAD),
    )
    ctx, hs = (Y, X, CORE), (SEQ, HEAD)
    return jax.shard_map(
        per_device,
        mesh=fine,
        in_specs=(
            P(hs, ctx, None),
            P(hs, ctx, None),
            P(hs, ctx, None),
            P(hs, ctx),
            P(),
            P(hs, None, None, None),
            P(hs, None, None, None),
            P(hs, None),
        ),
        out_specs=(P(hs, ctx, None), P(hs, None, None, None)),
        check_vma=False,
    )
```

time: 114 us -> 87.4 us (0.77)
  local copies, waits for them, and re-layouts: 18.4 us -> 3.73 us
  starting transfers between devices: 38.5 us -> 28.3 us
  other arithmetic: 2.95 us -> 0.48 us
  waiting for transfers between devices: 23.8 us -> 25.6 us
    unnamed x34 -> x24, local copies, waits for them, and re-layouts: 14.3 us -> 3.67 us
    ppermute x21 -> x15, starting transfers between devices: 26.8 us -> 20.5 us  [swap(): lax.ppermute(x, axis, [(i, i ^ by) for i in range(lax.axis_size(axis))])]
    ppermute x2 -> x1, starting transfers between devices: 3.82 us -> 0.01 us  [per_device(): rim = lax.ppermute(rim, ctx, [(i, (i + 1) % n) for i in range(n)])]
    squeeze x2 -> x0, local copies, waits for them, and re-layouts: 2.73 us -> none  [the longest x1 1.91 us: per_device(): rim_values = lax.ppermute(values[0, rows - WINDOW:], ctx, ahead)]
    convert_element_type x4 -> x0, other arithmetic: 2.43 us -> none  [added(): return sum((x.astype(F32) for x in xs)).astype(BF16)]
    concatenate x2 -> x0, local copies, waits for them, and re-layouts: 1.33 us -> none  [the longest x1 0.69 us: gather_a(): new = jnp.concatenate([new, swap(new, X, 1)], axis=0)]
    ppermute x21 -> x15, waiting for transfers between devices: 21.9 us -> 22.8 us  [swap(): lax.ppermute(x, axis, [(i, i ^ by) for i in range(lax.axis_size(axis))])]
    pallas_call x6 -> x10, Pallas kernels: 16.2 us -> 17 us  [the longest x1 8.16 us: gradients(): pl.pallas_call(functools.partial(grad_kernel, inv), grid_spec=pltpu.Prefe...]
  transfers between devices with their start and end apart: 25 -> 18, of which waited for: 11 -> 14; matrix products, arithmetic and copies ran while one was open for 9% -> 1% of each run, Pallas kernels for 20% -> 24%
where the time goes in v2:
time: 87.4 us; the launch traced here: 87.1 us
  starting transfers between devices  28.3 us (32%)
  Pallas kernels  28.1 us (32%)
  waiting for transfers between devices  25.6 us (29%)
  local copies, waits for them, and re-layouts  3.73 us (4%)
    ppermute x15, waiting for transfers between devices, swap(): lax.ppermute(x, axis, [(i, i ^ by) for i in range(lax.axis_size(axis))])  22.8 us
    ppermute x15, starting transfers between devices, swap(): lax.ppermute(x, axis, [(i, i ^ by) for i in range(lax.axis_size(axis))])  20.5 us
    pallas_call x1, Pallas kernels, gradients(): pl.pallas_call(functools.partial(grad_kernel, inv), grid_spec=pltpu.Prefe...  8.16 us
    ppermute x1, starting transfers between devices, ring_sum(): lax.ppermute(s, HEAD, [(i, (i + 1) % n if i % 2 else (i - 1) % n) for i i...  5.86 us
    pallas_call x2, Pallas kernels, attention(): pl.pallas_call(functools.partial(attn_kernel, math.log2(math.e) / math.sq...  5.09 us
    unnamed x24, local copies, waits for them, and re-layouts  3.67 us
    pallas_call x1, Pallas kernels, outputs(): pl.pallas_call(out_kernel, grid=(rows // TILE,), in_specs=[pl.BlockSpec((...  3.2 us
    pallas_call x3, Pallas kernels, added(): pl.pallas_call(kernel, in_specs=[whole()] * len(arrays), out_specs=[whole...  3.09 us
  transfers between devices with their start and end apart: 18, of which 14 were waited for; matrix products, arithmetic and copies ran while one was open for 1% of the time, Pallas kernels for 24%

profile of v2, /device:TPU:6, one launch (start us, length us, event | category | flops | bytes accessed | tf_op | source)
XLA Modules:
  0.0 87.1 jit_solution(2075142854921652318)
XLA Ops:
  0.7 0.1 pad_add_fusion.me_ref
  0.8 2.2 %rim.1 = bf16[2,512,512]{2,1,0:T(8,128)(2,1)} custom-call(bf16[1,1024,512]{2,1,0:T(8,128)(2,1)} %refs_2_.3, bf16[1,1024,512]{2,1,0:T(8,128)(2,1)} %refs_3_.1), custom_call_target="tpu_custom_call" | custom-call | flops 1 | bytes 3145728 | tf_op jit(solution)/shard_map/rim/pallas_call | solution.py:131
  3.0 8.2 %grad.1 = (bf16[2,8,3,16,512]{4,3,2,1,0:T(8,128)(2,1)S(1)}, bf16[2,8,3,16,512]{4,3,2,1,0:T(8,128)(2,1)}) custom-call(s32[2]{0:T(128)S(1)} %pad_add_fusion.me_ref, bf16[1,1024,512]{2,1,0:T(8,128)(2,1)} %refs_2_.3, bf16[1,1024,512]{2,1,0:T(8,128)(2,1)} %refs_3_.1, f32[1,1024]{1,0:T(1,128)S(1)} %copy-done.11, bf16[1,3,512,512]{3,2,1,0:T(8,128)(2,1)} %w_ref.3), custom_call_target="tpu_custom_call" | custom-call | flops 3221225472 | bytes 6291456 | tf_op jit(solution)/shard_map/grad/pallas_call | solution.py:97
  11.2 0.9 %copy-done.6 = bf16[2,8,3,16,512]{4,3,2,1,0:T(8,128)(2,1)} copy-done((bf16[2,8,3,16,512]{4,3,2,1,0:T(8,128)(2,1)}, bf16[2,8,3,16,512]{4,3,2,1,0:T(8,128)(2,1)S(1)}, u32[]{:S(2)}) %copy-start.6) | copy-done | bytes 786456
  12.1 1.9 %collective-permute-start = (bf16[2,8,3,16,512]{4,3,2,1,0:T(8,128)(2,1)}, bf16[2,8,3,16,512]{4,3,2,1,0:T(8,128)(2,1)}, u32[]{:S(2)}, u32[]{:S(2)}) collective-permute-start(bf16[2,8,3,16,512]{4,3,2,1,0:T(8,128)(2,1)} %get-tuple-element.50), channel_id=1, source_target_pairs={{0,16},{16,0},{1,17},{17,1},{2,18},{18,2},{3,19},{19,3},{4,20},{20... | collective-permute-start | bytes 2359304 | tf_op jit(solution)/shard_map/ppermute | solution.py:400
  14.1 2.2 %collective-permute-done.got_ref = bf16[2,8,3,16,512]{4,3,2,1,0:T(8,128)(2,1)} collective-permute-done((bf16[2,8,3,16,512]{4,3,2,1,0:T(8,128)(2,1)}, bf16[2,8,3,16,512]{4,3,2,1,0:T(8,128)(2,1)}, u32[]{:S(2)}, u32[]{:S(2)}) %collective-permute-start) | collective-permute-done | bytes 786464 | tf_op jit(solution)/shard_map/ppermute | solution.py:400
  16.3 1.1 %copy-done.7 = bf16[2,8,3,16,512]{4,3,2,1,0:T(8,128)(2,1)S(1)} copy-done((bf16[2,8,3,16,512]{4,3,2,1,0:T(8,128)(2,1)S(1)}, bf16[2,8,3,16,512]{4,3,2,1,0:T(8,128)(2,1)}, u32[]{:S(2)}) %copy-start.7) | copy-done | bytes 786456
  17.4 1.9 %add8.1 = (bf16[4,3,16,512]{3,2,1,0:T(8,128)(2,1)S(1)}, bf16[4,3,16,512]{3,2,1,0:T(8,128)(2,1)}, bf16[4,3,16,512]{3,2,1,0:T(8,128)(2,1)S(1)}, bf16[4,3,16,512]{3,2,1,0:T(8,128)(2,1)}) custom-call(bf16[2,8,3,16,512]{4,3,2,1,0:T(8,128)(2,1)S(1)} %copy-done.7, bf16[2,8,3,16,512]{4,3,2,1,0:T(8,128)(2,1)} %collective-permute-done.got_ref), custom_call_target="tpu_custom_call" | custom-call | flops 1048576 | bytes 1048576 | tf_op jit(solution)/shard_map/add8/pallas_call | solution.py:426
  19.4 0.7 copy-done.8
  20.0 0.2 collective-permute-start.1
  20.2 1.6 %collective-permute-start.2 = (bf16[4,3,16,512]{3,2,1,0:T(8,128)(2,1)}, bf16[4,3,16,512]{3,2,1,0:T(8,128)(2,1)}, u32[]{:S(2)}, u32[]{:S(2)}) collective-permute-start(bf16[4,3,16,512]{3,2,1,0:T(8,128)(2,1)} %get-tuple-element.55), channel_id=1, source_target_pairs={{0,64},{64,0},{128,192},{192,128},{1,65},{65,1},{129,193},{193,129... | collective-permute-start | bytes 589832 | tf_op jit(solution)/shard_map/ppermute | solution.py:400
  21.8 0.3 convert_reduce_fusion
  22.2 2.2 %attnb.1.hi_ref = f32[512,512]{1,0:T(8,128)S(1)} custom-call(s32[4]{0:T(128)S(1)} %pad_add_fusion.1.meta_ref, bf16[1,1024,512]{2,1,0:T(8,128)(2,1)S(1)} %copy-done.3, bf16[1,1024,512]{2,1,0:T(8,128)(2,1)S(1)} %copy-done.1, bf16[1,1024,512]{2,1,0:T(8,128)(2,1)S(1)} %copy-done.2), custom_call_target="tpu_custom_call" | custom-call | flops 805306368 | bytes 4194304 | tf_op jit(solution)/shard_map/attnb/pallas_call | solution.py:201
  24.4 3.1 %collective-permute-done.1.refs_1_ = bf16[4,3,16,512]{3,2,1,0:T(8,128)(2,1)} collective-permute-done((bf16[4,3,16,512]{3,2,1,0:T(8,128)(2,1)}, bf16[4,3,16,512]{3,2,1,0:T(8,128)(2,1)}, u32[]{:S(2)}, u32[]{:S(2)}) %collective-permute-start.1) | collective-permute-done | bytes 196640 | tf_op jit(solution)/shard_map/ppermute | solution.py:400
  27.5 0.9 %copy-done.9 = bf16[4,3,16,512]{3,2,1,0:T(8,128)(2,1)S(1)} copy-done((bf16[4,3,16,512]{3,2,1,0:T(8,128)(2,1)S(1)}, bf16[4,3,16,512]{3,2,1,0:T(8,128)(2,1)}, u32[]{:S(2)}) %copy-start.9) | copy-done | bytes 196632
  28.5 1.1 %add4.1 = (bf16[2,3,16,512]{3,2,1,0:T(8,128)(2,1)S(1)}, bf16[2,3,16,512]{3,2,1,0:T(8,128)(2,1)S(1)}, bf16[2,3,16,512]{3,2,1,0:T(8,128)(2,1)S(1)}, bf16[2,3,16,512]{3,2,1,0:T(8,128)(2,1)S(1)}) custom-call(bf16[4,3,16,512]{3,2,1,0:T(8,128)(2,1)S(1)} %get-tuple-element.53.refs_0_, bf16[4,3,16,512]{3,2,1,0:T(8,128)(2,1)} %collective-permute-done.1.refs_1_, ...), custom_call_target="tpu_custom_call" | custom-call | flops 1048576 | bytes 1048576 | tf_op jit(solution)/shard_map/add4/pallas_call | solution.py:426
  29.6 1.7 %collective-permute-start.3 = (bf16[2,3,16,512]{3,2,1,0:T(8,128)(2,1)S(1)}, bf16[2,3,16,512]{3,2,1,0:T(8,128)(2,1)S(1)}, u32[]{:S(2)}, u32[]{:S(2)}) collective-permute-start(bf16[2,3,16,512]{3,2,1,0:T(8,128)(2,1)S(1)} %get-tuple-element.60), channel_id=1, source_target_pairs={{0,64},{64,0},{128,192},{192,128},{1,65},{65,1},{129,193},{193,129... | collective-permute-start | bytes 294920 | tf_op jit(solution)/shard_map/ppermute | solution.py:400
  31.2 2.1 %collective-permute-start.4 = (bf16[2,3,16,512]{3,2,1,0:T(8,128)(2,1)S(1)}, bf16[2,3,16,512]{3,2,1,0:T(8,128)(2,1)S(1)}, u32[]{:S(2)}, u32[]{:S(2)}) collective-permute-start(bf16[2,3,16,512]{3,2,1,0:T(8,128)(2,1)S(1)} %get-tuple-element.61), channel_id=1, source_target_pairs={{0,192},{64,128},{128,64},{192,0},{1,193},{65,129},{129,65},{193,1... | collective-permute-start | bytes 294920 | tf_op jit(solution)/shard_map/ppermute | solution.py:400
  33.3 2.0 %prep.1 = (f32[2,3,16,512]{3,2,1,0:T(8,128)S(1)}, f32[2,3,16,128]{3,2,1,0:T(8,128)S(1)}) custom-call(s32[2]{0:T(128)S(1)} %pad_add_fusion.me_ref, bf16[1,3,512,512]{3,2,1,0:T(8,128)(2,1)S(1)} %copy-done.5, f32[1,3,512,512]{3,2,1,0:T(8,128)S(1)} %copy-done.4), custom_call_target="tpu_custom_call" | custom-call | flops 3145728 | bytes 3145728 | tf_op jit(solution)/shard_map/prep/pallas_call | solution.py:231
  35.3 1.7 %collective-permute-done.4.refs_3_ = bf16[2,3,16,512]{3,2,1,0:T(8,128)(2,1)S(1)} collective-permute-done((bf16[2,3,16,512]{3,2,1,0:T(8,128)(2,1)S(1)}, bf16[2,3,16,512]{3,2,1,0:T(8,128)(2,1)S(1)}, u32[]{:S(2)}, u32[]{:S(2)}) %collective-permute-start.4) | collective-permute-done | bytes 98336 | tf_op jit(solution)/shard_map/ppermute | solution.py:400
  37.1 2.2 %collective-permute-start.5 = (bf16[1,3,16,512]{3,2,1,0:T(8,128)(2,1)S(1)}, bf16[1,3,16,512]{3,2,1,0:T(8,128)(2,1)S(1)}, u32[]{:S(2)}, u32[]{:S(2)}) collective-permute-start(bf16[1,3,16,512]{3,2,1,0:T(8,128)(2,1)S(1)} %get-tuple-element.74), channel_id=1, source_target_pairs={{0,192},{64,128},{128,64},{192,0},{1,193},{65,129},{129,65},{193,1... | collective-permute-start | bytes 147464 | tf_op jit(solution)/shard_map/ppermute | solution.py:400
  39.3 1.5 %collective-permute-start.6 = (bf16[1,3,16,512]{3,2,1,0:T(8,128)(2,1)S(1)}, bf16[1,3,16,512]{3,2,1,0:T(8,128)(2,1)S(1)}, u32[]{:S(2)}, u32[]{:S(2)}) collective-permute-start(bf16[1,3,16,512]{3,2,1,0:T(8,128)(2,1)S(1)} %get-tuple-element.76), channel_id=1, source_target_pairs={{0,32},{32,0},{1,33},{33,1},{2,34},{34,2},{3,35},{35,3},{4,36},{36... | collective-permute-start | bytes 147464 | tf_op jit(solution)/shard_map/ppermute | solution.py:400
  40.8 1.7 %collective-permute-done.5.ga_ref = bf16[1,3,16,512]{3,2,1,0:T(8,128)(2,1)S(1)} collective-permute-done((bf16[1,3,16,512]{3,2,1,0:T(8,128)(2,1)S(1)}, bf16[1,3,16,512]{3,2,1,0:T(8,128)(2,1)S(1)}, u32[]{:S(2)}, u32[]{:S(2)}) %collective-permute-start.5) | collective-permute-done | bytes 49184 | tf_op jit(solution)/shard_map/ppermute | solution.py:400
  42.5 0.9 %collective-permute-done.6.gb_ref = bf16[1,3,16,512]{3,2,1,0:T(8,128)(2,1)S(1)} collective-permute-done((bf16[1,3,16,512]{3,2,1,0:T(8,128)(2,1)S(1)}, bf16[1,3,16,512]{3,2,1,0:T(8,128)(2,1)S(1)}, u32[]{:S(2)}, u32[]{:S(2)}) %collective-permute-start.6) | collective-permute-done | bytes 49184 | tf_op jit(solution)/shard_map/ppermute | solution.py:400
  43.4 0.2 renew.1
  43.6 1.3 %collective-permute-start.7 = (bf16[1,3,16,512]{3,2,1,0:T(8,128)(2,1)S(1)}, bf16[1,3,16,512]{3,2,1,0:T(8,128)(2,1)S(1)}, u32[]{:S(2)}, u32[]{:S(2)}) collective-permute-start(bf16[1,3,16,512]{3,2,1,0:T(8,128)(2,1)S(1)} %get-tuple-element.77.a_ref), channel_id=1, source_target_pairs={{0,192},{64,128},{128,64},{192,0},{1,193},{65,129},{129,65},{193,1... | collective-permute-start | bytes 147464 | tf_op jit(solution)/shard_map/ppermute | solution.py:400
  44.9 1.7 %collective-permute-start.8 = (bf16[1,3,16,512]{3,2,1,0:T(8,128)(2,1)S(1)}, bf16[1,3,16,512]{3,2,1,0:T(8,128)(2,1)S(1)}, u32[]{:S(2)}, u32[]{:S(2)}) collective-permute-start(bf16[1,3,16,512]{3,2,1,0:T(8,128)(2,1)S(1)} %get-tuple-element.78.b_ref), channel_id=1, source_target_pairs={{0,32},{32,0},{1,33},{33,1},{2,34},{34,2},{3,35},{35,3},{4,36},{36... | collective-permute-start | bytes 147464 | tf_op jit(solution)/shard_map/ppermute | solution.py:400
  46.6 2.9 %collective-permute-done.7.ga_ref = bf16[1,3,16,512]{3,2,1,0:T(8,128)(2,1)S(1)} collective-permute-done((bf16[1,3,16,512]{3,2,1,0:T(8,128)(2,1)S(1)}, bf16[1,3,16,512]{3,2,1,0:T(8,128)(2,1)S(1)}, u32[]{:S(2)}, u32[]{:S(2)}) %collective-permute-start.7) | collective-permute-done | bytes 49184 | tf_op jit(solution)/shard_map/ppermute | solution.py:400
  49.5 0.1 collective-permute-start.9
  49.6 1.6 %collective-permute-start.10 = (bf16[2,3,16,512]{3,2,1,0:T(8,128)(2,1)S(1)}, bf16[2,3,16,512]{3,2,1,0:T(8,128)(2,1)S(1)}, u32[]{:S(2)}, u32[]{:S(2)}) collective-permute-start(bf16[2,3,16,512]{3,2,1,0:T(8,128)(2,1)S(1)} %get-tuple-element.80.b_ref), channel_id=1, source_target_pairs={{0,192},{64,128},{128,64},{192,0},{1,193},{65,129},{129,65},{193,1... | collective-permute-start | bytes 294920 | tf_op jit(solution)/shard_map/ppermute | solution.py:400
  51.2 3.5 %collective-permute-done.9.ga_ref = bf16[2,3,16,512]{3,2,1,0:T(8,128)(2,1)S(1)} collective-permute-done((bf16[2,3,16,512]{3,2,1,0:T(8,128)(2,1)S(1)}, bf16[2,3,16,512]{3,2,1,0:T(8,128)(2,1)S(1)}, u32[]{:S(2)}, u32[]{:S(2)}) %collective-permute-start.9) | collective-permute-done | bytes 98336 | tf_op jit(solution)/shard_map/ppermute | solution.py:400
  54.7 0.8 collective-permute-done.10.gb_ref
  55.6 1.8 %collective-permute-start.11 = (bf16[4,3,16,512]{3,2,1,0:T(8,128)(2,1)S(1)}, bf16[4,3,16,512]{3,2,1,0:T(8,128)(2,1)S(1)}, u32[]{:S(2)}, u32[]{:S(2)}) collective-permute-start(bf16[4,3,16,512]{3,2,1,0:T(8,128)(2,1)S(1)} %get-tuple-element.88.a_ref), channel_id=1, source_target_pairs={{0,32},{32,0},{1,33},{33,1},{2,34},{34,2},{3,35},{35,3},{4,36},{36... | collective-permute-start | bytes 589832 | tf_op jit(solution)/shard_map/ppermute | solution.py:400
  57.4 0.7 collective-permute-start.12
  58.1 2.9 %attna.1.lo_ref = f32[512,512]{1,0:T(8,128)S(1)} custom-call(s32[4]{0:T(128)S(1)} %pad_add_fusion.1.meta_ref, bf16[1,1024,512]{2,1,0:T(8,128)(2,1)S(1)} %copy-done.3, bf16[2,512,512]{2,1,0:T(8,128)(2,1)} %collective-permute-done.13.refs_1_, bf16[1,1024,512]{2,1,0:T(8,128)(2,1)S(1)} %copy-done.1, bf16[1,1024,512]{2,1,0:T(8,128)(2,1)S(1)} %copy-done.2), custom_call_target="tpu_custom_call" | custom-call | flops 805306368 | bytes 4194304 | tf_op jit(solution)/shard_map/attna/pallas_call | solution.py:201
  61.0 0.5 collective-permute-done.11.ga_ref
  61.5 1.6 %collective-permute-done.12.gb_ref = bf16[4,3,16,512]{3,2,1,0:T(8,128)(2,1)S(1)} collective-permute-done((bf16[4,3,16,512]{3,2,1,0:T(8,128)(2,1)S(1)}, bf16[4,3,16,512]{3,2,1,0:T(8,128)(2,1)S(1)}, u32[]{:S(2)}, u32[]{:S(2)}) %collective-permute-start.12) | collective-permute-done | bytes 196640 | tf_op jit(solution)/shard_map/ppermute | solution.py:400
  63.1 0.1 collective-permute-start.14
  63.2 2.3 %collective-permute-done.14.other_ref = bf16[2,8,3,16,512]{4,3,2,1,0:T(8,128)(2,1)S(1)} collective-permute-done((bf16[2,8,3,16,512]{4,3,2,1,0:T(8,128)(2,1)S(1)}, bf16[2,8,3,16,512]{4,3,2,1,0:T(8,128)(2,1)S(1)}, u32[]{:S(2)}, u32[]{:S(2)}) %collective-permute-start.14) | collective-permute-done | bytes 786464 | tf_op jit(solution)/shard_map/ppermute | solution.py:400
  65.5 3.2 %out.1 = (f32[1024,512]{1,0:T(8,128)S(1)}, f32[8,128]{1,0:T(8,128)S(1)}) custom-call(bf16[1,1024,512]{2,1,0:T(8,128)(2,1)S(1)} %copy-done.3, f32[512,512]{1,0:T(8,128)S(1)} %attna.1.lo_ref, f32[512,512]{1,0:T(8,128)S(1)} %attnb.1.hi_ref, bf16[2,8,3,16,512]{4,3,2,1,0:T(8,128)(2,1)S(1)} %join4.1.mine_ref, ...), custom_call_target="tpu_custom_call" | custom-call | flops 1610612736 | bytes 6291456 | tf_op jit(solution)/shard_map/out/pallas_call | solution.py:313
  68.7 2.0 %collective-permute-start.15 = (f32[8,128]{1,0:T(8,128)S(1)}, f32[8,128]{1,0:T(8,128)S(1)}, u32[]{:S(2)}, u32[]{:S(2)}) collective-permute-start(f32[8,128]{1,0:T(8,128)S(1)} %get-tuple-element.93), channel_id=1, source_target_pairs={{0,1},{1,0},{2,3},{3,2},{4,5},{5,4},{6,7},{7,6},{8,9},{9,8},{10,11... | collective-permute-start | bytes 12296 | tf_op jit(solution)/shard_map/ppermute | solution.py:400
  70.7 1.7 %collective-permute-done.15 = f32[8,128]{1,0:T(8,128)S(1)} collective-permute-done((f32[8,128]{1,0:T(8,128)S(1)}, f32[8,128]{1,0:T(8,128)S(1)}, u32[]{:S(2)}, u32[]{:S(2)}) %collective-permute-start.15) | collective-permute-done | bytes 4128 | tf_op jit(solution)/shard_map/ppermute | solution.py:400
  72.4 5.9 %collective-permute-start.16 = (f32[8,128]{1,0:T(8,128)S(1)}, f32[8,128]{1,0:T(8,128)S(1)}, u32[]{:S(2)}, u32[]{:S(2)}) collective-permute-start(f32[8,128]{1,0:T(8,128)S(1)} %add.61), channel_id=1, source_target_pairs={{0,7},{1,2},{2,1},{3,4},{4,3},{5,6},{6,5},{7,0},{8,15},{9,10},{10,... | collective-permute-start | bytes 12296 | tf_op jit(solution)/shard_map/ppermute | solution.py:463
  78.3 1.6 %collective-permute-done.16 = f32[8,128]{1,0:T(8,128)S(1)} collective-permute-done((f32[8,128]{1,0:T(8,128)S(1)}, f32[8,128]{1,0:T(8,128)S(1)}, u32[]{:S(2)}, u32[]{:S(2)}) %collective-permute-start.16) | collective-permute-done | bytes 4128 | tf_op jit(solution)/shard_map/ppermute | solution.py:463
  79.9 2.0 %collective-permute-start.17 = (f32[8,128]{1,0:T(8,128)S(1)}, f32[8,128]{1,0:T(8,128)S(1)}, u32[]{:S(2)}, u32[]{:S(2)}) collective-permute-start(f32[8,128]{1,0:T(8,128)S(1)} %add.62.a_ref), channel_id=1, source_target_pairs={{3,0},{6,1},{5,2},{0,3},{7,4},{2,5},{1,6},{4,7},{11,8},{14,9},{13,... | collective-permute-start | bytes 12296 | tf_op jit(solution)/shard_map/ppermute | solution.py:464
  81.9 2.2 %weightsout.1 = bf16[1,3,512,512]{3,2,1,0:T(8,128)(2,1)} custom-call(s32[2]{0:T(128)S(1)} %pad_add_fusion.me_ref, bf16[2,8,3,16,512]{4,3,2,1,0:T(8,128)(2,1)S(1)} %join4.1.mine_ref, bf16[2,8,3,16,512]{4,3,2,1,0:T(8,128)(2,1)S(1)} %collective-permute-done.14.other_ref), custom_call_target="tpu_custom_call" | custom-call | flops 1048576 | bytes 3145728 | tf_op jit(solution)/shard_map/weightsout/pallas_call | solution.py:353
  84.1 1.2 %collective-permute-done.17.b_ref = f32[8,128]{1,0:T(8,128)S(1)} collective-permute-done((f32[8,128]{1,0:T(8,128)S(1)}, f32[8,128]{1,0:T(8,128)S(1)}, u32[]{:S(2)}, u32[]{:S(2)}) %collective-permute-start.17) | collective-permute-done | bytes 4128 | tf_op jit(solution)/shard_map/ppermute | solution.py:464
  85.3 1.8 %norm.1 = bf16[1,1024,512]{2,1,0:T(8,128)(2,1)} custom-call(f32[1024,512]{1,0:T(8,128)S(1)} %get-tuple-element.92.y_ref, f32[8,128]{1,0:T(8,128)S(1)} %add.62.a_ref, f32[8,128]{1,0:T(8,128)S(1)} %collective-permute-done.17.b_ref, f32[1,512]{1,0:T(1,128)S(1)} %copy-done.10), custom_call_target="tpu_custom_call" | custom-call | flops 1048576 | bytes 3145728 | tf_op jit(solution)/shard_map/norm/pallas_call | solution.py:382
  (34 shorter events, 0.3 us)
Async XLA Ops:
  0.6 13.4 %copy-start = (s32[2,16384]{1,0:T(2,128)S(1)}, s32[2,16384]{1,0:T(2,128)}, u32[]{:S(2)}) copy-start(s32[2,16384]{1,0:T(2,128)} %param.12) | copy-start | bytes 393220
  0.6 2.4 %copy-start.11 = (f32[1,1024]{1,0:T(1,128)S(1)}, f32[1,1024]{1,0:T(1,128)}, u32[]{:S(2)}) copy-start(f32[1,1024]{1,0:T(1,128)} %r_ref.1) | copy-start | bytes 12292
  3.0 55.1 %collective-permute-start.13 = (bf16[2,512,512]{2,1,0:T(8,128)(2,1)}, bf16[2,512,512]{2,1,0:T(8,128)(2,1)}, u32[]{:S(2)}, u32[]{:S(2)}) collective-permute-start(bf16[2,512,512]{2,1,0:T(8,128)(2,1)} %rim.1), channel_id=1, source_target_pairs={{0,16},{16,32},{32,48},{48,64},{64,80},{80,96},{96,112},{112,128},... | collective-permute-start | bytes 3145736 | tf_op jit(solution)/shard_map/ppermute | solution.py:489
  3.0 19.2 %copy-start.2 = (bf16[1,1024,512]{2,1,0:T(8,128)(2,1)S(1)}, bf16[1,1024,512]{2,1,0:T(8,128)(2,1)}, u32[]{:S(2)}) copy-start(bf16[1,1024,512]{2,1,0:T(8,128)(2,1)} %refs_3_.1) | copy-start | bytes 3145732
  3.0 19.2 %copy-start.3 = (bf16[1,1024,512]{2,1,0:T(8,128)(2,1)S(1)}, bf16[1,1024,512]{2,1,0:T(8,128)(2,1)}, u32[]{:S(2)}) copy-start(bf16[1,1024,512]{2,1,0:T(8,128)(2,1)} %q_ref.1) | copy-start | bytes 3145732
  11.2 0.9 %copy-start.6 = (bf16[2,8,3,16,512]{4,3,2,1,0:T(8,128)(2,1)}, bf16[2,8,3,16,512]{4,3,2,1,0:T(8,128)(2,1)S(1)}, u32[]{:S(2)}) copy-start(bf16[2,8,3,16,512]{4,3,2,1,0:T(8,128)(2,1)S(1)} %get-tuple-element.49.keep_ref) | copy-start | bytes 2359300
  12.1 10.1 %copy-start.1 = (bf16[1,1024,512]{2,1,0:T(8,128)(2,1)S(1)}, bf16[1,1024,512]{2,1,0:T(8,128)(2,1)}, u32[]{:S(2)}) copy-start(bf16[1,1024,512]{2,1,0:T(8,128)(2,1)} %refs_2_.3) | copy-start | bytes 3145732
  12.1 4.2 %collective-permute-start = (bf16[2,8,3,16,512]{4,3,2,1,0:T(8,128)(2,1)}, bf16[2,8,3,16,512]{4,3,2,1,0:T(8,128)(2,1)}, u32[]{:S(2)}, u32[]{:S(2)}) collective-permute-start(bf16[2,8,3,16,512]{4,3,2,1,0:T(8,128)(2,1)} %get-tuple-element.50), channel_id=1, source_target_pairs={{0,16},{16,0},{1,17},{17,1},{2,18},{18,2},{3,19},{19,3},{4,20},{20... | collective-permute-start | bytes 2359304 | tf_op jit(solution)/shard_map/ppermute | solution.py:400
  16.3 1.1 %copy-start.7 = (bf16[2,8,3,16,512]{4,3,2,1,0:T(8,128)(2,1)S(1)}, bf16[2,8,3,16,512]{4,3,2,1,0:T(8,128)(2,1)}, u32[]{:S(2)}) copy-start(bf16[2,8,3,16,512]{4,3,2,1,0:T(8,128)(2,1)} %copy-done.6) | copy-start | bytes 2359300
  19.4 0.7 copy-start.8
  20.0 7.5 %collective-permute-start.1 = (bf16[4,3,16,512]{3,2,1,0:T(8,128)(2,1)}, bf16[4,3,16,512]{3,2,1,0:T(8,128)(2,1)}, u32[]{:S(2)}, u32[]{:S(2)}) collective-permute-start(bf16[4,3,16,512]{3,2,1,0:T(8,128)(2,1)} %get-tuple-element.54), channel_id=1, source_target_pairs={{0,32},{32,0},{1,33},{33,1},{2,34},{34,2},{3,35},{35,3},{4,36},{36... | collective-permute-start | bytes 589832 | tf_op jit(solution)/shard_map/ppermute | solution.py:400
  20.2 7.3 %collective-permute-start.2 = (bf16[4,3,16,512]{3,2,1,0:T(8,128)(2,1)}, bf16[4,3,16,512]{3,2,1,0:T(8,128)(2,1)}, u32[]{:S(2)}, u32[]{:S(2)}) collective-permute-start(bf16[4,3,16,512]{3,2,1,0:T(8,128)(2,1)} %get-tuple-element.55), channel_id=1, source_target_pairs={{0,64},{64,0},{128,192},{192,128},{1,65},{65,1},{129,193},{193,129... | collective-permute-start | bytes 589832 | tf_op jit(solution)/shard_map/ppermute | solution.py:400
  22.2 11.1 %copy-start.4 = (f32[1,3,512,512]{3,2,1,0:T(8,128)S(1)}, f32[1,3,512,512]{3,2,1,0:T(8,128)}, u32[]{:S(2)}) copy-start(f32[1,3,512,512]{3,2,1,0:T(8,128)} %m_ref.1) | copy-start | bytes 9437188
  22.2 11.1 %copy-start.5 = (bf16[1,3,512,512]{3,2,1,0:T(8,128)(2,1)S(1)}, bf16[1,3,512,512]{3,2,1,0:T(8,128)(2,1)}, u32[]{:S(2)}) copy-start(bf16[1,3,512,512]{3,2,1,0:T(8,128)(2,1)} %w_ref.3) | copy-start | bytes 4718596
  27.5 0.9 %copy-start.9 = (bf16[4,3,16,512]{3,2,1,0:T(8,128)(2,1)S(1)}, bf16[4,3,16,512]{3,2,1,0:T(8,128)(2,1)}, u32[]{:S(2)}) copy-start(bf16[4,3,16,512]{3,2,1,0:T(8,128)(2,1)} %copy-done.8) | copy-start | bytes 589828
  29.6 5.7 %collective-permute-start.3 = (bf16[2,3,16,512]{3,2,1,0:T(8,128)(2,1)S(1)}, bf16[2,3,16,512]{3,2,1,0:T(8,128)(2,1)S(1)}, u32[]{:S(2)}, u32[]{:S(2)}) collective-permute-start(bf16[2,3,16,512]{3,2,1,0:T(8,128)(2,1)S(1)} %get-tuple-element.60), channel_id=1, source_target_pairs={{0,64},{64,0},{128,192},{192,128},{1,65},{65,1},{129,193},{193,129... | collective-permute-start | bytes 294920 | tf_op jit(solution)/shard_map/ppermute | solution.py:400
  31.2 5.8 %collective-permute-start.4 = (bf16[2,3,16,512]{3,2,1,0:T(8,128)(2,1)S(1)}, bf16[2,3,16,512]{3,2,1,0:T(8,128)(2,1)S(1)}, u32[]{:S(2)}, u32[]{:S(2)}) collective-permute-start(bf16[2,3,16,512]{3,2,1,0:T(8,128)(2,1)S(1)} %get-tuple-element.61), channel_id=1, source_target_pairs={{0,192},{64,128},{128,64},{192,0},{1,193},{65,129},{129,65},{193,1... | collective-permute-start | bytes 294920 | tf_op jit(solution)/shard_map/ppermute | solution.py:400
  37.1 5.4 %collective-permute-start.5 = (bf16[1,3,16,512]{3,2,1,0:T(8,128)(2,1)S(1)}, bf16[1,3,16,512]{3,2,1,0:T(8,128)(2,1)S(1)}, u32[]{:S(2)}, u32[]{:S(2)}) collective-permute-start(bf16[1,3,16,512]{3,2,1,0:T(8,128)(2,1)S(1)} %get-tuple-element.74), channel_id=1, source_target_pairs={{0,192},{64,128},{128,64},{192,0},{1,193},{65,129},{129,65},{193,1... | collective-permute-start | bytes 147464 | tf_op jit(solution)/shard_map/ppermute | solution.py:400
  39.3 4.1 %collective-permute-start.6 = (bf16[1,3,16,512]{3,2,1,0:T(8,128)(2,1)S(1)}, bf16[1,3,16,512]{3,2,1,0:T(8,128)(2,1)S(1)}, u32[]{:S(2)}, u32[]{:S(2)}) collective-permute-start(bf16[1,3,16,512]{3,2,1,0:T(8,128)(2,1)S(1)} %get-tuple-element.76), channel_id=1, source_target_pairs={{0,32},{32,0},{1,33},{33,1},{2,34},{34,2},{3,35},{35,3},{4,36},{36... | collective-permute-start | bytes 147464 | tf_op jit(solution)/shard_map/ppermute | solution.py:400
  43.6 5.9 %collective-permute-start.7 = (bf16[1,3,16,512]{3,2,1,0:T(8,128)(2,1)S(1)}, bf16[1,3,16,512]{3,2,1,0:T(8,128)(2,1)S(1)}, u32[]{:S(2)}, u32[]{:S(2)}) collective-permute-start(bf16[1,3,16,512]{3,2,1,0:T(8,128)(2,1)S(1)} %get-tuple-element.77.a_ref), channel_id=1, source_target_pairs={{0,192},{64,128},{128,64},{192,0},{1,193},{65,129},{129,65},{193,1... | collective-permute-start | bytes 147464 | tf_op jit(solution)/shard_map/ppermute | solution.py:400
  44.9 4.6 %collective-permute-start.8 = (bf16[1,3,16,512]{3,2,1,0:T(8,128)(2,1)S(1)}, bf16[1,3,16,512]{3,2,1,0:T(8,128)(2,1)S(1)}, u32[]{:S(2)}, u32[]{:S(2)}) collective-permute-start(bf16[1,3,16,512]{3,2,1,0:T(8,128)(2,1)S(1)} %get-tuple-element.78.b_ref), channel_id=1, source_target_pairs={{0,32},{32,0},{1,33},{33,1},{2,34},{34,2},{3,35},{35,3},{4,36},{36... | collective-permute-start | bytes 147464 | tf_op jit(solution)/shard_map/ppermute | solution.py:400
  49.5 5.2 %collective-permute-start.9 = (bf16[2,3,16,512]{3,2,1,0:T(8,128)(2,1)S(1)}, bf16[2,3,16,512]{3,2,1,0:T(8,128)(2,1)S(1)}, u32[]{:S(2)}, u32[]{:S(2)}) collective-permute-start(bf16[2,3,16,512]{3,2,1,0:T(8,128)(2,1)S(1)} %get-tuple-element.79.a_ref), channel_id=1, source_target_pairs={{0,64},{64,0},{128,192},{192,128},{1,65},{65,1},{129,193},{193,129... | collective-permute-start | bytes 294920 | tf_op jit(solution)/shard_map/ppermute | solution.py:400
  49.6 5.9 %collective-permute-start.10 = (bf16[2,3,16,512]{3,2,1,0:T(8,128)(2,1)S(1)}, bf16[2,3,16,512]{3,2,1,0:T(8,128)(2,1)S(1)}, u32[]{:S(2)}, u32[]{:S(2)}) collective-permute-start(bf16[2,3,16,512]{3,2,1,0:T(8,128)(2,1)S(1)} %get-tuple-element.80.b_ref), channel_id=1, source_target_pairs={{0,192},{64,128},{128,64},{192,0},{1,193},{65,129},{129,65},{193,1... | collective-permute-start | bytes 294920 | tf_op jit(solution)/shard_map/ppermute | solution.py:400
  55.6 5.9 %collective-permute-start.11 = (bf16[4,3,16,512]{3,2,1,0:T(8,128)(2,1)S(1)}, bf16[4,3,16,512]{3,2,1,0:T(8,128)(2,1)S(1)}, u32[]{:S(2)}, u32[]{:S(2)}) collective-permute-start(bf16[4,3,16,512]{3,2,1,0:T(8,128)(2,1)S(1)} %get-tuple-element.88.a_ref), channel_id=1, source_target_pairs={{0,32},{32,0},{1,33},{33,1},{2,34},{34,2},{3,35},{35,3},{4,36},{36... | collective-permute-start | bytes 589832 | tf_op jit(solution)/shard_map/ppermute | solution.py:400
  57.4 5.7 %collective-permute-start.12 = (bf16[4,3,16,512]{3,2,1,0:T(8,128)(2,1)S(1)}, bf16[4,3,16,512]{3,2,1,0:T(8,128)(2,1)S(1)}, u32[]{:S(2)}, u32[]{:S(2)}) collective-permute-start(bf16[4,3,16,512]{3,2,1,0:T(8,128)(2,1)S(1)} %get-tuple-element.90.b_ref), channel_id=1, source_target_pairs={{0,64},{64,0},{128,192},{192,128},{1,65},{65,1},{129,193},{193,129... | collective-permute-start | bytes 589832 | tf_op jit(solution)/shard_map/ppermute | solution.py:400
  63.1 2.4 %collective-permute-start.14 = (bf16[2,8,3,16,512]{4,3,2,1,0:T(8,128)(2,1)S(1)}, bf16[2,8,3,16,512]{4,3,2,1,0:T(8,128)(2,1)S(1)}, u32[]{:S(2)}, u32[]{:S(2)}) collective-permute-start(bf16[2,8,3,16,512]{4,3,2,1,0:T(8,128)(2,1)S(1)} %join4.1.mine_ref), channel_id=1, source_target_pairs={{0,16},{16,0},{1,17},{17,1},{2,18},{18,2},{3,19},{19,3},{4,20},{20... | collective-permute-start | bytes 2359304 | tf_op jit(solution)/shard_map/ppermute | solution.py:400
  68.7 16.6 %copy-start.10 = (f32[1,512]{1,0:T(1,128)S(1)}, f32[1,512]{1,0:T(1,128)}, u32[]{:S(2)}) copy-start(f32[1,512]{1,0:T(1,128)} %gain_ref.1) | copy-start | bytes 6148
  68.7 3.7 %collective-permute-start.15 = (f32[8,128]{1,0:T(8,128)S(1)}, f32[8,128]{1,0:T(8,128)S(1)}, u32[]{:S(2)}, u32[]{:S(2)}) collective-permute-start(f32[8,128]{1,0:T(8,128)S(1)} %get-tuple-element.93), channel_id=1, source_target_pairs={{0,1},{1,0},{2,3},{3,2},{4,5},{5,4},{6,7},{7,6},{8,9},{9,8},{10,11... | collective-permute-start | bytes 12296 | tf_op jit(solution)/shard_map/ppermute | solution.py:400
  72.4 7.4 %collective-permute-start.16 = (f32[8,128]{1,0:T(8,128)S(1)}, f32[8,128]{1,0:T(8,128)S(1)}, u32[]{:S(2)}, u32[]{:S(2)}) collective-permute-start(f32[8,128]{1,0:T(8,128)S(1)} %add.61), channel_id=1, source_target_pairs={{0,7},{1,2},{2,1},{3,4},{4,3},{5,6},{6,5},{7,0},{8,15},{9,10},{10,... | collective-permute-start | bytes 12296 | tf_op jit(solution)/shard_map/ppermute | solution.py:463
  79.9 5.4 %collective-permute-start.17 = (f32[8,128]{1,0:T(8,128)S(1)}, f32[8,128]{1,0:T(8,128)S(1)}, u32[]{:S(2)}, u32[]{:S(2)}) collective-permute-start(f32[8,128]{1,0:T(8,128)S(1)} %add.62.a_ref), channel_id=1, source_target_pairs={{3,0},{6,1},{5,2},{0,3},{7,4},{2,5},{1,6},{4,7},{11,8},{14,9},{13,... | collective-permute-start | bytes 12296 | tf_op jit(solution)/shard_map/ppermute | solution.py:464

commit v3 on v2

v3 whole, which is shorter than its diff:
```python
import functools
import math

import jax
import jax.numpy as jnp
from jax import lax
from jax.experimental import pallas as pl
from jax.experimental.pallas import tpu as pltpu
from jax.sharding import Mesh, PartitionSpec as P

WINDOW = 512
TILE = 256
BLOCK = 32
MIB = 1024 * 1024
BF16 = jnp.bfloat16
F32 = jnp.float32
NEG = -1e30

Y, X, CORE, SEQ, HEAD = "y", "x", "core", "seq", "head"


def nt(a, b):
    return lax.dot_general(a, b, (((1,), (1,)), ((), ())), preferred_element_type=F32)


def nn(a, b):
    return lax.dot_general(a, b, (((1,), (0,)), ((), ())), preferred_element_type=F32)


def tn(a, b):
    return lax.dot_general(a, b, (((0,), (0,)), ((), ())), preferred_element_type=F32)


def whole():
    return pl.BlockSpec(memory_space=pltpu.VMEM)


def params(limit, **kw):
    return pltpu.CompilerParams(vmem_limit_bytes=limit * MIB, **kw)


def cost(flops, read, trans=0):
    return pl.CostEstimate(flops=int(flops), bytes_accessed=int(read), transcendentals=int(trans))


def column_of(row):
    return jnp.transpose(jnp.broadcast_to(row, (128, 128)))


def grad_kernel(inv, me_ref, k_ref, v_ref, r_ref, w_ref, keep_ref, send_ref, kk, uu, dd, acc):
    step = pl.program_id(0)
    last = pl.num_programs(0) - 1
    here = pl.ds(pl.multiple_of(step * TILE, TILE), TILE)
    keys = k_ref[0]
    kk[here, :] = keys
    tiles = TILE // 128
    parts = []
    for t in range(tiles):
        rate = column_of(r_ref[0:1, t * 128 : (t + 1) * 128])
        rows = v_ref[0, t * 128 : (t + 1) * 128, :].astype(F32)
        wide = jnp.concatenate([rate] * (rows.shape[1] // 128), axis=1)
        parts.append((wide * rows * inv).astype(BF16))
    u = jnp.concatenate(parts, axis=0)
    uu[here, :] = u
    h1 = nn(keys, w_ref[0, 0])
    h3 = nn(keys, w_ref[0, 1])
    dg = nn(u, w_ref[0, 2])
    sig = 0.5 + 0.5 * jnp.tanh(0.5 * h1)
    act = h1 * sig
    dd[0, here, :] = (dg * h3 * (sig + act * (1.0 - sig))).astype(BF16)
    dd[1, here, :] = (dg * act).astype(BF16)
    dd[2, here, :] = (act * h3).astype(BF16)

    @pl.when(step == last)
    def _():
        acc[0] = tn(dd[0], kk[...]).astype(BF16)
        acc[1] = tn(dd[1], kk[...]).astype(BF16)
        acc[2] = tn(dd[2], uu[...]).astype(BF16)
        chips = keep_ref.shape[0]
        core = me_ref[0] // chips
        for d in range(chips):
            for o, ref in ((core, keep_ref), (1 - core, send_ref)):
                at = pl.multiple_of((o * chips + d) * BLOCK, BLOCK)
                ref[d] = acc[:, pl.ds(at, BLOCK), :]


def gradients(me, keys, values, rates, weights, inv):
    rows, dim = keys.shape[1:]
    hidden = weights.shape[3]
    out = jax.ShapeDtypeStruct((hidden // BLOCK // 2, 3, BLOCK, dim), BF16)
    tile = pl.BlockSpec((1, TILE, dim), lambda i, s: (0, i, 0))
    return pl.pallas_call(
        functools.partial(grad_kernel, inv),
        grid_spec=pltpu.PrefetchScalarGridSpec(
            num_scalar_prefetch=1,
            grid=(rows // TILE,),
            in_specs=[
                tile,
                tile,
                pl.BlockSpec((1, TILE), lambda i, s: (0, i)),
                pl.BlockSpec(weights.shape, lambda i, s: (0, 0, 0, 0)),
            ],
            out_specs=[whole()] * 2,
            scratch_shapes=[
                pltpu.VMEM((rows, dim), BF16),
                pltpu.VMEM((rows, dim), BF16),
                pltpu.VMEM((3, rows, hidden), BF16),
                pltpu.VMEM((3, hidden, dim), BF16),
            ],
        ),
        out_shape=[out, out],
        compiler_params=params(24),
        cost_estimate=cost(1000, MIB),
        name="grad",
    )(me, keys, values, rates, weights)


def rim_kernel(k_ref, v_ref, rim_ref):
    rim_ref[0] = k_ref[0]
    rim_ref[1] = v_ref[0]


def rim_of(keys, values):
    rows, dim = keys.shape[1:]
    end = pl.BlockSpec((1, WINDOW, dim), lambda i: (0, rows // WINDOW - 1, 0))
    return pl.pallas_call(
        rim_kernel,
        grid=(1,),
        in_specs=[end, end],
        out_specs=whole(),
        out_shape=jax.ShapeDtypeStruct((2, WINDOW, dim), BF16),
        compiler_params=params(6),
        cost_estimate=cost(1, 3 * MIB),
        name="rim",
    )(keys, values)


def attend(q, ks, vs, first, low, scale):
    tile = q.shape[0]
    col = lax.broadcasted_iota(jnp.int32, (tile, tile), 1)
    row = lax.broadcasted_iota(jnp.int32, (tile, tile), 0)
    scores = []
    for b in range(3):
        s = nt(q, ks[b])
        ok = col >= low - (first + b * tile)
        if b == 2:
            ok = ok & (col <= row)
        scores.append(jnp.where(ok, s, NEG))
    top = jnp.max(jnp.maximum(jnp.maximum(scores[0], scores[1]), scores[2]), axis=1, keepdims=True)
    total, out = None, None
    for b in range(3):
        p = jnp.exp2((scores[b] - top) * scale)
        total = p if total is None else total + p
        o = nn(p.astype(BF16), vs[b])
        out = o if out is None else out + o
    return out / jnp.sum(total, axis=1, keepdims=True)


def lowest(meta_ref, first, tile):
    pos = first + 2 * tile + lax.broadcasted_iota(jnp.int32, (tile, 1), 0)
    low = jnp.zeros_like(pos)
    for b in range(1, 4):
        low = jnp.where(pos >= meta_ref[b], meta_ref[b], low)
    return jnp.maximum(low, pos - (WINDOW - 1))


def bounds_kernel(place_ref, docs_ref, meta_ref):
    docs = docs_ref[...]
    own = lax.broadcasted_iota(jnp.int32, docs.shape, 0) == place_ref[1]
    meta_ref[0] = place_ref[2]
    for b in range(1, 4):
        meta_ref[b] = jnp.sum(jnp.where(own & (docs < b), 1.0, 0.0)).astype(jnp.int32)


def bounds(place, docs):
    return pl.pallas_call(
        bounds_kernel,
        grid=(1,),
        in_specs=[pl.BlockSpec(memory_space=pltpu.SMEM), pl.BlockSpec(docs.shape, lambda i: (0, 0))],
        out_specs=pl.BlockSpec(memory_space=pltpu.SMEM),
        out_shape=jax.ShapeDtypeStruct((4,), jnp.int32),
        compiler_params=params(4),
        cost_estimate=cost(6 * docs.size, 4 * docs.size),
        name="bounds",
    )(place, docs)


def attn_kernel(scale, part, meta_ref, *refs):
    if part == 0:
        q_ref, rim_ref, k_ref, v_ref, o_ref = refs
    else:
        q_ref, k_ref, v_ref, o_ref = refs
    for t in range(WINDOW // TILE):
        first = meta_ref[0] + part * WINDOW + (t - 2) * TILE
        ks, vs = [], []
        for b in range(3):
            at = part * WINDOW + (t + b - 2) * TILE
            if at < 0:
                at += WINDOW
                ks.append(rim_ref[0, at : at + TILE, :])
                vs.append(rim_ref[1, at : at + TILE, :])
            else:
                ks.append(k_ref[0, at : at + TILE, :])
                vs.append(v_ref[0, at : at + TILE, :])
        q = q_ref[0, t * TILE : (t + 1) * TILE, :]
        o_ref[t * TILE : (t + 1) * TILE, :] = attend(
            q, ks, vs, first, lowest(meta_ref, first, TILE), scale
        )


def attention(part, meta, queries, rims, keys, values):
    dim = queries.shape[2]
    rows = keys.shape[1] if part else WINDOW
    smem = pl.BlockSpec(memory_space=pltpu.SMEM)
    own = pl.BlockSpec((1, rows, dim), lambda i: (0, 0, 0))
    rim = pl.BlockSpec((2, WINDOW, dim), lambda i: (0, 0, 0))
    return pl.pallas_call(
        functools.partial(attn_kernel, math.log2(math.e) / math.sqrt(dim), part),
        grid=(1,),
        in_specs=[smem, pl.BlockSpec((1, WINDOW, dim), lambda i: (0, part, 0))]
        + [rim] * len(rims)
        + [own, own],
        out_specs=pl.BlockSpec((WINDOW, dim), lambda i: (0, 0)),
        out_shape=jax.ShapeDtypeStruct((WINDOW, dim), F32),
        compiler_params=params(14),
        cost_estimate=cost(4 * WINDOW * 3 * TILE * dim, 4 * MIB, 3 * WINDOW * TILE),
        name="attn" + "ab"[part],
    )(meta, queries, *rims, keys, values)


def prep_kernel(me_ref, w_ref, m_ref, base_ref, rms_ref, wt, mt):
    at = pl.multiple_of(me_ref[0] % (128 // BLOCK) * BLOCK, BLOCK)
    for m in range(3):
        wt[...] = jnp.transpose(w_ref[0, m].astype(F32))
        mt[...] = jnp.transpose(m_ref[0, m])
        w = wt[pl.ds(at, BLOCK), :]
        base_ref[m] = w - 0.9 * mt[pl.ds(at, BLOCK), :]
        rms = jnp.sqrt(jnp.mean(w * w, axis=1, keepdims=True) + 1e-06)
        rms_ref[m] = jnp.broadcast_to(rms, (BLOCK, 128))


def prepare(me, weights, momentum):
    dim = weights.shape[2]
    pick = pl.BlockSpec((1, 3, dim, 128), lambda i, s: (0, 0, 0, s[0] // (128 // BLOCK)))
    shapes = [(3, BLOCK, dim), (3, BLOCK, 128)]
    return pl.pallas_call(
        prep_kernel,
        grid_spec=pltpu.PrefetchScalarGridSpec(
            num_scalar_prefetch=1,
            grid=(1,),
            in_specs=[pick] * 2,
            out_specs=[whole()] * 2,
            scratch_shapes=[pltpu.VMEM((128, dim), F32)] * 2,
        ),
        out_shape=[jax.ShapeDtypeStruct(shape, F32) for shape in shapes],
        compiler_params=params(8),
        cost_estimate=cost(3 * MIB, 3 * MIB),
        name="prep",
    )(me, weights, momentum)


def renew_kernel(base_ref, rms_ref, pieces_ref, out_ref):
    cand = base_ref[...]
    for d in range(pieces_ref.shape[0]):
        cand = cand + pieces_ref[d].astype(F32)
    new = lax.rsqrt(jnp.mean(cand * cand, axis=2, keepdims=True) + 1e-06)
    rows = (cand * (rms_ref[...][:, :, :1] * new)).astype(BF16)
    for d in range(out_ref.shape[0]):
        out_ref[d] = rows


def renew(base, rms, pieces):
    return pl.pallas_call(
        renew_kernel,
        in_specs=[whole()] * 3,
        out_specs=whole(),
        out_shape=jax.ShapeDtypeStruct(pieces.shape, BF16),
        compiler_params=params(8),
        cost_estimate=cost(MIB, MIB),
        name="renew",
    )(base, rms, pieces)


def fill(new, mine_ref, other_ref):
    chips, _, block, dim = mine_ref.shape
    size = chips * block
    for m in range(3):
        new[m, :size, :] = mine_ref[:, m].reshape(size, dim)
        new[m, size:, :] = other_ref[:, m].reshape(size, dim)


def out_kernel(q_ref, lo_ref, hi_ref, mine_ref, other_ref, y_ref, ss_ref, new):
    step = pl.program_id(0)

    @pl.when(step == 0)
    def _():
        fill(new, mine_ref, other_ref)

    q = q_ref[0]
    one = nt(q, new[0])
    three = nt(q, new[1])
    gq = (one * (0.5 + 0.5 * jnp.tanh(0.5 * one)) * three).astype(BF16)
    attn = jnp.where(step < pl.num_programs(0) // 2, lo_ref[...], hi_ref[...])
    y = attn + nn(gq, new[2])
    y_ref[...] = y
    sq = y * y
    lanes = sq[:, :128]
    for c in range(1, sq.shape[1] // 128):
        lanes = lanes + sq[:, c * 128 : (c + 1) * 128]
    tiles = TILE // 128
    for t in range(tiles):
        turned = jnp.transpose(lanes[t * 128 : (t + 1) * 128, :])
        row = jnp.sum(turned, axis=0, keepdims=True)
        for h in range(ss_ref.shape[0]):
            ss_ref[h, pl.ds(step * tiles + t, 1), :] = row


def outputs(queries, lo, hi, mine, other, copies):
    rows, dim = queries.shape[1:]
    hidden = 2 * mine.shape[0] * BLOCK
    mid = rows // TILE // 2
    tile = pl.BlockSpec((TILE, dim), lambda i: (i, 0))
    low = pl.BlockSpec((TILE, dim), lambda i: (jnp.minimum(i, mid - 1), 0))
    high = pl.BlockSpec((TILE, dim), lambda i: (jnp.maximum(i - mid, 0), 0))
    return pl.pallas_call(
        out_kernel,
        grid=(rows // TILE,),
        in_specs=[pl.BlockSpec((1, TILE, dim), lambda i: (0, i, 0)), low, high, whole(), whole()],
        out_specs=[tile, whole()],
        out_shape=[
            jax.ShapeDtypeStruct((rows, dim), F32),
            jax.ShapeDtypeStruct((copies, rows // 128, 128), F32),
        ],
        scratch_shapes=[pltpu.VMEM((3, hidden, dim), BF16)],
        compiler_params=params(14),
        cost_estimate=cost(6 * rows * dim * hidden, 6 * MIB, rows * hidden),
        name="out",
    )(queries, lo, hi, mine, other)


def final_kernel(count, me_ref, y_ref, sums_ref, gain_ref, mine_ref, other_ref, out_ref, new_ref, rows):
    step = pl.program_id(0)
    chips = mine_ref.shape[0]
    own = me_ref[0] // chips == step // 2
    for m in range(3):
        for b in range(chips // 2):
            at = step % 2 * (chips // 2) + b
            rows[m, b * BLOCK : (b + 1) * BLOCK, :] = jnp.where(
                own, mine_ref[at, m], other_ref[at, m]
            )
        new_ref[0, m] = jnp.transpose(rows[m])
    tiles = y_ref.shape[0] // 128
    dim = y_ref.shape[1]
    gain = gain_ref[...]
    for t in range(tiles):
        at = pl.ds(step * tiles + t, 1)
        total = sums_ref[0, at, :]
        for h in range(1, sums_ref.shape[0]):
            total = total + sums_ref[h, at, :]
        scale = column_of(lax.rsqrt(total * (1.0 / count) + 1e-06))
        wide = jnp.concatenate([scale] * (dim // 128), axis=1)
        part = slice(t * 128, (t + 1) * 128)
        out_ref[0, part, :] = (y_ref[part, :] * wide * gain).astype(BF16)


def final(me, y, sums, gain, mine, other, count):
    rows, dim = y.shape
    hidden = 2 * mine.shape[0] * BLOCK
    steps = 4
    full = lambda shape: pl.BlockSpec(shape, lambda i: (0,) * len(shape))
    return pl.pallas_call(
        functools.partial(final_kernel, count),
        grid=(steps,),
        in_specs=[
            pl.BlockSpec(memory_space=pltpu.SMEM),
            pl.BlockSpec((rows // steps, dim), lambda i: (i, 0)),
            full(sums.shape),
            full((1, dim)),
            whole(),
            whole(),
        ],
        out_specs=[
            pl.BlockSpec((1, rows // steps, dim), lambda i: (0, i, 0)),
            pl.BlockSpec((1, 3, dim, hidden // steps), lambda i: (0, 0, 0, i)),
        ],
        out_shape=[
            jax.ShapeDtypeStruct((1, rows, dim), BF16),
            jax.ShapeDtypeStruct((1, 3, dim, hidden), BF16),
        ],
        scratch_shapes=[pltpu.VMEM((3, hidden // steps, dim), BF16)],
        compiler_params=params(16),
        cost_estimate=cost(MIB, 6 * MIB),
        name="final",
    )(me, y, sums, gain, mine, other)


def swap(x, axis, by):
    return lax.ppermute(x, axis, [(i, i ^ by) for i in range(lax.axis_size(axis))])


def added_kernel(a_ref, b_ref, out_ref):
    out_ref[...] = (a_ref[...].astype(F32) + b_ref[...].astype(F32)).astype(BF16)


def added(a, b):
    return pl.pallas_call(
        added_kernel,
        in_specs=[whole()] * 2,
        out_specs=whole(),
        out_shape=jax.ShapeDtypeStruct(a.shape, BF16),
        compiler_params=params(8),
        cost_estimate=cost(MIB, MIB),
        name="added",
    )(a, b)


def per_device(queries, keys, values, rates, doc_ids, fast_weights, momentum, head_gain):
    rows, dim = queries.shape[1:]
    y, x, core = lax.axis_index(Y), lax.axis_index(X), lax.axis_index(CORE)
    ctx = (Y, X, CORE)
    n = lax.axis_size(Y) * lax.axis_size(X) * lax.axis_size(CORE)
    chip = y * lax.axis_size(X) + x
    me = core * (n // 2) + chip
    offset = lax.axis_index(ctx) * rows
    me = jnp.stack([me, lax.axis_index(SEQ), offset]).astype(jnp.int32)
    inv = 1.0 / math.sqrt(rows * n)
    hbm = lambda array: pltpu.with_memory_space_constraint(array, pltpu.HBM)

    rim = rim_of(hbm(keys), hbm(values))
    rim, me = lax.optimization_barrier((rim, me))
    rim = lax.ppermute(rim, ctx, [(i, (i + 1) % n) for i in range(n)])
    keep, send = gradients(me, hbm(keys), hbm(values), rates, hbm(fast_weights), inv)
    got = swap(send, CORE, 1)
    keep, me = lax.optimization_barrier((keep, me))
    base, rms = prepare(me, fast_weights, momentum)
    meta = bounds(me, doc_ids)
    hi = attention(1, meta, queries, (), keys, values)
    got, base, rms, rim, hi, meta = lax.optimization_barrier((got, base, rms, rim, hi, meta))
    pieces = lax.all_to_all(added(keep, got), (Y, X), 0, 0)

    mine = lax.all_to_all(renew(base, rms, pieces), (Y, X), 0, 0)
    other = swap(mine, CORE, 1)
    mine, rim, meta = lax.optimization_barrier((mine, rim, meta))
    lo = attention(0, meta, queries, (rim,), keys, values)
    other, lo = lax.optimization_barrier((other, lo))
    heads = lax.axis_size(HEAD)
    mixed, squares = outputs(queries, lo, hi, mine, other, heads)
    sums = lax.all_to_all(squares, HEAD, 0, 0)
    result, fresh = final(me, mixed, sums, head_gain, mine, other, heads * dim)
    return result, fresh


def solution(mesh):
    seqs = 2
    sizes = mesh.shape
    fine = Mesh(
        mesh.devices.reshape(sizes["ctx"] // 4, 2, 2, seqs, sizes["hs"] // seqs),
        (Y, X, CORE, SEQ, HEAD),
    )
    ctx, hs = (Y, X, CORE), (SEQ, HEAD)
    return jax.shard_map(
        per_device,
        mesh=fine,
        in_specs=(
            P(hs, ctx, None),
            P(hs, ctx, None),
            P(hs, ctx, None),
            P(hs, ctx),
            P(),
            P(hs, None, None, None),
            P(hs, None, None, None),
            P(hs, None),
        ),
        out_specs=(P(hs, ctx, None), P(hs, None, None, None)),
        check_vma=False,
    )
```

time: 87.4 us -> 74.9 us (0.86)
  blocking collectives: 0 us -> 48.1 us
  starting transfers between devices: 28.3 us -> 2.03 us
  waiting for transfers between devices: 25.6 us -> 0.03 us
  Pallas kernels: 28.1 us -> 22.5 us
  local copies, waits for them, and re-layouts: 3.73 us -> 0.7 us
    all_to_all x0 -> x3, blocking collectives: none -> 48.1 us  [the longest x1 17.3 us: per_device(): pieces = lax.all_to_all(added(keep, got), (Y, X), 0, 0)]
    ppermute x15 -> x2, waiting for transfers between devices: 22.8 us -> 0.03 us  [swap(): lax.ppermute(x, axis, [(i, i ^ by) for i in range(lax.axis_size(axis))])]
    ppermute x15 -> x2, starting transfers between devices: 20.5 us -> 2.01 us  [swap(): lax.ppermute(x, axis, [(i, i ^ by) for i in range(lax.axis_size(axis))])]
    ppermute x2 -> x0, starting transfers between devices: 7.86 us -> none  [the longest x1 5.86 us: ring_sum(): lax.ppermute(s, HEAD, [(i, (i + 1) % n if i % 2 else (i - 1) % n) for i i...]
    unnamed x24 -> x16, local copies, waits for them, and re-layouts: 3.67 us -> 0.7 us
    ppermute x2 -> x0, waiting for transfers between devices: 2.79 us -> none  [the longest x1 1.58 us: ring_sum(): lax.ppermute(s, HEAD, [(i, (i + 1) % n if i % 2 else (i - 1) % n) for i i...]
    pallas_call x9 -> x4, Pallas kernels: 7.38 us -> 4.89 us  [the longest x1 2.8 us: final(): pl.pallas_call(functools.partial(final_kernel, count), grid=(steps,), in_...]
    pallas_call x1, Pallas kernels: 8.16 us -> 7.26 us  [gradients(): pl.pallas_call(functools.partial(grad_kernel, inv), grid_spec=pltpu.Prefe...]
  transfers between devices with their start and end apart: 18 -> 3, of which waited for: 14 -> 0; matrix products, arithmetic and copies ran while one was open for 1% -> 0% of each run, Pallas kernels for 24% -> 20%
where the time goes in v3:
time: 74.9 us; the launch traced here: 74.3 us
  blocking collectives  48.1 us (64%)
  Pallas kernels  22.5 us (30%)
  starting transfers between devices  2.03 us (3%)
  between operations  0.82 us (1%)
    all_to_all x1, blocking collectives, per_device(): pieces = lax.all_to_all(added(keep, got), (Y, X), 0, 0)  17.3 us
    all_to_all x1, blocking collectives, per_device(): sums = lax.all_to_all(squares, HEAD, 0, 0)  16.3 us
    all_to_all x1, blocking collectives, per_device(): mine = lax.all_to_all(renew(base, rms, pieces), (Y, X), 0, 0)  14.5 us
    pallas_call x1, Pallas kernels, gradients(): pl.pallas_call(functools.partial(grad_kernel, inv), grid_spec=pltpu.Prefe...  7.26 us
    pallas_call x2, Pallas kernels, attention(): pl.pallas_call(functools.partial(attn_kernel, math.log2(math.e) / math.sq...  4.51 us
    pallas_call x1, Pallas kernels, outputs(): pl.pallas_call(out_kernel, grid=(rows // TILE,), in_specs=[pl.BlockSpec((...  3.22 us
    pallas_call x1, Pallas kernels, final(): pl.pallas_call(functools.partial(final_kernel, count), grid=(steps,), in_...  2.8 us
    ppermute x2, starting transfers between devices, swap(): lax.ppermute(x, axis, [(i, i ^ by) for i in range(lax.axis_size(axis))])  2.01 us
  transfers between devices with their start and end apart: 3, of which 0 were waited for; matrix products, arithmetic and copies ran while one was open for 0% of the time, Pallas kernels for 20%

profile of v3, /device:TPU:6, one launch (start us, length us, event | category | flops | bytes accessed | tf_op | source)
XLA Modules:
  0.0 74.3 jit_solution(13669171952879199776)
XLA Ops:
  0.6 0.0 copy-start.6
  0.7 0.0 copy-start.4
  0.7 1.4 %rim.1 = bf16[2,512,512]{2,1,0:T(8,128)(2,1)S(1)} custom-call(bf16[1,1024,512]{2,1,0:T(8,128)(2,1)} %refs_2_.3, bf16[1,1024,512]{2,1,0:T(8,128)(2,1)} %refs_3_.1), custom_call_target="tpu_custom_call" | custom-call | flops 1 | bytes 3145728 | tf_op jit(solution)/shard_map/rim/pallas_call | solution.py:126
  2.1 0.0 copy-start.5
  2.1 0.0 copy-start.2
  2.1 0.1 pad_add_fusion.me_ref.place_ref
  2.2 0.0 collective-permute-start.1
  2.2 0.0 copy-done.6
  2.2 7.3 %grad.1 = (bf16[8,3,32,512]{3,2,1,0:T(8,128)(2,1)S(1)}, bf16[8,3,32,512]{3,2,1,0:T(8,128)(2,1)S(1)}) custom-call(s32[3]{0:T(128)S(1)} %pad_add_fusion.me_ref.place_ref, bf16[1,1024,512]{2,1,0:T(8,128)(2,1)} %refs_2_.3, bf16[1,1024,512]{2,1,0:T(8,128)(2,1)} %refs_3_.1, f32[1,1024]{1,0:T(1,128)S(1)} %copy-done.6, bf16[1,3,512,512]{3,2,1,0:T(8,128)(2,1)} %w_ref.3), custom_call_target="tpu_custom_call" | custom-call | flops 1000 | bytes 1048576 | tf_op jit(solution)/shard_map/grad/pallas_call | solution.py:92
  9.5 2.0 %collective-permute-start = (bf16[8,3,32,512]{3,2,1,0:T(8,128)(2,1)S(1)}, bf16[8,3,32,512]{3,2,1,0:T(8,128)(2,1)S(1)}, u32[]{:S(2)}, u32[]{:S(2)}) collective-permute-start(bf16[8,3,32,512]{3,2,1,0:T(8,128)(2,1)S(1)} %get-tuple-element.26), channel_id=1, source_target_pairs={{0,16},{16,0},{1,17},{17,1},{2,18},{18,2},{3,19},{19,3},{4,20},{20... | collective-permute-start | bytes 2359304 | tf_op jit(solution)/shard_map/ppermute | solution.py:398
  11.5 0.0 copy-done.5
  11.5 1.6 %bounds.1.meta_ref = s32[4]{0:T(128)S(1)} custom-call(s32[3]{0:T(128)S(1)} %pad_add_fusion.me_ref.place_ref, s32[2,16384]{1,0:T(2,128)S(1)} %copy-done.5), custom_call_target="tpu_custom_call" | custom-call | flops 196608 | bytes 131072 | tf_op jit(solution)/shard_map/bounds/pallas_call | solution.py:176
  13.1 0.0 copy-done.4
  13.1 0.0 copy-done.2
  13.2 0.0 copy-start
  13.2 0.0 copy-start.1
  13.2 0.0 copy-start.3
  13.2 1.2 %prep.1 = (f32[3,32,512]{2,1,0:T(8,128)S(1)}, f32[3,32,128]{2,1,0:T(8,128)S(1)}) custom-call(s32[3]{0:T(128)S(1)} %pad_add_fusion.me_ref.place_ref, bf16[1,3,512,512]{3,2,1,0:T(8,128)(2,1)S(1)} %copy-done.2, f32[1,3,512,512]{3,2,1,0:T(8,128)S(1)} %copy-done.4), custom_call_target="tpu_custom_call" | custom-call | flops 3145728 | bytes 3145728 | tf_op jit(solution)/shard_map/prep/pallas_call | solution.py:246
  14.4 0.0 copy-done
  14.4 0.3 copy-done.1
  14.7 0.3 copy-done.3
  15.0 2.3 %attnb.1.hi_ref = f32[512,512]{1,0:T(8,128)S(1)} custom-call(s32[4]{0:T(128)S(1)} %bounds.1.meta_ref, bf16[1,1024,512]{2,1,0:T(8,128)(2,1)S(1)} %copy-done.3, bf16[1,1024,512]{2,1,0:T(8,128)(2,1)S(1)} %copy-done, bf16[1,1024,512]{2,1,0:T(8,128)(2,1)S(1)} %copy-done.1), custom_call_target="tpu_custom_call" | custom-call | flops 805306368 | bytes 4194304 | tf_op jit(solution)/shard_map/attnb/pallas_call | solution.py:217
  17.3 0.0 collective-permute-done.b_ref
  17.3 0.0 collective-permute-done.1.refs_1_
  17.3 0.2 added.1
  17.5 17.3 %all_to_all.15.pieces_ref = bf16[8,3,32,512]{3,2,1,0:T(8,128)(2,1)S(1)} all-to-all(bf16[8,3,32,512]{3,2,1,0:T(8,128)(2,1)S(1)} %added.1), channel_id=1, replica_groups=mesh['y'=4,'x'=2,'core'=2,'seq'=2,'head'=8] {'y','x'}, dimensions={0} | all-to-all | bytes 1572864 | tf_op jit(solution)/shard_map/all_to_all | solution.py:439
  34.9 0.3 renew.1
  35.2 14.5 %all_to_all.16.mine_ref = bf16[8,3,32,512]{3,2,1,0:T(8,128)(2,1)S(1)} all-to-all(bf16[8,3,32,512]{3,2,1,0:T(8,128)(2,1)S(1)} %renew.1), channel_id=1, replica_groups=mesh['y'=4,'x'=2,'core'=2,'seq'=2,'head'=8] {'y','x'}, dimensions={0} | all-to-all | bytes 1572864 | tf_op jit(solution)/shard_map/all_to_all | solution.py:441
  49.7 0.0 collective-permute-start.2
  49.7 2.2 %attna.1.lo_ref = f32[512,512]{1,0:T(8,128)S(1)} custom-call(s32[4]{0:T(128)S(1)} %bounds.1.meta_ref, bf16[1,1024,512]{2,1,0:T(8,128)(2,1)S(1)} %copy-done.3, bf16[2,512,512]{2,1,0:T(8,128)(2,1)S(1)} %collective-permute-done.1.refs_1_, bf16[1,1024,512]{2,1,0:T(8,128)(2,1)S(1)} %copy-done, bf16[1,1024,512]{2,1,0:T(8,128)(2,1)S(1)} %copy-done.1), custom_call_target="tpu_custom_call" | custom-call | flops 805306368 | bytes 4194304 | tf_op jit(solution)/shard_map/attna/pallas_call | solution.py:217
  51.9 0.0 copy-start.7
  51.9 0.0 collective-permute-done.2.other_ref
  51.9 3.2 %out.1 = (f32[1024,512]{1,0:T(8,128)S(1)}, f32[8,8,128]{2,1,0:T(8,128)S(1)}) custom-call(bf16[1,1024,512]{2,1,0:T(8,128)(2,1)S(1)} %copy-done.3, f32[512,512]{1,0:T(8,128)S(1)} %attna.1.lo_ref, f32[512,512]{1,0:T(8,128)S(1)} %attnb.1.hi_ref, bf16[8,3,32,512]{3,2,1,0:T(8,128)(2,1)S(1)} %all_to_all.16.mine_ref, ...), custom_call_target="tpu_custom_call" | custom-call | flops 1610612736 | bytes 6291456 | tf_op jit(solution)/shard_map/out/pallas_call | solution.py:325
  55.2 16.3 %all_to_all.17.sums_ref = f32[8,8,128]{2,1,0:T(8,128)S(1)} all-to-all(f32[8,8,128]{2,1,0:T(8,128)S(1)} %get-tuple-element.43), channel_id=1, replica_groups=mesh['y'=4,'x'=2,'core'=2,'seq'=2,'head'=8] {'head'}, dimensions={0} | all-to-all | bytes 65536 | tf_op jit(solution)/shard_map/all_to_all | solution.py:448
  71.5 0.0 copy-done.7
  71.5 2.8 %final.1 = (bf16[1,1024,512]{2,1,0:T(8,128)(2,1)}, bf16[1,3,512,512]{3,2,1,0:T(8,128)(2,1)}) custom-call(s32[3]{0:T(128)S(1)} %pad_add_fusion.me_ref.place_ref, f32[1024,512]{1,0:T(8,128)S(1)} %get-tuple-element.42.y_ref, f32[8,8,128]{2,1,0:T(8,128)S(1)} %all_to_all.17.sums_ref, f32[1,512]{1,0:T(1,128)S(1)} %copy-done.7, ...), custom_call_target="tpu_custom_call" | custom-call | flops 1048576 | bytes 6291456 | tf_op jit(solution)/shard_map/final/pallas_call | solution.py:371
Async XLA Ops:
  0.6 1.6 %copy-start.6 = (f32[1,1024]{1,0:T(1,128)S(1)}, f32[1,1024]{1,0:T(1,128)}, u32[]{:S(2)}) copy-start(f32[1,1024]{1,0:T(1,128)} %r_ref.1) | copy-start | bytes 12292
  0.7 12.5 %copy-start.4 = (f32[1,3,512,512]{3,2,1,0:T(8,128)S(1)}, f32[1,3,512,512]{3,2,1,0:T(8,128)}, u32[]{:S(2)}) copy-start(f32[1,3,512,512]{3,2,1,0:T(8,128)} %m_ref.1) | copy-start | bytes 9437188
  2.1 9.4 %copy-start.5 = (s32[2,16384]{1,0:T(2,128)S(1)}, s32[2,16384]{1,0:T(2,128)}, u32[]{:S(2)}) copy-start(s32[2,16384]{1,0:T(2,128)} %docs_ref.1) | copy-start | bytes 393220
  2.1 11.1 %copy-start.2 = (bf16[1,3,512,512]{3,2,1,0:T(8,128)(2,1)S(1)}, bf16[1,3,512,512]{3,2,1,0:T(8,128)(2,1)}, u32[]{:S(2)}) copy-start(bf16[1,3,512,512]{3,2,1,0:T(8,128)(2,1)} %w_ref.3) | copy-start | bytes 4718596
  2.2 15.1 %collective-permute-start.1 = (bf16[2,512,512]{2,1,0:T(8,128)(2,1)S(1)}, bf16[2,512,512]{2,1,0:T(8,128)(2,1)S(1)}, u32[]{:S(2)}, u32[]{:S(2)}) collective-permute-start(bf16[2,512,512]{2,1,0:T(8,128)(2,1)S(1)} %rim.1), channel_id=1, source_target_pairs={{0,16},{16,32},{32,48},{48,64},{64,80},{80,96},{96,112},{112,128},... | collective-permute-start | bytes 3145736 | tf_op jit(solution)/shard_map/ppermute | solution.py:431
  9.5 7.8 %collective-permute-start = (bf16[8,3,32,512]{3,2,1,0:T(8,128)(2,1)S(1)}, bf16[8,3,32,512]{3,2,1,0:T(8,128)(2,1)S(1)}, u32[]{:S(2)}, u32[]{:S(2)}) collective-permute-start(bf16[8,3,32,512]{3,2,1,0:T(8,128)(2,1)S(1)} %get-tuple-element.26), channel_id=1, source_target_pairs={{0,16},{16,0},{1,17},{17,1},{2,18},{18,2},{3,19},{19,3},{4,20},{20... | collective-permute-start | bytes 2359304 | tf_op jit(solution)/shard_map/ppermute | solution.py:398
  13.2 1.2 %copy-start = (bf16[1,1024,512]{2,1,0:T(8,128)(2,1)S(1)}, bf16[1,1024,512]{2,1,0:T(8,128)(2,1)}, u32[]{:S(2)}) copy-start(bf16[1,1024,512]{2,1,0:T(8,128)(2,1)} %refs_2_.3) | copy-start | bytes 3145732
  13.2 1.5 %copy-start.1 = (bf16[1,1024,512]{2,1,0:T(8,128)(2,1)S(1)}, bf16[1,1024,512]{2,1,0:T(8,128)(2,1)}, u32[]{:S(2)}) copy-start(bf16[1,1024,512]{2,1,0:T(8,128)(2,1)} %refs_3_.1) | copy-start | bytes 3145732
  13.2 1.8 %copy-start.3 = (bf16[1,1024,512]{2,1,0:T(8,128)(2,1)S(1)}, bf16[1,1024,512]{2,1,0:T(8,128)(2,1)}, u32[]{:S(2)}) copy-start(bf16[1,1024,512]{2,1,0:T(8,128)(2,1)} %q_ref.1) | copy-start | bytes 3145732
  49.7 2.3 %collective-permute-start.2 = (bf16[8,3,32,512]{3,2,1,0:T(8,128)(2,1)S(1)}, bf16[8,3,32,512]{3,2,1,0:T(8,128)(2,1)S(1)}, u32[]{:S(2)}, u32[]{:S(2)}) collective-permute-start(bf16[8,3,32,512]{3,2,1,0:T(8,128)(2,1)S(1)} %all_to_all.16.mine_ref), channel_id=1, source_target_pairs={{0,16},{16,0},{1,17},{17,1},{2,18},{18,2},{3,19},{19,3},{4,20},{20... | collective-permute-start | bytes 2359304 | tf_op jit(solution)/shard_map/ppermute | solution.py:398
  51.9 19.6 %copy-start.7 = (f32[1,512]{1,0:T(1,128)S(1)}, f32[1,512]{1,0:T(1,128)}, u32[]{:S(2)}) copy-start(f32[1,512]{1,0:T(1,128)} %gain_ref.1) | copy-start | bytes 6148

commit v4 on v3

--- a/solution.py
+++ b/solution.py
@@ -10,6 +10,7 @@
 
 WINDOW = 512
 TILE = 256
+OUT_TILE = 512
 BLOCK = 32
 MIB = 1024 * 1024
 BF16 = jnp.bfloat16
@@ -47,92 +48,75 @@
     return jnp.transpose(jnp.broadcast_to(row, (128, 128)))
 
 
-def grad_kernel(inv, me_ref, k_ref, v_ref, r_ref, w_ref, keep_ref, send_ref, kk, uu, dd, acc):
-    step = pl.program_id(0)
-    last = pl.num_programs(0) - 1
-    here = pl.ds(pl.multiple_of(step * TILE, TILE), TILE)
-    keys = k_ref[0]
-    kk[here, :] = keys
-    tiles = TILE // 128
-    parts = []
-    for t in range(tiles):
-        rate = column_of(r_ref[0:1, t * 128 : (t + 1) * 128])
-        rows = v_ref[0, t * 128 : (t + 1) * 128, :].astype(F32)
-        wide = jnp.concatenate([rate] * (rows.shape[1] // 128), axis=1)
-        parts.append((wide * rows * inv).astype(BF16))
-    u = jnp.concatenate(parts, axis=0)
-    uu[here, :] = u
-    h1 = nn(keys, w_ref[0, 0])
-    h3 = nn(keys, w_ref[0, 1])
-    dg = nn(u, w_ref[0, 2])
-    sig = 0.5 + 0.5 * jnp.tanh(0.5 * h1)
-    act = h1 * sig
-    dd[0, here, :] = (dg * h3 * (sig + act * (1.0 - sig))).astype(BF16)
-    dd[1, here, :] = (dg * act).astype(BF16)
-    dd[2, here, :] = (act * h3).astype(BF16)
-
-    @pl.when(step == last)
-    def _():
-        acc[0] = tn(dd[0], kk[...]).astype(BF16)
-        acc[1] = tn(dd[1], kk[...]).astype(BF16)
-        acc[2] = tn(dd[2], uu[...]).astype(BF16)
-        chips = keep_ref.shape[0]
-        core = me_ref[0] // chips
-        for d in range(chips):
-            for o, ref in ((core, keep_ref), (1 - core, send_ref)):
-                at = pl.multiple_of((o * chips + d) * BLOCK, BLOCK)
-                ref[d] = acc[:, pl.ds(at, BLOCK), :]
-
-
-def gradients(me, keys, values, rates, weights, inv):
-    rows, dim = keys.shape[1:]
-    hidden = weights.shape[3]
-    out = jax.ShapeDtypeStruct((hidden // BLOCK // 2, 3, BLOCK, dim), BF16)
-    tile = pl.BlockSpec((1, TILE, dim), lambda i, s: (0, i, 0))
-    return pl.pallas_call(
-        functools.partial(grad_kernel, inv),
-        grid_spec=pltpu.PrefetchScalarGridSpec(
-            num_scalar_prefetch=1,
-            grid=(rows // TILE,),
-            in_specs=[
-                tile,
-                tile,
-                pl.BlockSpec((1, TILE), lambda i, s: (0, i)),
-                pl.BlockSpec(weights.shape, lambda i, s: (0, 0, 0, 0)),
-            ],
-            out_specs=[whole()] * 2,
-            scratch_shapes=[
-                pltpu.VMEM((rows, dim), BF16),
-                pltpu.VMEM((rows, dim), BF16),
-                pltpu.VMEM((3, rows, hidden), BF16),
-                pltpu.VMEM((3, hidden, dim), BF16),
-            ],
-        ),
-        out_shape=[out, out],
+def load_kernel(part, k_ref, v_ref, out_ref, sems):
+    rows = pl.ds(part * WINDOW, WINDOW)
+    copies = [
+        pltpu.make_async_copy(ref.at[0, rows, :], out_ref.at[j], sems.at[j])
+        for j, ref in enumerate((k_ref, v_ref))
+    ]
+    for copy in copies:
+        copy.start()
+    for copy in copies:
+        copy.wait()
+
+
+def load(part, keys, values):
+    return pl.pallas_call(
+        functools.partial(load_kernel, part),
+        in_specs=[pl.BlockSpec(memory_space=pl.ANY)] * 2,
+        out_specs=whole(),
+        out_shape=jax.ShapeDtypeStruct((2, WINDOW, keys.shape[2]), BF16),
+        scratch_shapes=[pltpu.SemaphoreType.DMA((2,))],
+        compiler_params=params(6),
+        cost_estimate=cost(1, 2 * MIB),
+        name="load" + "ab"[part],
+    )(keys, values)
+
+
+def grad_kernel(own, inv, me_ref, first_ref, last_ref, r_ref, w_ref, out_ref):
+    chips, _, block, dim = out_ref.shape
+    half = chips * block
+    core = me_ref[0] // chips
+    units = pl.ds(pl.multiple_of((core if own else 1 - core) * half, half), half)
+    sums = [None] * 3
+    for c, ref in enumerate((first_ref, last_ref)):
+        keys = ref[0]
+        parts = []
+        for t in range(WINDOW // 128):
+            at = c * WINDOW + t * 128
+            rate = column_of(r_ref[0:1, at : at + 128] * inv)
+            rows = ref[1, t * 128 : (t + 1) * 128, :].astype(F32)
+            wide = jnp.concatenate([rate] * (dim // 128), axis=1)
+            parts.append((wide * rows).astype(BF16))
+        u = jnp.concatenate(parts, axis=0)
+        h1 = nn(keys, w_ref[0, 0, :, units])
+        h3 = nn(keys, w_ref[0, 1, :, units])
+        dg = nn(u, w_ref[0, 2, :, units])
+        sig = 0.5 + 0.5 * jnp.tanh(0.5 * h1)
+        act = h1 * sig
+        parts = (
+            tn((dg * h3 * (sig + act * (1.0 - sig))).astype(BF16), keys),
+            tn((dg * act).astype(BF16), keys),
+            tn((act * h3).astype(BF16), u),
+        )
+        sums = [p if s is None else s + p for s, p in zip(sums, parts)]
+    for m in range(3):
+        out_ref[:, m] = sums[m].reshape(chips, block, dim).astype(BF16)
+
+
+def gradients(own, me, first, last, rates, weights, inv):
+    rows, dim = 2 * WINDOW, first.shape[2]
+    hidden = weights.shape[3] // 2
+    chips = hidden // BLOCK
+    return pl.pallas_call(
+        functools.partial(grad_kernel, own, inv),
+        in_specs=[pl.BlockSpec(memory_space=pltpu.SMEM)] + [whole()] * 4,
+        out_specs=whole(),
+        out_shape=jax.ShapeDtypeStruct((chips, 3, BLOCK, dim), BF16),
         compiler_params=params(24),
         cost_estimate=cost(1000, MIB),
-        name="grad",
-    )(me, keys, values, rates, weights)
-
-
-def rim_kernel(k_ref, v_ref, rim_ref):
-    rim_ref[0] = k_ref[0]
-    rim_ref[1] = v_ref[0]
-
-
-def rim_of(keys, values):
-    rows, dim = keys.shape[1:]
-    end = pl.BlockSpec((1, WINDOW, dim), lambda i: (0, rows // WINDOW - 1, 0))
-    return pl.pallas_call(
-        rim_kernel,
-        grid=(1,),
-        in_specs=[end, end],
-        out_specs=whole(),
-        out_shape=jax.ShapeDtypeStruct((2, WINDOW, dim), BF16),
-        compiler_params=params(6),
-        cost_estimate=cost(1, 3 * MIB),
-        name="rim",
-    )(keys, values)
+        name="grad" + ("own" if own else "other"),
+    )(me, first, last, rates, weights)
 
 
 def attend(q, ks, vs, first, low, scale):
@@ -185,47 +169,33 @@
     )(place, docs)
 
 
-def attn_kernel(scale, part, meta_ref, *refs):
-    if part == 0:
-        q_ref, rim_ref, k_ref, v_ref, o_ref = refs
-    else:
-        q_ref, k_ref, v_ref, o_ref = refs
+def attn_kernel(scale, part, meta_ref, q_ref, before_ref, own_ref, o_ref):
     for t in range(WINDOW // TILE):
         first = meta_ref[0] + part * WINDOW + (t - 2) * TILE
         ks, vs = [], []
         for b in range(3):
-            at = part * WINDOW + (t + b - 2) * TILE
-            if at < 0:
-                at += WINDOW
-                ks.append(rim_ref[0, at : at + TILE, :])
-                vs.append(rim_ref[1, at : at + TILE, :])
-            else:
-                ks.append(k_ref[0, at : at + TILE, :])
-                vs.append(v_ref[0, at : at + TILE, :])
-        q = q_ref[0, t * TILE : (t + 1) * TILE, :]
+            at = (t + b) * TILE
+            ref, at = (before_ref, at) if at < WINDOW else (own_ref, at - WINDOW)
+            ks.append(ref[0, at : at + TILE, :])
+            vs.append(ref[1, at : at + TILE, :])
+        at = part * WINDOW + t * TILE
+        q = q_ref[0, at : at + TILE, :]
         o_ref[t * TILE : (t + 1) * TILE, :] = attend(
             q, ks, vs, first, lowest(meta_ref, first, TILE), scale
         )
 
 
-def attention(part, meta, queries, rims, keys, values):
+def attention(part, meta, queries, before, own):
     dim = queries.shape[2]
-    rows = keys.shape[1] if part else WINDOW
-    smem = pl.BlockSpec(memory_space=pltpu.SMEM)
-    own = pl.BlockSpec((1, rows, dim), lambda i: (0, 0, 0))
-    rim = pl.BlockSpec((2, WINDOW, dim), lambda i: (0, 0, 0))
     return pl.pallas_call(
         functools.partial(attn_kernel, math.log2(math.e) / math.sqrt(dim), part),
-        grid=(1,),
-        in_specs=[smem, pl.BlockSpec((1, WINDOW, dim), lambda i: (0, part, 0))]
-        + [rim] * len(rims)
-        + [own, own],
-        out_specs=pl.BlockSpec((WINDOW, dim), lambda i: (0, 0)),
+        in_specs=[pl.BlockSpec(memory_space=pltpu.SMEM)] + [whole()] * 3,
+        out_specs=whole(),
         out_shape=jax.ShapeDtypeStruct((WINDOW, dim), F32),
         compiler_params=params(14),
         cost_estimate=cost(4 * WINDOW * 3 * TILE * dim, 4 * MIB, 3 * WINDOW * TILE),
         name="attn" + "ab"[part],
-    )(meta, queries, *rims, keys, values)
+    )(meta, queries, before, own)
 
 
 def prep_kernel(me_ref, w_ref, m_ref, base_ref, rms_ref, wt, mt):
@@ -307,7 +277,7 @@
     lanes = sq[:, :128]
     for c in range(1, sq.shape[1] // 128):
         lanes = lanes + sq[:, c * 128 : (c + 1) * 128]
-    tiles = TILE // 128
+    tiles = OUT_TILE // 128
     for t in range(tiles):
         turned = jnp.transpose(lanes[t * 128 : (t + 1) * 128, :])
         row = jnp.sum(turned, axis=0, keepdims=True)
@@ -318,14 +288,14 @@
 def outputs(queries, lo, hi, mine, other, copies):
     rows, dim = queries.shape[1:]
     hidden = 2 * mine.shape[0] * BLOCK
-    mid = rows // TILE // 2
-    tile = pl.BlockSpec((TILE, dim), lambda i: (i, 0))
-    low = pl.BlockSpec((TILE, dim), lambda i: (jnp.minimum(i, mid - 1), 0))
-    high = pl.BlockSpec((TILE, dim), lambda i: (jnp.maximum(i - mid, 0), 0))
+    mid = rows // OUT_TILE // 2
+    tile = pl.BlockSpec((OUT_TILE, dim), lambda i: (i, 0))
+    low = pl.BlockSpec((OUT_TILE, dim), lambda i: (jnp.minimum(i, mid - 1), 0))
+    high = pl.BlockSpec((OUT_TILE, dim), lambda i: (jnp.maximum(i - mid, 0), 0))
     return pl.pallas_call(
         out_kernel,
-        grid=(rows // TILE,),
-        in_specs=[pl.BlockSpec((1, TILE, dim), lambda i: (0, i, 0)), low, high, whole(), whole()],
+        grid=(rows // OUT_TILE,),
+        in_specs=[pl.BlockSpec((1, OUT_TILE, dim), lambda i: (0, i, 0)), low, high, whole(), whole()],
         out_specs=[tile, whole()],
         out_shape=[
             jax.ShapeDtypeStruct((rows, dim), F32),
@@ -426,22 +396,26 @@
     inv = 1.0 / math.sqrt(rows * n)
     hbm = lambda array: pltpu.with_memory_space_constraint(array, pltpu.HBM)
 
-    rim = rim_of(hbm(keys), hbm(values))
-    rim, me = lax.optimization_barrier((rim, me))
-    rim = lax.ppermute(rim, ctx, [(i, (i + 1) % n) for i in range(n)])
-    keep, send = gradients(me, hbm(keys), hbm(values), rates, hbm(fast_weights), inv)
+    last = load(1, hbm(keys), hbm(values))
+    last, me, weights = lax.optimization_barrier((last, me, fast_weights))
+    rim = lax.ppermute(last, ctx, [(i, (i + 1) % n) for i in range(n)])
+    keys, values, me = lax.optimization_barrier((keys, values, me, last))[:3]
+    first = load(0, hbm(keys), hbm(values))
+    send = gradients(False, me, first, last, rates, weights, inv)
     got = swap(send, CORE, 1)
+    me, first = lax.optimization_barrier((me, first, send))[:2]
+    keep = gradients(True, me, first, last, rates, weights, inv)
     keep, me = lax.optimization_barrier((keep, me))
-    base, rms = prepare(me, fast_weights, momentum)
+    base, rms = prepare(me, weights, momentum)
     meta = bounds(me, doc_ids)
-    hi = attention(1, meta, queries, (), keys, values)
+    hi = attention(1, meta, queries, first, last)
     got, base, rms, rim, hi, meta = lax.optimization_barrier((got, base, rms, rim, hi, meta))
     pieces = lax.all_to_all(added(keep, got), (Y, X), 0, 0)
 
     mine = lax.all_to_all(renew(base, rms, pieces), (Y, X), 0, 0)
     other = swap(mine, CORE, 1)
     mine, rim, meta = lax.optimization_barrier((mine, rim, meta))
-    lo = attention(0, meta, queries, (rim,), keys, values)
+    lo = attention(0, meta, queries, rim, first)
     other, lo = lax.optimization_barrier((other, lo))
     heads = lax.axis_size(HEAD)
     mixed, squares = outputs(queries, lo, hi, mine, other, heads)

time: 74.9 us -> 71.8 us (0.959)
  Pallas kernels: 22.5 us -> 20.9 us
  blocking collectives: 48.1 us -> 46.9 us
    pallas_call x3 -> x5, Pallas kernels: 11.9 us -> 10.3 us  [the longest x2 5.37 us: gradients(): pl.pallas_call(functools.partial(grad_kernel, own, inv), in_specs=[pl.Blo...]
    all_to_all x1, blocking collectives: 14.5 us -> 13.6 us  [per_device(): mine = lax.all_to_all(renew(base, rms, pieces), (Y, X), 0, 0)]
  transfers between devices with their start and end apart: 3 -> 3, of which waited for: 0 -> 1; matrix products, arithmetic and copies ran while one was open for 0% -> 0% of each run, Pallas kernels for 20% -> 20%
where the time goes in v4:
time: 71.8 us; the launch traced here: 71.2 us
  blocking collectives  46.9 us (65%)
  Pallas kernels  20.9 us (29%)
  starting transfers between devices  1.69 us (2%)
  between operations  0.8 us (1%)
    all_to_all x1, blocking collectives, per_device(): pieces = lax.all_to_all(added(keep, got), (Y, X), 0, 0)  17 us
    all_to_all x1, blocking collectives, per_device(): sums = lax.all_to_all(squares, HEAD, 0, 0)  16.3 us
    all_to_all x1, blocking collectives, per_device(): mine = lax.all_to_all(renew(base, rms, pieces), (Y, X), 0, 0)  13.6 us
    pallas_call x2, Pallas kernels, gradients(): pl.pallas_call(functools.partial(grad_kernel, own, inv), in_specs=[pl.Blo...  5.37 us
    pallas_call x2, Pallas kernels, attention(): pl.pallas_call(functools.partial(attn_kernel, math.log2(math.e) / math.sq...  4.48 us
    pallas_call x1, Pallas kernels, final(): pl.pallas_call(functools.partial(final_kernel, count), grid=(steps,), in_...  2.84 us
    pallas_call x2, Pallas kernels, load(): pl.pallas_call(functools.partial(load_kernel, part), in_specs=[pl.BlockSp...  2.53 us
    pallas_call x1, Pallas kernels, outputs(): pl.pallas_call(out_kernel, grid=(rows // OUT_TILE,), in_specs=[pl.BlockSp...  2.41 us
  transfers between devices with their start and end apart: 3, of which 1 were waited for; matrix products, arithmetic and copies ran while one was open for 0% of the time, Pallas kernels for 20%

profile of v4, /device:TPU:6, one launch (start us, length us, event | category | flops | bytes accessed | tf_op | source)
XLA Modules:
  0.0 71.2 jit_solution(6090002779329373859)
XLA Ops:
  0.6 1.2 %loadb.1.last_ref.own_ref = bf16[2,512,512]{2,1,0:T(8,128)(2,1)S(1)} custom-call(bf16[1,1024,512]{2,1,0:T(8,128)(2,1)} %k_ref.2, bf16[1,1024,512]{2,1,0:T(8,128)(2,1)} %v_ref.2), custom_call_target="tpu_custom_call" | custom-call | flops 1 | bytes 2097152 | tf_op jit(solution)/shard_map/loadb/pallas_call | solution.py:64
  1.9 0.0 copy-start
  1.9 0.0 copy-start.4
  1.9 0.1 pad_add_fusion.me_ref.place_ref
  2.0 0.0 collective-permute-start.1
  2.0 1.3 %loada.1.first_ref.before_ref.own_ref = bf16[2,512,512]{2,1,0:T(8,128)(2,1)S(1)} custom-call(bf16[1,1024,512]{2,1,0:T(8,128)(2,1)} %k_ref.2, bf16[1,1024,512]{2,1,0:T(8,128)(2,1)} %v_ref.2), custom_call_target="tpu_custom_call" | custom-call | flops 1 | bytes 2097152 | tf_op jit(solution)/shard_map/loada/pallas_call | solution.py:64
  3.3 0.3 copy-done
  3.6 0.0 copy-done.4
  3.6 2.7 %gradother.1 = bf16[8,3,32,512]{3,2,1,0:T(8,128)(2,1)S(1)} custom-call(s32[3]{0:T(128)S(1)} %pad_add_fusion.me_ref.place_ref, bf16[2,512,512]{2,1,0:T(8,128)(2,1)S(1)} %loada.1.first_ref.before_ref.own_ref, bf16[2,512,512]{2,1,0:T(8,128)(2,1)S(1)} %loadb.1.last_ref.own_ref, f32[1,1024]{1,0:T(1,128)S(1)} %copy-done.4, bf16[1,3,512,512]{3,2,1,0:T(8,128)(2,1)S(1)} %copy-done), custom_call_target="tpu_custom_call" | custom-call | flops 1000 | bytes 1048576 | tf_op jit(solution)/shard_map/gradother/pallas_call | solution.py:111
  6.3 0.0 copy-start.3
  6.3 0.0 copy-start.2
  6.3 1.7 %collective-permute-start = (bf16[8,3,32,512]{3,2,1,0:T(8,128)(2,1)S(1)}, bf16[8,3,32,512]{3,2,1,0:T(8,128)(2,1)S(1)}, u32[]{:S(2)}, u32[]{:S(2)}) collective-permute-start(bf16[8,3,32,512]{3,2,1,0:T(8,128)(2,1)S(1)} %gradother.1), channel_id=1, source_target_pairs={{0,16},{16,0},{1,17},{17,1},{2,18},{18,2},{3,19},{19,3},{4,20},{20... | collective-permute-start | bytes 2359304 | tf_op jit(solution)/shard_map/ppermute | solution.py:368
  8.0 2.7 %gradown.1.a_ref = bf16[8,3,32,512]{3,2,1,0:T(8,128)(2,1)S(1)} custom-call(s32[3]{0:T(128)S(1)} %pad_add_fusion.me_ref.place_ref, bf16[2,512,512]{2,1,0:T(8,128)(2,1)S(1)} %loada.1.first_ref.before_ref.own_ref, bf16[2,512,512]{2,1,0:T(8,128)(2,1)S(1)} %loadb.1.last_ref.own_ref, f32[1,1024]{1,0:T(1,128)S(1)} %copy-done.4, bf16[1,3,512,512]{3,2,1,0:T(8,128)(2,1)S(1)} %copy-done), custom_call_target="tpu_custom_call" | custom-call | flops 1000 | bytes 1048576 | tf_op jit(solution)/shard_map/gradown/pallas_call | solution.py:111
  10.7 0.0 copy-done.3
  10.7 1.6 %bounds.1.meta_ref = s32[4]{0:T(128)S(1)} custom-call(s32[3]{0:T(128)S(1)} %pad_add_fusion.me_ref.place_ref, s32[2,16384]{1,0:T(2,128)S(1)} %copy-done.3), custom_call_target="tpu_custom_call" | custom-call | flops 196608 | bytes 131072 | tf_op jit(solution)/shard_map/bounds/pallas_call | solution.py:160
  12.3 0.0 copy-done.2
  12.3 0.0 copy-start.1
  12.3 1.2 %prep.1 = (f32[3,32,512]{2,1,0:T(8,128)S(1)}, f32[3,32,128]{2,1,0:T(8,128)S(1)}) custom-call(s32[3]{0:T(128)S(1)} %pad_add_fusion.me_ref.place_ref, bf16[1,3,512,512]{3,2,1,0:T(8,128)(2,1)S(1)} %copy-done, f32[1,3,512,512]{3,2,1,0:T(8,128)S(1)} %copy-done.2), custom_call_target="tpu_custom_call" | custom-call | flops 3145728 | bytes 3145728 | tf_op jit(solution)/shard_map/prep/pallas_call | solution.py:216
  13.5 0.1 copy-done.1
  13.5 2.2 %attnb.1.hi_ref = f32[512,512]{1,0:T(8,128)S(1)} custom-call(s32[4]{0:T(128)S(1)} %bounds.1.meta_ref, bf16[1,1024,512]{2,1,0:T(8,128)(2,1)S(1)} %copy-done.1, bf16[2,512,512]{2,1,0:T(8,128)(2,1)S(1)} %loada.1.first_ref.before_ref.own_ref, bf16[2,512,512]{2,1,0:T(8,128)(2,1)S(1)} %loadb.1.last_ref.own_ref), custom_call_target="tpu_custom_call" | custom-call | flops 805306368 | bytes 4194304 | tf_op jit(solution)/shard_map/attnb/pallas_call | solution.py:190
  15.8 0.0 collective-permute-done.b_ref
  15.8 0.4 collective-permute-done.1.before_ref
  16.2 0.2 added.1
  16.4 17.0 %all_to_all.15.pieces_ref = bf16[8,3,32,512]{3,2,1,0:T(8,128)(2,1)S(1)} all-to-all(bf16[8,3,32,512]{3,2,1,0:T(8,128)(2,1)S(1)} %added.1), channel_id=1, replica_groups=mesh['y'=4,'x'=2,'core'=2,'seq'=2,'head'=8] {'y','x'}, dimensions={0} | all-to-all | bytes 1572864 | tf_op jit(solution)/shard_map/all_to_all | solution.py:413
  33.4 0.3 renew.1
  33.7 13.6 %all_to_all.16.mine_ref = bf16[8,3,32,512]{3,2,1,0:T(8,128)(2,1)S(1)} all-to-all(bf16[8,3,32,512]{3,2,1,0:T(8,128)(2,1)S(1)} %renew.1), channel_id=1, replica_groups=mesh['y'=4,'x'=2,'core'=2,'seq'=2,'head'=8] {'y','x'}, dimensions={0} | all-to-all | bytes 1572864 | tf_op jit(solution)/shard_map/all_to_all | solution.py:415
  47.3 0.0 collective-permute-start.2
  47.3 2.2 %attna.1.lo_ref = f32[512,512]{1,0:T(8,128)S(1)} custom-call(s32[4]{0:T(128)S(1)} %bounds.1.meta_ref, bf16[1,1024,512]{2,1,0:T(8,128)(2,1)S(1)} %copy-done.1, bf16[2,512,512]{2,1,0:T(8,128)(2,1)S(1)} %collective-permute-done.1.before_ref, bf16[2,512,512]{2,1,0:T(8,128)(2,1)S(1)} %loada.1.first_ref.before_ref.own_ref), custom_call_target="tpu_custom_call" | custom-call | flops 805306368 | bytes 4194304 | tf_op jit(solution)/shard_map/attna/pallas_call | solution.py:190
  49.5 0.0 copy-start.5
  49.6 0.0 collective-permute-done.2.other_ref
  49.6 2.4 %out.1 = (f32[1024,512]{1,0:T(8,128)S(1)}, f32[8,8,128]{2,1,0:T(8,128)S(1)}) custom-call(bf16[1,1024,512]{2,1,0:T(8,128)(2,1)S(1)} %copy-done.1, f32[512,512]{1,0:T(8,128)S(1)} %attna.1.lo_ref, f32[512,512]{1,0:T(8,128)S(1)} %attnb.1.hi_ref, bf16[8,3,32,512]{3,2,1,0:T(8,128)(2,1)S(1)} %all_to_all.16.mine_ref, ...), custom_call_target="tpu_custom_call" | custom-call | flops 1610612736 | bytes 6291456 | tf_op jit(solution)/shard_map/out/pallas_call | solution.py:295
  52.0 16.3 %all_to_all.17.sums_ref = f32[8,8,128]{2,1,0:T(8,128)S(1)} all-to-all(f32[8,8,128]{2,1,0:T(8,128)S(1)} %get-tuple-element.51), channel_id=1, replica_groups=mesh['y'=4,'x'=2,'core'=2,'seq'=2,'head'=8] {'head'}, dimensions={0} | all-to-all | bytes 65536 | tf_op jit(solution)/shard_map/all_to_all | solution.py:422
  68.3 0.0 copy-done.5
  68.3 2.8 %final.1 = (bf16[1,1024,512]{2,1,0:T(8,128)(2,1)}, bf16[1,3,512,512]{3,2,1,0:T(8,128)(2,1)}) custom-call(s32[3]{0:T(128)S(1)} %pad_add_fusion.me_ref.place_ref, f32[1024,512]{1,0:T(8,128)S(1)} %get-tuple-element.50.y_ref, f32[8,8,128]{2,1,0:T(8,128)S(1)} %all_to_all.17.sums_ref, f32[1,512]{1,0:T(1,128)S(1)} %copy-done.5, ...), custom_call_target="tpu_custom_call" | custom-call | flops 1048576 | bytes 6291456 | tf_op jit(solution)/shard_map/final/pallas_call | solution.py:341
Async XLA Ops:
  1.9 1.7 %copy-start = (bf16[1,3,512,512]{3,2,1,0:T(8,128)(2,1)S(1)}, bf16[1,3,512,512]{3,2,1,0:T(8,128)(2,1)}, u32[]{:S(2)}) copy-start(bf16[1,3,512,512]{3,2,1,0:T(8,128)(2,1)} %w_ref.2) | copy-start | bytes 4718596
  1.9 1.7 %copy-start.4 = (f32[1,1024]{1,0:T(1,128)S(1)}, f32[1,1024]{1,0:T(1,128)}, u32[]{:S(2)}) copy-start(f32[1,1024]{1,0:T(1,128)} %r_ref.3) | copy-start | bytes 12292
  2.0 14.2 %collective-permute-start.1 = (bf16[2,512,512]{2,1,0:T(8,128)(2,1)S(1)}, bf16[2,512,512]{2,1,0:T(8,128)(2,1)S(1)}, u32[]{:S(2)}, u32[]{:S(2)}) collective-permute-start(bf16[2,512,512]{2,1,0:T(8,128)(2,1)S(1)} %loadb.1.last_ref.own_ref), channel_id=1, source_target_pairs={{0,16},{16,32},{32,48},{48,64},{64,80},{80,96},{96,112},{112,128},... | collective-permute-start | bytes 3145736 | tf_op jit(solution)/shard_map/ppermute | solution.py:401
  6.3 4.4 %copy-start.3 = (s32[2,16384]{1,0:T(2,128)S(1)}, s32[2,16384]{1,0:T(2,128)}, u32[]{:S(2)}) copy-start(s32[2,16384]{1,0:T(2,128)} %docs_ref.1) | copy-start | bytes 393220
  6.3 6.0 %copy-start.2 = (f32[1,3,512,512]{3,2,1,0:T(8,128)S(1)}, f32[1,3,512,512]{3,2,1,0:T(8,128)}, u32[]{:S(2)}) copy-start(f32[1,3,512,512]{3,2,1,0:T(8,128)} %m_ref.1) | copy-start | bytes 9437188
  6.3 9.5 %collective-permute-start = (bf16[8,3,32,512]{3,2,1,0:T(8,128)(2,1)S(1)}, bf16[8,3,32,512]{3,2,1,0:T(8,128)(2,1)S(1)}, u32[]{:S(2)}, u32[]{:S(2)}) collective-permute-start(bf16[8,3,32,512]{3,2,1,0:T(8,128)(2,1)S(1)} %gradother.1), channel_id=1, source_target_pairs={{0,16},{16,0},{1,17},{17,1},{2,18},{18,2},{3,19},{19,3},{4,20},{20... | collective-permute-start | bytes 2359304 | tf_op jit(solution)/shard_map/ppermute | solution.py:368
  12.3 1.2 %copy-start.1 = (bf16[1,1024,512]{2,1,0:T(8,128)(2,1)S(1)}, bf16[1,1024,512]{2,1,0:T(8,128)(2,1)}, u32[]{:S(2)}) copy-start(bf16[1,1024,512]{2,1,0:T(8,128)(2,1)} %q_ref.5) | copy-start | bytes 3145732
  47.3 2.3 %collective-permute-start.2 = (bf16[8,3,32,512]{3,2,1,0:T(8,128)(2,1)S(1)}, bf16[8,3,32,512]{3,2,1,0:T(8,128)(2,1)S(1)}, u32[]{:S(2)}, u32[]{:S(2)}) collective-permute-start(bf16[8,3,32,512]{3,2,1,0:T(8,128)(2,1)S(1)} %all_to_all.16.mine_ref), channel_id=1, source_target_pairs={{0,16},{16,0},{1,17},{17,1},{2,18},{18,2},{3,19},{19,3},{4,20},{20... | collective-permute-start | bytes 2359304 | tf_op jit(solution)/shard_map/ppermute | solution.py:368
  49.5 18.8 %copy-start.5 = (f32[1,512]{1,0:T(1,128)S(1)}, f32[1,512]{1,0:T(1,128)}, u32[]{:S(2)}) copy-start(f32[1,512]{1,0:T(1,128)} %gain_ref.1) | copy-start | bytes 6148

commit v5 on v4

--- a/solution.py
+++ b/solution.py
@@ -311,12 +311,11 @@
 def final_kernel(count, me_ref, y_ref, sums_ref, gain_ref, mine_ref, other_ref, out_ref, new_ref, rows):
     step = pl.program_id(0)
     chips = mine_ref.shape[0]
-    own = me_ref[0] // chips == step // 2
+    own = me_ref[0] // chips == step
     for m in range(3):
-        for b in range(chips // 2):
-            at = step % 2 * (chips // 2) + b
+        for b in range(chips):
             rows[m, b * BLOCK : (b + 1) * BLOCK, :] = jnp.where(
-                own, mine_ref[at, m], other_ref[at, m]
+                own, mine_ref[b, m], other_ref[b, m]
             )
         new_ref[0, m] = jnp.transpose(rows[m])
     tiles = y_ref.shape[0] // 128
@@ -336,7 +335,7 @@
 def final(me, y, sums, gain, mine, other, count):
     rows, dim = y.shape
     hidden = 2 * mine.shape[0] * BLOCK
-    steps = 4
+    steps = 2
     full = lambda shape: pl.BlockSpec(shape, lambda i: (0,) * len(shape))
     return pl.pallas_call(
         functools.partial(final_kernel, count),

time: 71.8 us -> 71.3 us (level)
  no operation moved by 1% of the time
where the time goes in v5:
time: 71.3 us; the launch traced here: 70.6 us
  blocking collectives  46.9 us (66%)
  Pallas kernels  20.4 us (29%)
  starting transfers between devices  1.69 us (2%)
  between operations  0.8 us (1%)
    all_to_all x1, blocking collectives, per_device(): pieces = lax.all_to_all(added(keep, got), (Y, X), 0, 0)  17 us
    all_to_all x1, blocking collectives, per_device(): sums = lax.all_to_all(squares, HEAD, 0, 0)  16.3 us
    all_to_all x1, blocking collectives, per_device(): mine = lax.all_to_all(renew(base, rms, pieces), (Y, X), 0, 0)  13.6 us
    pallas_call x2, Pallas kernels, gradients(): pl.pallas_call(functools.partial(grad_kernel, own, inv), in_specs=[pl.Blo...  5.37 us
    pallas_call x2, Pallas kernels, attention(): pl.pallas_call(functools.partial(attn_kernel, math.log2(math.e) / math.sq...  4.48 us
    pallas_call x2, Pallas kernels, load(): pl.pallas_call(functools.partial(load_kernel, part), in_specs=[pl.BlockSp...  2.53 us
    pallas_call x1, Pallas kernels, outputs(): pl.pallas_call(out_kernel, grid=(rows // OUT_TILE,), in_specs=[pl.BlockSp...  2.41 us
    pallas_call x1, Pallas kernels, final(): pl.pallas_call(functools.partial(final_kernel, count), grid=(steps,), in_...  2.3 us
  transfers between devices with their start and end apart: 3, of which 1 were waited for; matrix products, arithmetic and copies ran while one was open for 0% of the time, Pallas kernels for 20%

profile of v5, /device:TPU:6, one launch (start us, length us, event | category | flops | bytes accessed | tf_op | source)
XLA Modules:
  0.0 70.6 jit_solution(16426921397624001925)
XLA Ops:
  0.6 1.2 %loadb.1.last_ref.own_ref = bf16[2,512,512]{2,1,0:T(8,128)(2,1)S(1)} custom-call(bf16[1,1024,512]{2,1,0:T(8,128)(2,1)} %k_ref.2, bf16[1,1024,512]{2,1,0:T(8,128)(2,1)} %v_ref.2), custom_call_target="tpu_custom_call" | custom-call | flops 1 | bytes 2097152 | tf_op jit(solution)/shard_map/loadb/pallas_call | solution.py:64
  1.9 0.0 copy-start
  1.9 0.0 copy-start.4
  1.9 0.1 pad_add_fusion.me_ref.place_ref
  2.0 0.0 collective-permute-start.1
  2.0 1.3 %loada.1.first_ref.before_ref.own_ref = bf16[2,512,512]{2,1,0:T(8,128)(2,1)S(1)} custom-call(bf16[1,1024,512]{2,1,0:T(8,128)(2,1)} %k_ref.2, bf16[1,1024,512]{2,1,0:T(8,128)(2,1)} %v_ref.2), custom_call_target="tpu_custom_call" | custom-call | flops 1 | bytes 2097152 | tf_op jit(solution)/shard_map/loada/pallas_call | solution.py:64
  3.3 0.3 copy-done
  3.6 0.0 copy-done.4
  3.6 2.7 %gradother.1 = bf16[8,3,32,512]{3,2,1,0:T(8,128)(2,1)S(1)} custom-call(s32[3]{0:T(128)S(1)} %pad_add_fusion.me_ref.place_ref, bf16[2,512,512]{2,1,0:T(8,128)(2,1)S(1)} %loada.1.first_ref.before_ref.own_ref, bf16[2,512,512]{2,1,0:T(8,128)(2,1)S(1)} %loadb.1.last_ref.own_ref, f32[1,1024]{1,0:T(1,128)S(1)} %copy-done.4, bf16[1,3,512,512]{3,2,1,0:T(8,128)(2,1)S(1)} %copy-done), custom_call_target="tpu_custom_call" | custom-call | flops 1000 | bytes 1048576 | tf_op jit(solution)/shard_map/gradother/pallas_call | solution.py:111
  6.3 0.0 copy-start.3
  6.3 0.0 copy-start.2
  6.3 1.7 %collective-permute-start = (bf16[8,3,32,512]{3,2,1,0:T(8,128)(2,1)S(1)}, bf16[8,3,32,512]{3,2,1,0:T(8,128)(2,1)S(1)}, u32[]{:S(2)}, u32[]{:S(2)}) collective-permute-start(bf16[8,3,32,512]{3,2,1,0:T(8,128)(2,1)S(1)} %gradother.1), channel_id=1, source_target_pairs={{0,16},{16,0},{1,17},{17,1},{2,18},{18,2},{3,19},{19,3},{4,20},{20... | collective-permute-start | bytes 2359304 | tf_op jit(solution)/shard_map/ppermute | solution.py:367
  8.0 2.7 %gradown.1.a_ref = bf16[8,3,32,512]{3,2,1,0:T(8,128)(2,1)S(1)} custom-call(s32[3]{0:T(128)S(1)} %pad_add_fusion.me_ref.place_ref, bf16[2,512,512]{2,1,0:T(8,128)(2,1)S(1)} %loada.1.first_ref.before_ref.own_ref, bf16[2,512,512]{2,1,0:T(8,128)(2,1)S(1)} %loadb.1.last_ref.own_ref, f32[1,1024]{1,0:T(1,128)S(1)} %copy-done.4, bf16[1,3,512,512]{3,2,1,0:T(8,128)(2,1)S(1)} %copy-done), custom_call_target="tpu_custom_call" | custom-call | flops 1000 | bytes 1048576 | tf_op jit(solution)/shard_map/gradown/pallas_call | solution.py:111
  10.7 0.0 copy-done.3
  10.7 1.6 %bounds.1.meta_ref = s32[4]{0:T(128)S(1)} custom-call(s32[3]{0:T(128)S(1)} %pad_add_fusion.me_ref.place_ref, s32[2,16384]{1,0:T(2,128)S(1)} %copy-done.3), custom_call_target="tpu_custom_call" | custom-call | flops 196608 | bytes 131072 | tf_op jit(solution)/shard_map/bounds/pallas_call | solution.py:160
  12.3 0.0 copy-done.2
  12.3 0.0 copy-start.1
  12.3 1.2 %prep.1 = (f32[3,32,512]{2,1,0:T(8,128)S(1)}, f32[3,32,128]{2,1,0:T(8,128)S(1)}) custom-call(s32[3]{0:T(128)S(1)} %pad_add_fusion.me_ref.place_ref, bf16[1,3,512,512]{3,2,1,0:T(8,128)(2,1)S(1)} %copy-done, f32[1,3,512,512]{3,2,1,0:T(8,128)S(1)} %copy-done.2), custom_call_target="tpu_custom_call" | custom-call | flops 3145728 | bytes 3145728 | tf_op jit(solution)/shard_map/prep/pallas_call | solution.py:216
  13.5 0.1 copy-done.1
  13.5 2.2 %attnb.1.hi_ref = f32[512,512]{1,0:T(8,128)S(1)} custom-call(s32[4]{0:T(128)S(1)} %bounds.1.meta_ref, bf16[1,1024,512]{2,1,0:T(8,128)(2,1)S(1)} %copy-done.1, bf16[2,512,512]{2,1,0:T(8,128)(2,1)S(1)} %loada.1.first_ref.before_ref.own_ref, bf16[2,512,512]{2,1,0:T(8,128)(2,1)S(1)} %loadb.1.last_ref.own_ref), custom_call_target="tpu_custom_call" | custom-call | flops 805306368 | bytes 4194304 | tf_op jit(solution)/shard_map/attnb/pallas_call | solution.py:190
  15.8 0.0 collective-permute-done.b_ref
  15.8 0.4 collective-permute-done.1.before_ref
  16.2 0.2 added.1
  16.4 17.0 %all_to_all.15.pieces_ref = bf16[8,3,32,512]{3,2,1,0:T(8,128)(2,1)S(1)} all-to-all(bf16[8,3,32,512]{3,2,1,0:T(8,128)(2,1)S(1)} %added.1), channel_id=1, replica_groups=mesh['y'=4,'x'=2,'core'=2,'seq'=2,'head'=8] {'y','x'}, dimensions={0} | all-to-all | bytes 1572864 | tf_op jit(solution)/shard_map/all_to_all | solution.py:412
  33.4 0.3 renew.1
  33.7 13.6 %all_to_all.16.mine_ref = bf16[8,3,32,512]{3,2,1,0:T(8,128)(2,1)S(1)} all-to-all(bf16[8,3,32,512]{3,2,1,0:T(8,128)(2,1)S(1)} %renew.1), channel_id=1, replica_groups=mesh['y'=4,'x'=2,'core'=2,'seq'=2,'head'=8] {'y','x'}, dimensions={0} | all-to-all | bytes 1572864 | tf_op jit(solution)/shard_map/all_to_all | solution.py:414
  47.3 0.0 collective-permute-start.2
  47.3 2.2 %attna.1.lo_ref = f32[512,512]{1,0:T(8,128)S(1)} custom-call(s32[4]{0:T(128)S(1)} %bounds.1.meta_ref, bf16[1,1024,512]{2,1,0:T(8,128)(2,1)S(1)} %copy-done.1, bf16[2,512,512]{2,1,0:T(8,128)(2,1)S(1)} %collective-permute-done.1.before_ref, bf16[2,512,512]{2,1,0:T(8,128)(2,1)S(1)} %loada.1.first_ref.before_ref.own_ref), custom_call_target="tpu_custom_call" | custom-call | flops 805306368 | bytes 4194304 | tf_op jit(solution)/shard_map/attna/pallas_call | solution.py:190
  49.5 0.0 copy-start.5
  49.6 0.0 collective-permute-done.2.other_ref
  49.6 2.4 %out.1 = (f32[1024,512]{1,0:T(8,128)S(1)}, f32[8,8,128]{2,1,0:T(8,128)S(1)}) custom-call(bf16[1,1024,512]{2,1,0:T(8,128)(2,1)S(1)} %copy-done.1, f32[512,512]{1,0:T(8,128)S(1)} %attna.1.lo_ref, f32[512,512]{1,0:T(8,128)S(1)} %attnb.1.hi_ref, bf16[8,3,32,512]{3,2,1,0:T(8,128)(2,1)S(1)} %all_to_all.16.mine_ref, ...), custom_call_target="tpu_custom_call" | custom-call | flops 1610612736 | bytes 6291456 | tf_op jit(solution)/shard_map/out/pallas_call | solution.py:295
  52.0 16.3 %all_to_all.17.sums_ref = f32[8,8,128]{2,1,0:T(8,128)S(1)} all-to-all(f32[8,8,128]{2,1,0:T(8,128)S(1)} %get-tuple-element.51), channel_id=1, replica_groups=mesh['y'=4,'x'=2,'core'=2,'seq'=2,'head'=8] {'head'}, dimensions={0} | all-to-all | bytes 65536 | tf_op jit(solution)/shard_map/all_to_all | solution.py:421
  68.3 0.0 copy-done.5
  68.3 2.3 %final.1 = (bf16[1,1024,512]{2,1,0:T(8,128)(2,1)}, bf16[1,3,512,512]{3,2,1,0:T(8,128)(2,1)}) custom-call(s32[3]{0:T(128)S(1)} %pad_add_fusion.me_ref.place_ref, f32[1024,512]{1,0:T(8,128)S(1)} %get-tuple-element.50.y_ref, f32[8,8,128]{2,1,0:T(8,128)S(1)} %all_to_all.17.sums_ref, f32[1,512]{1,0:T(1,128)S(1)} %copy-done.5, ...), custom_call_target="tpu_custom_call" | custom-call | flops 1048576 | bytes 6291456 | tf_op jit(solution)/shard_map/final/pallas_call | solution.py:340
Async XLA Ops:
  1.9 1.7 %copy-start = (bf16[1,3,512,512]{3,2,1,0:T(8,128)(2,1)S(1)}, bf16[1,3,512,512]{3,2,1,0:T(8,128)(2,1)}, u32[]{:S(2)}) copy-start(bf16[1,3,512,512]{3,2,1,0:T(8,128)(2,1)} %w_ref.2) | copy-start | bytes 4718596
  1.9 1.7 %copy-start.4 = (f32[1,1024]{1,0:T(1,128)S(1)}, f32[1,1024]{1,0:T(1,128)}, u32[]{:S(2)}) copy-start(f32[1,1024]{1,0:T(1,128)} %r_ref.3) | copy-start | bytes 12292
  2.0 14.2 %collective-permute-start.1 = (bf16[2,512,512]{2,1,0:T(8,128)(2,1)S(1)}, bf16[2,512,512]{2,1,0:T(8,128)(2,1)S(1)}, u32[]{:S(2)}, u32[]{:S(2)}) collective-permute-start(bf16[2,512,512]{2,1,0:T(8,128)(2,1)S(1)} %loadb.1.last_ref.own_ref), channel_id=1, source_target_pairs={{0,16},{16,32},{32,48},{48,64},{64,80},{80,96},{96,112},{112,128},... | collective-permute-start | bytes 3145736 | tf_op jit(solution)/shard_map/ppermute | solution.py:400
  6.3 4.4 %copy-start.3 = (s32[2,16384]{1,0:T(2,128)S(1)}, s32[2,16384]{1,0:T(2,128)}, u32[]{:S(2)}) copy-start(s32[2,16384]{1,0:T(2,128)} %docs_ref.1) | copy-start | bytes 393220
  6.3 6.0 %copy-start.2 = (f32[1,3,512,512]{3,2,1,0:T(8,128)S(1)}, f32[1,3,512,512]{3,2,1,0:T(8,128)}, u32[]{:S(2)}) copy-start(f32[1,3,512,512]{3,2,1,0:T(8,128)} %m_ref.1) | copy-start | bytes 9437188
  6.3 9.5 %collective-permute-start = (bf16[8,3,32,512]{3,2,1,0:T(8,128)(2,1)S(1)}, bf16[8,3,32,512]{3,2,1,0:T(8,128)(2,1)S(1)}, u32[]{:S(2)}, u32[]{:S(2)}) collective-permute-start(bf16[8,3,32,512]{3,2,1,0:T(8,128)(2,1)S(1)} %gradother.1), channel_id=1, source_target_pairs={{0,16},{16,0},{1,17},{17,1},{2,18},{18,2},{3,19},{19,3},{4,20},{20... | collective-permute-start | bytes 2359304 | tf_op jit(solution)/shard_map/ppermute | solution.py:367
  12.3 1.2 %copy-start.1 = (bf16[1,1024,512]{2,1,0:T(8,128)(2,1)S(1)}, bf16[1,1024,512]{2,1,0:T(8,128)(2,1)}, u32[]{:S(2)}) copy-start(bf16[1,1024,512]{2,1,0:T(8,128)(2,1)} %q_ref.5) | copy-start | bytes 3145732
  47.3 2.3 %collective-permute-start.2 = (bf16[8,3,32,512]{3,2,1,0:T(8,128)(2,1)S(1)}, bf16[8,3,32,512]{3,2,1,0:T(8,128)(2,1)S(1)}, u32[]{:S(2)}, u32[]{:S(2)}) collective-permute-start(bf16[8,3,32,512]{3,2,1,0:T(8,128)(2,1)S(1)} %all_to_all.16.mine_ref), channel_id=1, source_target_pairs={{0,16},{16,0},{1,17},{17,1},{2,18},{18,2},{3,19},{19,3},{4,20},{20... | collective-permute-start | bytes 2359304 | tf_op jit(solution)/shard_map/ppermute | solution.py:367
  49.5 18.8 %copy-start.5 = (f32[1,512]{1,0:T(1,128)S(1)}, f32[1,512]{1,0:T(1,128)}, u32[]{:S(2)}) copy-start(f32[1,512]{1,0:T(1,128)} %gain_ref.1) | copy-start | bytes 6148
